TPU v7x, 32 devices: a whole 2x2x4 slice. The times are simulated.
32 devices in a mesh: batch: 8 (over z, y), fsdp: 4 (over x, core).
Axes of the slice: x: 2, y: 2, z: 4, core: 2. Of those that a mesh axis runs over, the one named last changes fastest.
Arguments:
- tokens: bfloat16 [128, 256, 768], P(('batch', 'fsdp')), may hold values from -6 to 6
- cotangent: bfloat16 [128, 256, 768], P(('batch', 'fsdp')), may hold values from -6 to 6
- mask_pos: int32 [128, 128], P(('batch', 'fsdp')), may hold values from 0 to 255, as said below
- mask_count: int32 [128], P(('batch', 'fsdp')), may hold values from 8 to 128, as said below
- w_qkv: float32 [768, 2304], P('fsdp'), may hold values from -0.21875 to 0.21875
- m_qkv: float32 [768, 2304], P(('fsdp', 'batch')), may hold values from -217.2232 to 217.2232
- v_qkv: float32 [768, 2304], P(('fsdp', 'batch')), may hold values from 1474.56 to 23592.96
- w_out: float32 [768, 768], P('fsdp'), may hold values from -0.875 to 0.875
- m_out: float32 [768, 768], P(('fsdp', 'batch')), may hold values from -50.685413 to 50.685413
- v_out: float32 [768, 768], P(('fsdp', 'batch')), may hold values from 80.2816 to 1284.5056
- w_fc1: float32 [768, 3072], P('fsdp'), may hold values from -0.21875 to 0.21875
- m_fc1: float32 [768, 3072], P(('fsdp', 'batch')), may hold values from -86.88928 to 86.88928
- v_fc1: float32 [768, 3072], P(('fsdp', 'batch')), may hold values from 235.9296 to 3774.8735
- w_fc2: float32 [3072, 768], P('fsdp'), may hold values from -0.109375 to 0.109375
- m_fc2: float32 [3072, 768], P(('fsdp', 'batch')), may hold values from -181.01933 to 181.01933
- v_fc2: float32 [3072, 768], P(('fsdp', 'batch')), may hold values from 1024 to 16384
- vectors: float32 [14, 768], P(None, 'fsdp'), may hold values from -1.2 to 1.6
- m_vec: float32 [14, 768], P(None, ('fsdp', 'batch')), may hold values from -217.2232 to 217.2232
- v_vec: float32 [14, 768], P(None, ('fsdp', 'batch')), may hold values from 1474.56 to 23592.96
Outputs:
- layer_out: bfloat16 [128, 256, 768], P(('batch', 'fsdp'))
- grad_tokens: float32 [128, 256, 768], P(('batch', 'fsdp'))
- new_w_qkv: float32 [768, 2304], P('fsdp')
- new_m_qkv: float32 [768, 2304], P(('fsdp', 'batch'))
- new_v_qkv: float32 [768, 2304], P(('fsdp', 'batch'))
- new_w_out: float32 [768, 768], P('fsdp')
- new_m_out: float32 [768, 768], P(('fsdp', 'batch'))
- new_v_out: float32 [768, 768], P(('fsdp', 'batch'))
- new_w_fc1: float32 [768, 3072], P('fsdp')
- new_m_fc1: float32 [768, 3072], P(('fsdp', 'batch'))
- new_v_fc1: float32 [768, 3072], P(('fsdp', 'batch'))
- new_w_fc2: float32 [3072, 768], P('fsdp')
- new_m_fc2: float32 [3072, 768], P(('fsdp', 'batch'))
- new_v_fc2: float32 [3072, 768], P(('fsdp', 'batch'))
- new_vectors: float32 [14, 768], P(None, 'fsdp')
- new_m_vec: float32 [14, 768], P(None, ('fsdp', 'batch'))
- new_v_vec: float32 [14, 768], P(None, ('fsdp', 'batch'))
Inputs may be any that keep to these rules, and one draw needn't show every extreme that they name: `mask_pos`: each row holds 128 different positions of the pair; its first mask_count entries are the masked tokens. `mask_count`: some pair has 128 masked tokens.
All inputs are finite; a program needn't handle non-finite values.
Results may differ from a plain program's by a relative error of at most 0.015.
Values may be sent and summed in bfloat16 or wider, within the bound.
No kernel may reach another device: no remote copies, remote signals or barrier semaphores. Data moves between devices by JAX's collectives and lax.ppermute only.
A program may use at most 192 MiB of HBM per device.

v0:
```python
import functools
import math

import jax
import jax.numpy as jnp
import numpy as np
from jax import lax
from jax.experimental import pallas as pl
from jax.experimental.pallas import tpu as pltpu
from jax.sharding import PartitionSpec as P

D = 768
HEADS = 12
HDIM = 64
FF = 3072
TEXT = 40
STEP = 3
MAXM = 128
NVEC = 14
PARTS = FF // D
LANES = 128
SLABS = D // LANES

BETA_ONE = 0.5
BETA_TWO = 0.5
EPS_ADAM = 1e-08
STEP_RATES = (0.03, 0.1, 0.03, 0.015, 0.3)
DECAY_RATES = (0.01, 0.01, 0.01, 0.01, 0.0)
INV_ROOT_TWO = 1.0 / math.sqrt(2.0)
INV_ROOT_TWOPI = 1.0 / math.sqrt(2.0 * math.pi)

KERNEL_VMEM = 20 * 2**20
FLOPS_SCALE = 3e9
BYTES_SCALE = 1e7
F32 = jnp.float32
BF16 = jnp.bfloat16


def dot(a, b):
    return lax.dot_general(a, b, (((1,), (0,)), ((), ())), preferred_element_type=F32)


def dot_first(a, b):
    return lax.dot_general(a, b, (((0,), (0,)), ((), ())), preferred_element_type=F32)


def dot_last(a, b):
    return lax.dot_general(a, b, (((1,), (1,)), ((), ())), preferred_element_type=F32)


def normalize(hidden):
    row_mean = jnp.mean(hidden, axis=-1, keepdims=True)
    centred = hidden - row_mean
    inv_scale = lax.rsqrt(jnp.mean(centred * centred, axis=-1, keepdims=True) + 1e-06)
    return centred * inv_scale, inv_scale


def norm_back(gradient, normed, inv_scale, gain_row):
    scaled = gradient * gain_row
    return inv_scale * (
        scaled
        - jnp.mean(scaled, axis=-1, keepdims=True)
        - normed * jnp.mean(scaled * normed, axis=-1, keepdims=True)
    )


def adamw(weight, gradient, moment_one, moment_two, step_rate, decay_rate):
    new_first = BETA_ONE * moment_one + (1.0 - BETA_ONE) * gradient
    new_second = BETA_TWO * moment_two + (1.0 - BETA_TWO) * gradient * gradient
    correct_one = 1.0 - BETA_ONE**STEP
    correct_two = 1.0 - BETA_TWO**STEP
    update = (
        new_first / correct_one / (jnp.sqrt(new_second / correct_two) + EPS_ADAM)
        + decay_rate * weight
    )
    return (weight - step_rate * update, new_first, new_second)


def spent(micros):
    return pl.CostEstimate(
        flops=int(micros * FLOPS_SCALE), bytes_accessed=int(micros * BYTES_SCALE), transcendentals=0
    )


def full(shape):
    zeros = (0,) * len(shape)
    return pl.BlockSpec(shape, lambda *_: zeros)


ANYWHERE = pl.BlockSpec(memory_space=pl.ANY)


class Plan:
    def __init__(self, mesh):
        self.nf = mesh.shape["fsdp"]
        self.nb = mesh.shape["batch"]
        self.nd = self.nf * self.nb
        self.fbits = self.nf.bit_length() - 1
        self.bbits = self.nb.bit_length() - 1
        assert self.nf == 1 << self.fbits and self.nb == 1 << self.bbits
        assert self.fbits == 2 and self.bbits >= 2
        near = [1, 2, 6] if self.bbits == 3 else [1 << k for k in range(self.bbits)]
        self.batch = [mask * self.nf for mask in near]
        first, second, *rest = self.batch
        self.scatter = ([1, 2, second, first] + rest, [1, first, 2, second] + rest)
        self.gather = (rest[::-1] + [second, first], rest[::-1] + [first, second])
        self.helper = (first, second)

    def exchange(self, value, even, odd=None):
        odd = even if odd is None else odd
        pairs = [(i, i ^ (odd if i & 1 else even)) for i in range(self.nd)]
        return lax.ppermute(value, ("batch", "fsdp"), pairs)

    def spans(self, gens):
        masks = np.zeros(1, np.int32)
        for mask in reversed(gens):
            masks = np.concatenate([masks, masks ^ mask])
        return masks

    def table(self):
        rows = []
        for index in range(self.nd):
            core, fi, bi = index & 1, index & (self.nf - 1), index >> self.fbits
            halves = (bi & 1, (bi >> 1) & 1)
            keep = index ^ self.spans(self.scatter[core][1:])
            send = (index ^ 1) ^ self.spans(self.scatter[1 - core][1:])
            order = np.concatenate([keep, send])
            owners = (order & (self.nf - 1)) * self.nb + (order >> self.fbits)
            places = bi ^ (self.spans(self.gather[core][::-1]) >> self.fbits)
            own = np.asarray([fi, halves[core], halves[1 - core], bi])
            rows.append(np.concatenate([own, owners, places, np.argsort(places)]))
        return np.stack(rows).astype(np.int32)


OWN = 4


PIECES = ((0, None), (1, None), (2, 0), (2, 1), (3, 2), (3, 3))


def piece_copies(refs, target, sems, place_ref, rows, start=0):
    copies = []
    cols = target.shape[1]
    for number, ((mask, kind), ref) in enumerate(zip(PIECES, refs)):
        row = (place_ref[0] ^ mask) * rows
        length = rows
        if kind is not None:
            length = rows // 2
            low = place_ref[1 + kind // 2]
            row = row + (low if kind % 2 == 0 else 1 - low) * length
        copies.append(
            pltpu.make_async_copy(
                ref.at[:, pl.ds(start, cols)],
                target.at[pl.ds(pl.multiple_of(row, 8), length)],
                sems.at[number],
            )
        )
    return copies


def start_all(copies):
    for copy in copies:
        copy.start()


def wait_all(copies):
    for copy in copies:
        copy.wait()


def cast_kernel(place_ref, *refs):
    parts, (shard_ref, mine_ref) = refs[:-2], refs[-2:]
    start = 0
    for part in parts:
        cols = slice(start, start + part.shape[1])
        low = part[...].astype(BF16)
        shard_ref[:, cols] = low

        @pl.when(pl.program_id(0) == 0)
        def _(low=low, cols=cols):
            mine_ref[:, cols] = low

        start += part.shape[1]


def order_kernel(count_ref, pos_ref, tok_ref, cot_ref, perm_ref, tokp_ref, img_ref, dy_ref):
    pair = pl.program_id(0)
    length = tok_ref.shape[1]
    slots = pos_ref.shape[2]
    token = lax.broadcasted_iota(jnp.int32, (length, slots), 0)
    slot = lax.broadcasted_iota(jnp.int32, (length, slots), 1)
    hit = jnp.where(token == pos_ref[0], 1.0, 0.0)
    free = 1.0 - jnp.sum(hit, axis=1, keepdims=True)
    below = lax.broadcasted_iota(jnp.int32, (length, length), 1) < lax.broadcasted_iota(
        jnp.int32, (length, length), 0
    )
    rank = dot(
        jnp.where(below, 1.0, 0.0).astype(BF16),
        jnp.broadcast_to(free, (length, slots)).astype(BF16),
    )
    rest = jnp.where(rank == slot.astype(F32), jnp.broadcast_to(free, (length, slots)), 0.0)
    perm = jnp.concatenate([hit, rest], axis=1).astype(BF16)
    perm_ref[0] = perm
    tokp_ref[0] = dot_first(perm, tok_ref[0]).astype(BF16)
    image = jnp.where(lax.broadcasted_iota(jnp.int32, (length, LANES), 0) >= TEXT, 1.0, 0.0)
    img_ref[0] = dot_first(perm, image.astype(BF16)).astype(BF16)
    chosen = dot_first(perm[:, :slots], cot_ref[0])
    live = lax.broadcasted_iota(jnp.int32, (slots, 1), 0) < count_ref[pair]
    dy_ref[0] = jnp.where(live, chosen, 0.0).astype(BF16)


def start_row(tok_ref, img_ref, vec_ref):
    return tok_ref[0].astype(F32) + jnp.where(
        img_ref[0][:, :1].astype(F32) > 0.5, vec_ref[1:2, :], vec_ref[0:1, :]
    )


def qkv_kernel(rows, place_ref, tok_ref, img_ref, vec_ref, *refs):
    pieces = refs[: len(PIECES)]
    n1_ref, qkv_ref, w_ref, sems = refs[len(PIECES) :]
    first = pl.program_id(0) == 0
    copies = piece_copies(pieces, w_ref, sems, place_ref, rows)

    @pl.when(first)
    def _():
        start_all(copies)

    normed, _ = normalize(start_row(tok_ref, img_ref, vec_ref))
    n1 = (normed * vec_ref[2:3, :] + vec_ref[3:4, :]).astype(BF16)
    n1_ref[0] = n1

    @pl.when(first)
    def _():
        wait_all(copies)

    qkv_ref[0, :, :D] = (dot(n1, w_ref[:, :D]) + vec_ref[4:5, :]).astype(BF16)
    qkv_ref[0, :, D : 2 * D] = dot(n1, w_ref[:, D : 2 * D]).astype(BF16)
    qkv_ref[0, :, 2 * D :] = (dot(n1, w_ref[:, 2 * D :]) + vec_ref[5:6, :]).astype(BF16)


def mix_kernel(qkv_ref, a_ref):
    low = lax.broadcasted_iota(jnp.int32, (1, LANES), 1) < HDIM
    for slab in range(SLABS):
        cols = slice(slab * LANES, (slab + 1) * LANES)
        q = qkv_ref[0, :, cols] * jnp.asarray(HDIM**-0.5, BF16)
        k = qkv_ref[0, :, D + slab * LANES : D + (slab + 1) * LANES]
        v = qkv_ref[0, :, 2 * D + slab * LANES : 2 * D + (slab + 1) * LANES]
        outs = []
        for head in range(2):
            mine = low if head == 0 else jnp.logical_not(low)
            scores = dot_last(jnp.where(mine, q, jnp.zeros_like(q)), k)
            e = jnp.exp(scores - jnp.max(scores, axis=-1, keepdims=True))
            p = (e * (1.0 / jnp.sum(e, axis=-1, keepdims=True))).astype(BF16)
            outs.append(dot(p, v))
        a_ref[0, :, cols] = jnp.where(low, outs[0], outs[1]).astype(BF16)


def fc1_kernel(rows, place_ref, tok_ref, img_ref, a_ref, vec_ref, *refs):
    pieces = refs[: len(PIECES)]
    h1_ref, n2_ref, z_ref, slope_ref, wo_ref, w1_ref, sem_o, sem_1 = refs[len(PIECES) :]
    first = pl.program_id(0) == 0
    copies_o = piece_copies(pieces, wo_ref, sem_o, place_ref, rows)
    copies_1 = piece_copies(pieces, w1_ref, sem_1, place_ref, rows, D)

    @pl.when(first)
    def _():
        start_all(copies_o)
        start_all(copies_1)
        wait_all(copies_o)

    h1 = start_row(tok_ref, img_ref, vec_ref) + dot(a_ref[0], wo_ref[...]) + vec_ref[6:7, :]
    h1_ref[0] = h1
    normed, _ = normalize(h1)
    n2 = (normed * vec_ref[7:8, :] + vec_ref[8:9, :]).astype(BF16)
    n2_ref[0] = n2

    @pl.when(first)
    def _():
        wait_all(copies_1)

    slots = slope_ref.shape[1]
    for part in range(PARTS):
        cols = slice(part * D, (part + 1) * D)
        f = dot(n2, w1_ref[:, cols]) + vec_ref[9 + part : 10 + part, :]
        phi = 0.5 * (1.0 + lax.erf(f * INV_ROOT_TWO))
        z_ref[0, :, cols] = (f * phi).astype(BF16)
        fs = f[:slots]
        slope = phi[:slots] + fs * jnp.exp(-0.5 * fs * fs) * INV_ROOT_TWOPI
        slope_ref[0, :, cols] = slope.astype(BF16)


def spread(acc_ref, owners_ref, outs):
    if len(outs) == 1:
        outs[0][...] = acc_ref[...].astype(BF16)
        return
    keep_ref, send_ref = outs
    half, block, _ = send_ref.shape

    def one(spot, _):
        for out_ref, base in ((send_ref, half), (keep_ref, 0)):
            start = pl.multiple_of(owners_ref[OWN + base + spot] * block, 8)
            out_ref[spot] = acc_ref[pl.ds(start, block), :].astype(BF16)
        return 0

    lax.fori_loop(0, half, one, 0)


def gw2_kernel(owners_ref, z_ref, dy_ref, *refs):
    outs, (sum_ref, zt_ref, acc_ref) = refs[:-3], refs[-3:]
    pairs, slots, width = z_ref.shape

    @pl.when(pl.program_id(0) == 0)
    def _():
        zt_ref[...] = z_ref[...].reshape(pairs * slots, width).T

    dy = dy_ref[...].reshape(pairs * slots, -1)
    acc_ref[...] = dot(zt_ref[...], dy)
    sum_ref[...] = jnp.sum(dy.astype(F32), axis=0, keepdims=True)
    spread(acc_ref, owners_ref, outs)


def df_kernel(rows, place_ref, dy_ref, slope_ref, *refs):
    pieces = refs[: len(PIECES)]
    df_ref, gb1_ref, w2_ref, sems = refs[len(PIECES) :]
    step = pl.program_id(0)
    pairs, slots, width = slope_ref.shape
    total = pairs * slots
    copies = piece_copies(pieces, w2_ref, sems, place_ref, rows)

    @pl.when(step == 0)
    def _():
        start_all(copies)
        wait_all(copies)

    dz = dot_last(
        dy_ref[...].reshape(total, D), w2_ref[pl.ds(pl.multiple_of(step * width, 8), width), :]
    )
    df = dz * slope_ref[...].reshape(total, width).astype(F32)
    gb1_ref[...] = jnp.sum(df, axis=0, keepdims=True)
    df_ref[...] = df.astype(BF16)


def mlp_back_kernel(rows, place_ref, df_ref, dy_ref, h1_ref, vec_ref, *refs):
    pieces = refs[: len(PIECES)]
    dh_ref, dhr_ref, da_ref, sum_ref, w1_ref, wo_ref, sem_1, sem_o = refs[len(PIECES) :]
    first = pl.program_id(0) == 0
    copies_1 = piece_copies(pieces, w1_ref, sem_1, place_ref, rows, D)
    copies_o = piece_copies(pieces, wo_ref, sem_o, place_ref, rows)

    @pl.when(first)
    def _():
        start_all(copies_1)
        start_all(copies_o)
        sum_ref[...] = jnp.zeros_like(sum_ref)
        wait_all(copies_1)
        wait_all(copies_o)

    some, slots, _ = dy_ref.shape
    total = some * slots
    dn2 = dot_last(df_ref[...], w1_ref[...])
    normed, scale = normalize(h1_ref[...].reshape(total, D))
    dh = dy_ref[...].reshape(total, D).astype(F32) + norm_back(dn2, normed, scale, vec_ref[7:8, :])
    dh_ref[...] = dh.reshape(some, slots, D)
    sum_ref[0:1, :] += jnp.sum(dh, axis=0, keepdims=True)
    sum_ref[1:2, :] += jnp.sum(dn2 * normed, axis=0, keepdims=True)
    sum_ref[2:3, :] += jnp.sum(dn2, axis=0, keepdims=True)
    low = dh.astype(BF16)
    dhr_ref[...] = low.reshape(some, slots, D)
    da_ref[...] = dot_last(low, wo_ref[...]).astype(BF16).reshape(some, slots, D)


def gw1o_kernel(owners_ref, n2_ref, df_ref, a_ref, dhr_ref, *refs):
    outs, (n2t_ref, acc_ref) = refs[:-2], refs[-2:]
    step = pl.program_id(0)
    pairs, slots, _ = n2_ref.shape
    total = pairs * slots

    @pl.when(step == 0)
    def _():
        n2t_ref[...] = n2_ref[...].reshape(total, D).T

    @pl.when(step < PARTS)
    def _():
        acc_ref[...] = dot(n2t_ref[...], df_ref[...])

    @pl.when(step == PARTS)
    def _():
        acc_ref[...] = dot_first(a_ref[...].reshape(total, D), dhr_ref[...].reshape(total, D))

    spread(acc_ref, owners_ref, outs)


def attn_back_kernel(more, qkv_ref, da_ref, *refs):
    if more:
        _, _, before_ref, dq_ref, dkv_ref, sum_ref = refs
    else:
        dq_ref, dkv_ref, sum_ref = refs
    slots = da_ref.shape[1]

    @pl.when(pl.program_id(0) == 0)
    def _():
        sum_ref[...] = before_ref[...] if more else jnp.zeros_like(sum_ref)

    low = lax.broadcasted_iota(jnp.int32, (1, LANES), 1) < HDIM
    scale = jnp.asarray(HDIM**-0.5, BF16)
    for slab in range(SLABS):
        cols = slice(slab * LANES, (slab + 1) * LANES)
        q = qkv_ref[0, :slots, cols] * scale
        k = qkv_ref[0, :, D + slab * LANES : D + (slab + 1) * LANES]
        v = qkv_ref[0, :, 2 * D + slab * LANES : 2 * D + (slab + 1) * LANES]
        da = da_ref[0, :, cols]
        gqs, gks, gvs = [], [], []
        for head in range(2):
            mine = low if head == 0 else jnp.logical_not(low)
            zero = jnp.zeros_like(q)
            scores = dot_last(jnp.where(mine, q, zero), k)
            e = jnp.exp(scores - jnp.max(scores, axis=-1, keepdims=True))
            p = e * (1.0 / jnp.sum(e, axis=-1, keepdims=True))
            gvs.append(dot_first(p.astype(BF16), da))
            dp = dot_last(jnp.where(mine, da, zero), v)
            ds = (p * (dp - jnp.sum(p * dp, axis=-1, keepdims=True))).astype(BF16)
            gqs.append(dot(ds, k))
            gks.append(dot_first(ds, q))
        gq = jnp.where(low, gqs[0], gqs[1]) * (HDIM**-0.5)
        gk = jnp.where(low, gks[0], gks[1])
        gv = jnp.where(low, gvs[0], gvs[1])
        dq_ref[0, :, cols] = gq.astype(BF16)
        dkv_ref[0, :, cols] = gk.astype(BF16)
        dkv_ref[0, :, D + slab * LANES : D + (slab + 1) * LANES] = gv.astype(BF16)
        sum_ref[0:1, cols] += jnp.sum(gq, axis=0, keepdims=True)
        sum_ref[1:2, cols] += jnp.sum(gv, axis=0, keepdims=True)


def gqkv_kernel(owners_ref, n1_ref, dq_ref, dkv_ref, *refs):
    outs, (n1t_ref, acc_ref) = refs[:-2], refs[-2:]
    step = pl.program_id(0)
    pairs, length, _ = n1_ref.shape
    slots = dq_ref.shape[1]

    @pl.when(step == 0)
    def _():
        n1t_ref[...] = n1_ref[...].reshape(pairs * length, D).T
        total = dot(n1t_ref[:, :slots], dq_ref[0])
        for pair in range(1, pairs):
            total += dot(n1t_ref[:, pair * length : pair * length + slots], dq_ref[pair])
        acc_ref[...] = total

    @pl.when(step > 0)
    def _():
        acc_ref[...] = dot(n1t_ref[...], dkv_ref[...].reshape(pairs * length, D))

    spread(acc_ref, owners_ref, outs)


def split_two(value):
    one = value.astype(BF16)
    return one, (value - one.astype(F32)).astype(BF16)


def grad_in_kernel(
    rows,
    place_ref,
    tok_ref,
    img_ref,
    vec_ref,
    dq_ref,
    dkv_ref,
    dh_ref,
    perm_ref,
    attn_sum_ref,
    mlp_sum_ref,
    gb1_ref,
    gb2_ref,
    *refs,
):
    pieces = refs[: len(PIECES)]
    out_ref, sum_ref, w_ref, sems = refs[len(PIECES) :]
    first = pl.program_id(0) == 0
    slots = dq_ref.shape[1]
    copies = piece_copies(pieces, w_ref, sems, place_ref, rows)

    @pl.when(first)
    def _():
        start_all(copies)
        sum_ref[...] = jnp.zeros_like(sum_ref)
        sum_ref[4:6, :] = attn_sum_ref[0:2, :]
        sum_ref[6:9, :] = mlp_sum_ref[0:3, :]
        for part in range(PARTS):
            sum_ref[9 + part : 10 + part, :] = gb1_ref[:, part * D : (part + 1) * D]
        sum_ref[9 + PARTS : 10 + PARTS, :] = gb2_ref[...]
        wait_all(copies)

    dn_all = dot_last(dkv_ref[0], w_ref[:, D:])
    dn_top = dn_all[:slots] + dot_last(dq_ref[0], w_ref[:, :D])
    dn = jnp.concatenate([dn_top, dn_all[slots:]], axis=0)
    normed, scale = normalize(start_row(tok_ref, img_ref, vec_ref))
    grad = norm_back(dn, normed, scale, vec_ref[2:3, :])
    grad = jnp.concatenate([grad[:slots] + dh_ref[0], grad[slots:]], axis=0)
    image = img_ref[0][:, :1].astype(F32) > 0.5
    sum_ref[0:1, :] += jnp.sum(jnp.where(image, 0.0, grad), axis=0, keepdims=True)
    sum_ref[1:2, :] += jnp.sum(jnp.where(image, grad, 0.0), axis=0, keepdims=True)
    sum_ref[2:3, :] += jnp.sum(dn * normed, axis=0, keepdims=True)
    sum_ref[3:4, :] += jnp.sum(dn, axis=0, keepdims=True)
    one, two = split_two(grad)
    perm = perm_ref[0]
    out_ref[0] = dot(perm, one) + dot(perm, two)


def out_kernel(rows, place_ref, z_ref, h1_ref, vec_ref, perm_ref, *refs):
    pieces = refs[: len(PIECES)]
    out_ref, w_ref, sems = refs[len(PIECES) :]
    first = pl.program_id(0) == 0
    copies = piece_copies(pieces, w_ref, sems, place_ref, rows)

    @pl.when(first)
    def _():
        start_all(copies)
        wait_all(copies)

    y = h1_ref[0] + dot(z_ref[0], w_ref[...]) + vec_ref[9 + PARTS : 10 + PARTS, :]
    out_ref[0] = dot(perm_ref[0], y.astype(BF16)).astype(BF16)


def place_kernel(number, base, rows, spots_ref, one_ref, two_ref, *refs):
    step = pl.program_id(0)
    count = one_ref.shape[0]

    def put(out_ref):
        def one(spot, _):
            for source, first in ((one_ref, base), (two_ref, base + count)):
                at = pl.ds(pl.multiple_of(spots_ref[first + spot] * rows, 8), rows)
                out_ref[at, :] = source[spot, :rows].astype(F32)
            return 0

        lax.fori_loop(0, count, one, 0)

    if number == 1:
        put(refs[0])
        return
    last = pl.num_programs(0) - 1

    @pl.when(step < last)
    def _():
        put(refs[0])

    @pl.when(step == last)
    def _():
        put(refs[1])


def later(value, dep):
    return lax.optimization_barrier((value, dep))[0]


class Chain:
    def __init__(self):
        self.last, self.waiting = None, []

    def pin(self, values):
        return lax.optimization_barrier((list(values), self.last))[0]

    def hold(self, value):
        self.waiting.append(value)
        return value

    def __call__(
        self, kernel, grid, scalars, ins, outs, scratch, estimate, name, after=(), aliases=None
    ):
        deps = list(after) + self.waiting
        self.waiting = []
        if self.last is not None:
            deps.append(self.last)
        fixed = len(scalars) + len(ins)
        extra = len(deps)

        def body(*refs):
            kernel(*refs[:fixed], *refs[fixed + extra :])

        got = pl.pallas_call(
            body,
            grid_spec=pltpu.PrefetchScalarGridSpec(
                num_scalar_prefetch=len(scalars),
                grid=grid,
                in_specs=[spec for _, spec in ins] + [ANYWHERE] * extra,
                out_specs=[spec for spec, _, _ in outs],
                scratch_shapes=scratch,
            ),
            out_shape=[jax.ShapeDtypeStruct(dims, kind) for _, dims, kind in outs],
            input_output_aliases={
                len(scalars) + k: v for k, v in (aliases or {}).items()
            },
            cost_estimate=estimate,
            compiler_params=pltpu.CompilerParams(vmem_limit_bytes=KERNEL_VMEM),
            name=name,
        )(*scalars, *[value for value, _ in ins], *deps)
        self.last = got[-1]
        return got


class Sum:
    def __init__(self, plan, call, keep, send):
        self.plan, self.call = plan, call
        self.parts, self.count, self.place = [keep], keep.shape[0], 0
        self.move(send)

    def move(self, send):
        got = self.plan.exchange(send, *(order[self.place] for order in self.plan.scatter))
        self.parts.append(got)
        self.place += 1

    def total(self, low, high):
        parts = self.call.pin(self.parts)
        total = parts[0][low:high].astype(F32)
        for part in parts[1:]:
            total = total + part[low:high].astype(F32)
        return total

    def add(self):
        self.count //= 2
        total = self.total(self.count, 2 * self.count)
        self.sent = self.call.hold(total.astype(BF16))
        self.move(self.sent)


class Spread:
    def __init__(self, plan, call, block):
        self.plan, self.call, self.place = plan, call, 0
        self.move(block)

    def move(self, blocks):
        self.blocks = self.call.hold(blocks)
        self.got = self.plan.exchange(blocks, *(order[self.place] for order in self.plan.gather))
        self.place += 1

    def join(self):
        self.move(jnp.concatenate(self.call.pin([self.blocks, self.got]), axis=0))

    def put(self, base, tab, widths, rows):
        count, whole, cols = self.blocks.shape
        step = D if len(widths) > 1 or cols > D else D // 3
        last = widths[0] // step - 1
        ins = [
            (value, pl.BlockSpec((count, whole, step), lambda i, *_: (0, 0, i)))
            for value in (self.blocks, self.got)
        ]
        maps = [lambda i, *_: (0, jnp.minimum(i, last)), lambda i, *_: (0, 0)]
        return self.call(
            functools.partial(place_kernel, len(widths), base, rows),
            (cols // step,),
            [tab],
            ins,
            [
                (pl.BlockSpec((2 * count * rows, step), idx), (2 * count * rows, width), F32)
                for idx, width in zip(maps, widths)
            ],
            [],
            spent(1),
            "place",
        )


def shards(
    plan,
    tokens,
    cotangent,
    mask_pos,
    mask_count,
    w_qkv,
    m_qkv,
    v_qkv,
    w_out,
    m_out,
    v_out,
    w_fc1,
    m_fc1,
    v_fc1,
    w_fc2,
    m_fc2,
    v_fc2,
    vectors,
    m_vec,
    v_vec,
):
    pairs, length, _ = tokens.shape
    slots = mask_pos.shape[1]
    nf, nb, nd = plan.nf, plan.nb, plan.nd
    fi = lax.axis_index("fsdp").astype(jnp.int32)
    bi = lax.axis_index("batch").astype(jnp.int32)
    tab = lax.dynamic_index_in_dim(jnp.asarray(plan.table()), bi * nf + fi, 0, keepdims=False)
    place = owners = tab
    call = Chain()


    def pair_spec(rows, cols):
        return pl.BlockSpec((1, rows, cols), lambda i, *_: (i, 0, 0))

    def piece_ins(pieces):
        return [(value, pl.BlockSpec(memory_space=pltpu.HBM)) for value in pieces]

    sems = pltpu.SemaphoreType.DMA((len(PIECES),))
    rows_d, rows_f = D // nf, FF // nf

    low_vec = vectors.astype(BF16)
    vec_parts = [low_vec, plan.exchange(low_vec, 1)]
    vec_parts += [plan.exchange(part, 2) for part in vec_parts]
    columns = []
    for spot in range(nf):
        chosen = vec_parts[0]
        for mask in range(1, nf):
            chosen = jnp.where((fi ^ mask) == spot, vec_parts[mask], chosen)
        columns.append(chosen)
    vec = jnp.concatenate(columns, axis=1).astype(F32)
    vec = jnp.pad(vec, ((0, 16 - NVEC), (0, 0)))
    vec_in = (vec, full(vec.shape))

    def cast(shard_list, after=()):
        rows = shard_list[0].shape[0]
        half = rows // 2
        cols = sum(value.shape[1] for value in shard_list)
        row = lambda i, place_ref: (i ^ place_ref[1], 0)
        shard, mine = call(
            cast_kernel,
            (2,),
            [place],
            [(value, pl.BlockSpec((half, value.shape[1]), row)) for value in shard_list],
            [
                (pl.BlockSpec((half, cols), row), (rows, cols), BF16),
                (pl.BlockSpec((half, cols), lambda i, *_: (0, 0)), (half, cols), BF16),
            ],
            [],
            spent(rows * cols / 2e5),
            "cast",
            after,
        )
        return [shard, plan.exchange(shard, 1), plan.exchange(mine, 2)]

    def spread_pieces(pieces, dep=None):
        near = pieces[2]
        ready = near if dep is None else later(near, dep)
        other = plan.exchange(ready, *plan.helper)
        return pieces[:2] + [near, other, plan.exchange(ready, 1)]

    def last_piece(pieces, dep=None):
        other = pieces[3]
        return pieces + [plan.exchange(other if dep is None else later(other, dep), 1)]

    set_a = cast([w_qkv])

    perm, tokp, img, dy = call(
        order_kernel,
        (pairs,),
        [mask_count],
        [
            (mask_pos.reshape(pairs, 1, slots), pl.BlockSpec((1, 1, slots), lambda i, *_: (i, 0, 0))),
            (tokens, pair_spec(length, D)),
            (cotangent, pair_spec(length, D)),
        ],
        [
            (pair_spec(length, length), (pairs, length, length), BF16),
            (pair_spec(length, D), (pairs, length, D), BF16),
            (pair_spec(length, LANES), (pairs, length, LANES), BF16),
            (pair_spec(slots, D), (pairs, slots, D), BF16),
        ],
        [],
        spent(6),
        "order",
    )

    set_b = cast([w_out, w_fc1])
    set_a = last_piece(spread_pieces(set_a, [set_b[0]] + vec_parts))

    n1, qkv = call(
        functools.partial(qkv_kernel, rows_d),
        (pairs,),
        [place],
        [(tokp, pair_spec(length, D)), (img, pair_spec(length, LANES)), vec_in] + piece_ins(set_a),
        [
            (pair_spec(length, D), (pairs, length, D), BF16),
            (pair_spec(length, 3 * D), (pairs, length, 3 * D), BF16),
        ],
        [pltpu.VMEM((D, 3 * D), BF16), sems],
        spent(1),
        "qkv",
    )

    set_c = cast([w_fc2])
    near_b = set_b[2]
    set_b = spread_pieces(set_b, set_c[0])
    (mixed,) = call(
        mix_kernel,
        (pairs,),
        [],
        [(qkv, pair_spec(length, 3 * D))],
        [(pair_spec(length, D), (pairs, length, D), BF16)],
        [],
        spent(1),
        "mix",
        [near_b],
    )

    set_b = last_piece(set_b, mixed)
    h1, n2, z, slope = call(
        functools.partial(fc1_kernel, rows_d),
        (pairs,),
        [place],
        [
            (tokp, pair_spec(length, D)),
            (img, pair_spec(length, LANES)),
            (mixed, pair_spec(length, D)),
            vec_in,
        ]
        + piece_ins(set_b),
        [
            (pair_spec(length, D), (pairs, length, D), F32),
            (pair_spec(length, D), (pairs, length, D), BF16),
            (pair_spec(length, FF), (pairs, length, FF), BF16),
            (pair_spec(slots, FF), (pairs, slots, FF), BF16),
        ],
        [pltpu.VMEM((D, D), BF16), pltpu.VMEM((D, FF), BF16), sems, sems],
        spent(18),
        "fc1",
    )

    def top_rows(cols, idx=lambda i, *_: (0, 0, 0)):
        return pl.BlockSpec((pairs, slots, cols), idx)

    def grad_outs(rows, cols, chunk):
        block = rows // nd
        if block % 8:
            return [(pl.BlockSpec((rows, chunk), lambda i, *_: (0, i)), (rows, cols), BF16)]
        spec = pl.BlockSpec((nd // 2, block, chunk), lambda i, *_: (0, 0, i))
        return [(spec, (nd // 2, block, cols), BF16)] * 2

    def grad_sum(outs):
        if len(outs) == 1:
            rows, cols = outs[0].shape
            blocks = jnp.take(outs[0].reshape(nd, rows // nd, cols), tab[OWN : OWN + nd], axis=0)
            outs = [blocks[: nd // 2], blocks[nd // 2 :]]
        return Sum(plan, call, *outs)

    set_c = spread_pieces(set_c, n2)

    chunk = 2 * LANES
    *got, gb2 = call(
        gw2_kernel,
        (D // chunk,),
        [owners],
        [
            (z, top_rows(FF)),
            (dy, top_rows(chunk, lambda i, *_: (0, 0, i))),
        ],
        grad_outs(FF, D, chunk) + [(pl.BlockSpec((1, chunk), lambda i, *_: (0, i)), (1, D), F32)],
        [pltpu.VMEM((FF, pairs * slots), BF16), pltpu.VMEM((FF, chunk), F32)],
        spent(8),
        "gw2",
    )
    sum_2 = grad_sum(got)
    set_c = last_piece(set_c, gb2)

    df, gb1 = call(
        functools.partial(df_kernel, rows_f),
        (PARTS,),
        [place],
        [(dy, top_rows(D)), (slope, top_rows(D, lambda i, *_: (0, 0, i)))] + piece_ins(set_c),
        [
            (pl.BlockSpec((pairs * slots, D), lambda i, *_: (0, i)), (pairs * slots, FF), BF16),
            (pl.BlockSpec((1, D), lambda i, *_: (0, i)), (1, FF), F32),
        ],
        [pltpu.VMEM((FF, D), BF16), sems],
        spent(7),
        "df",
    )
    sum_2.add()

    some = 2 if pairs % 2 == 0 else 1
    some_spec = pl.BlockSpec((some, slots, D), lambda i, *_: (i, 0, 0))
    dh, dhr, da, mlp_sum = call(
        functools.partial(mlp_back_kernel, rows_d),
        (pairs // some,),
        [place],
        [
            (df, pl.BlockSpec((some * slots, FF), lambda i, *_: (i, 0))),
            (dy, some_spec),
            (h1, some_spec),
            vec_in,
        ]
        + piece_ins(set_b),
        [
            (some_spec, (pairs, slots, D), F32),
            (some_spec, (pairs, slots, D), BF16),
            (some_spec, (pairs, slots, D), BF16),
            (full((8, D)), (8, D), F32),
        ],
        [pltpu.VMEM((D, FF), BF16), pltpu.VMEM((D, D), BF16), sems, sems],
        spent(10),
        "mlp_back",
    )

    got = call(
        gw1o_kernel,
        (PARTS + 1,),
        [owners],
        [
            (n2, top_rows(D)),
            (
                df,
                pl.BlockSpec((pairs * slots, D), lambda i, *_: (0, jnp.minimum(i, PARTS - 1))),
            ),
            (mixed, top_rows(D)),
            (dhr, top_rows(D)),
        ],
        grad_outs(D, FF + D, D),
        [pltpu.VMEM((D, pairs * slots), BF16), pltpu.VMEM((D, D), F32)],
        spent(9),
        "gw1o",
    )
    sum_1 = grad_sum(got)
    sum_2.add()

    part_pairs = pairs // 2 if pairs % 2 == 0 else pairs
    back = None
    for number in range(pairs // part_pairs):
        base = number * part_pairs
        at = lambda rows, cols, base=base: pl.BlockSpec(
            (1, rows, cols), lambda i, *_: (base + i, 0, 0)
        )
        ins = [(qkv, at(length, 3 * D)), (da, at(slots, D))]
        if back is not None:
            ins += [(back[0], ANYWHERE), (back[1], ANYWHERE), (back[2], full((8, D)))]
        back = call(
            functools.partial(attn_back_kernel, back is not None),
            (part_pairs,),
            [],
            ins,
            [
                (at(slots, D), (pairs, slots, D), BF16),
                (at(length, 2 * D), (pairs, length, 2 * D), BF16),
                (full((8, D)), (8, D), F32),
            ],
            [],
            spent(12),
            "attn_back",
            aliases=None if back is None else {2: 0, 3: 1},
        )
        if number == 0:
            sum_1.add()
        sum_2.add()
    dq, dkv, attn_sum = back

    got = call(
        gqkv_kernel,
        (3,),
        [owners],
        [
            (n1, full((pairs, length, D))),
            (dq, full((pairs, slots, D))),
            (
                dkv,
                pl.BlockSpec((pairs, length, D), lambda i, *_: (0, 0, jnp.where(i == 2, 1, 0))),
            ),
        ],
        grad_outs(D, 3 * D, D),
        [pltpu.VMEM((D, pairs * length), BF16), pltpu.VMEM((D, D), F32)],
        spent(9),
        "gqkv",
    )
    sum_3 = grad_sum(got)
    sum_1.add()

    fallback = (D // nd) % 8 != 0 or (FF // nd) % 8 != 0
    places = OWN + nd
    order = tab[places + nb :]

    held = jnp.concatenate([m_vec, v_vec], axis=0).reshape(-1)
    held = jnp.pad(held, (0, -held.size % 8)).reshape(8, -1)
    riders = jnp.concatenate(split_two(held), axis=1)
    rider_cols = riders.shape[1]
    riders = jnp.pad(riders, ((0, 0), (0, D - rider_cols)))

    def finish(total, which, masters, moments, extra=None):
        _, rows, cols = total.parts[0].shape
        grad = total.total(0, 1)[0]
        start, news, made = 0, [], []
        for kind, master, (first, second) in zip(which, masters, moments):
            width = master.shape[1]
            own = lax.dynamic_slice_in_dim(master, bi * rows, rows, 0)
            new_w, new_m, new_v = adamw(
                own,
                grad[:, start : start + width],
                first,
                second,
                STEP_RATES[kind],
                DECAY_RATES[kind],
            )
            news.append(new_w.astype(BF16))
            made += [new_m, new_v]
            start += width
        block = jnp.concatenate(news, axis=1)
        if extra is not None:
            block = jnp.concatenate([block, extra], axis=0)
        return Spread(plan, call, block[None]), made

    def put(moved, widths, rows):
        if not fallback:
            return moved.put(places, tab, widths, rows)
        blocks = jnp.concatenate([moved.blocks, moved.got], axis=0)[:, :rows]
        cols = blocks.shape[2]
        blocks = jnp.take(blocks, order, axis=0).reshape(nb * rows, cols).astype(F32)
        cuts = np.cumsum([0] + list(widths))
        return [blocks[:, a:b] for a, b in zip(cuts[:-1], cuts[1:])]

    sum_3.add()

    grad_tokens, vec_sum = call(
        functools.partial(grad_in_kernel, rows_d),
        (pairs,),
        [place],
        [
            (tokp, pair_spec(length, D)),
            (img, pair_spec(length, LANES)),
            vec_in,
            (dq, pair_spec(slots, D)),
            (dkv, pair_spec(length, 2 * D)),
            (dh, pair_spec(slots, D)),
            (perm, pair_spec(length, length)),
            (attn_sum, full((8, D))),
            (mlp_sum, full((8, D))),
            (gb1, full((1, FF))),
            (gb2, full((1, D))),
        ]
        + piece_ins(set_a),
        [
            (pair_spec(length, D), (pairs, length, D), F32),
            (full((16, D)), (16, D), F32),
        ],
        [pltpu.VMEM((D, 3 * D), BF16), sems],
        spent(15),
        "grad_in",
    )

    vec_gens = [1, 2] + plan.batch
    vec_got = plan.exchange(vec_sum, vec_gens[0])

    last = plan.bbits
    sum_3.add()
    sum_1.add()
    while sum_2.count > 1:
        sum_2.add()
    moved_2, (new_m2, new_v2) = finish(sum_2, (3,), (w_fc2,), ((m_fc2, v_fc2),), riders)

    (layer_out,) = call(
        functools.partial(out_kernel, rows_f),
        (pairs,),
        [place],
        [
            (z, pair_spec(length, FF)),
            (h1, pair_spec(length, D)),
            vec_in,
            (perm, pair_spec(length, length)),
        ]
        + piece_ins(set_c),
        [(pair_spec(length, D), (pairs, length, D), BF16)],
        [pltpu.VMEM((FF, D), BF16), sems],
        spent(13),
        "out",
    )

    vec_place = 1

    def vec_step():
        nonlocal vec_sum, vec_got, vec_place
        if vec_place > len(vec_gens):
            return
        one, two = call.pin([vec_sum, vec_got])
        vec_sum = one + two
        if vec_place < len(vec_gens):
            vec_got = plan.exchange(vec_sum, vec_gens[vec_place])
        vec_place += 1

    moved_1 = moved_3 = None
    while moved_3 is None or moved_3.place < last:
        token = None
        if sum_3.count > 1:
            sum_3.add()
            token = sum_3.sent
        elif moved_3 is None:
            moved_3, (new_mq, new_vq) = finish(sum_3, (0,), (w_qkv,), ((m_qkv, v_qkv),))
            token = moved_3.blocks
        else:
            moved_3.join()
            token = moved_3.blocks
        if sum_1.count > 1:
            sum_1.add()
        elif moved_1 is None:
            moved_1, (new_m1, new_v1, new_mo, new_vo) = finish(
                sum_1, (2, 1), (w_fc1, w_out), ((m_fc1, v_fc1), (m_out, v_out))
            )
        elif moved_1.place < last:
            moved_1.join()
        if moved_2.place < last:
            moved_2.join()
        vec_step()
        call.last = token
    while len(vec_gens) >= vec_place:
        vec_step()
    while moved_1.place < last:
        moved_1.join()
    while moved_2.place < last:
        moved_2.join()
    call.waiting = []
    (new_2,) = put(moved_2, (D,), FF // nd)
    new_1, new_o = put(moved_1, (FF, D), D // nd)
    (new_q,) = put(moved_3, (3 * D,), D // nd)

    own_cols = D // nd
    got = jnp.concatenate([moved_2.blocks[:, FF // nd :], moved_2.got[:, FF // nd :]], axis=0)
    half = rider_cols // 2
    held = got[:, :, :half].astype(F32) + got[:, :, half:rider_cols].astype(F32)
    held = held.reshape(nb, -1)[:, : 2 * NVEC * own_cols].reshape(nb, 2 * NVEC, own_cols)
    held = jnp.take(held, order, axis=0)
    states = jnp.transpose(held, (1, 0, 2)).reshape(2 * NVEC, nb * own_cols)
    grad_vec = lax.dynamic_slice_in_dim(vec_sum[:NVEC], fi * nb * own_cols, nb * own_cols, 1)
    vec_new, _, _ = adamw(
        vectors, grad_vec, states[:NVEC], states[NVEC:], STEP_RATES[4], DECAY_RATES[4]
    )
    own_grad = lax.dynamic_slice_in_dim(grad_vec, bi * own_cols, own_cols, 1)
    _, new_mv, new_vv = adamw(0.0, own_grad, m_vec, v_vec, STEP_RATES[4], DECAY_RATES[4])

    return (
        layer_out,
        grad_tokens,
        new_q,
        new_mq,
        new_vq,
        new_o,
        new_mo,
        new_vo,
        new_1,
        new_m1,
        new_v1,
        new_2,
        new_m2,
        new_v2,
        vec_new,
        new_mv,
        new_vv,
    )


def solution(mesh):
    pairs = P(("batch", "fsdp"), None, None)
    weight = P("fsdp", None)
    state = P(("fsdp", "batch"), None)
    vec_state = P(None, ("fsdp", "batch"))
    matrix = (weight, state, state)
    return jax.shard_map(
        functools.partial(shards, Plan(mesh)),
        mesh=mesh,
        in_specs=(pairs, pairs, P(("batch", "fsdp"), None), P(("batch", "fsdp")))
        + matrix * 4
        + (P(None, "fsdp"), vec_state, vec_state),
        out_specs=(pairs, pairs) + matrix * 4 + (P(None, "fsdp"), vec_state, vec_state),
        check_vma=False,
    )
```

profile of v0, /device:TPU:0, one launch (start us, length us, event | category | flops | bytes accessed | tf_op | source)
XLA Modules:
  0.0 260.2 jit_solution(4449226747923132478)
XLA Ops:
  1.9 2.5 collective-permute-start.2
  9.2 3.3 %order.1 = (bf16[4,256,256]{2,1,0:T(8,128)(2,1)S(1)}, bf16[4,256,768]{2,1,0:T(8,128)(2,1)S(1)}, bf16[4,256,128]{2,1,0:T(8,128)(2,1)S(1)}, bf16[4,128,768]{2,1,0:T(8,128)(2,1)S(1)}) custom-call(s32[4]{0:T(128)S(1)} %copy-done.19, s32[4,1,128]{2,1,0:T(1,128)S(1)} %bitcast.29, bf16[4,256,768]{2,1,0:T(8,128)(2,1)S(1)} %copy-done.4, ...), custom_call_target="tpu_custom_call" | custom-call | flops 17999998976 | bytes 60000000 | tf_op jit(solution)/shard_map/order/pallas_call | solution.py:579
  16.7 3.6 %collective-permute-done.1 = bf16[14,192]{1,0:T(8,128)(2,1)S(1)} collective-permute-done((bf16[14,192]{1,0:T(8,128)(2,1)S(1)}, bf16[14,192]{1,0:T(8,128)(2,1)S(1)}, u32[]{:S(2)}, u32[]{:S(2)}) %collective-permute-start.1) | collective-permute-done | bytes 5408 | tf_op jit(solution)/shard_map/ppermute | solution.py:112
  22.4 6.6 %collective-permute-done.5.refs_7_.refs_15_ = bf16[96,2304]{1,0:T(8,128)(2,1)} collective-permute-done((bf16[96,2304]{1,0:T(8,128)(2,1)}, bf16[96,2304]{1,0:T(8,128)(2,1)}, u32[]{:S(2)}, u32[]{:S(2)}) %collective-permute-start.5) | collective-permute-done | bytes 442400 | tf_op jit(solution)/shard_map/ppermute | solution.py:112
  33.5 8.0 %qkv.1 = (bf16[4,256,768]{2,1,0:T(8,128)(2,1)S(1)}, bf16[4,256,2304]{2,1,0:T(8,128)(2,1)S(1)}) custom-call(s32[52]{0:T(128)S(1)} %get-tuple-element.292.refs_0_, bf16[4,256,768]{2,1,0:T(8,128)(2,1)S(1)} %copy-done.26, bf16[4,256,128]{2,1,0:T(8,128)(2,1)S(1)} %copy-done.31, f32[16,768]{1,0:T(8,128)S(1)} %fusion.12.refs_3_.refs_4_, ...), custom_call_target="tpu_custom_call" | custom-call | flops 3000000000 | bytes 10000000 | tf_op jit(solution)/shard_map/qkv/pallas_call | solution.py:579
  42.7 2.2 cast.5
  44.8 3.3 %collective-permute-done.8.refs_1_.refs_7_ = bf16[96,3840]{1,0:T(8,128)(2,1)} collective-permute-done((bf16[96,3840]{1,0:T(8,128)(2,1)}, bf16[96,3840]{1,0:T(8,128)(2,1)}, u32[]{:S(2)}, u32[]{:S(2)}) %collective-permute-start.8) | collective-permute-done | bytes 737312 | tf_op jit(solution)/shard_map/ppermute | solution.py:112
  50.2 8.3 %mix.1.refs_3_.refs_11_ = bf16[4,256,768]{2,1,0:T(8,128)(2,1)S(1)} custom-call(bf16[4,256,2304]{2,1,0:T(8,128)(2,1)S(1)} %get-tuple-element.151.refs_2_.refs_0_, bf16[96,3840]{1,0:T(8,128)(2,1)} %collective-permute-done.8.refs_1_.refs_7_, bf16[384,768]{1,0:T(8,128)(2,1)S(1)} %get-tuple-element.152.refs_2_), custom_call_target="tpu_custom_call" | custom-call | flops 3000000000 | bytes 10000000 | tf_op jit(solution)/shard_map/mix/pallas_call | solution.py:579
  62.1 13.5 %fc1.1 = (f32[4,256,768]{2,1,0:T(8,128)S(1)}, bf16[4,256,768]{2,1,0:T(8,128)(2,1)S(1)}, bf16[4,256,3072]{2,1,0:T(8,128)(2,1)S(1)}, bf16[4,128,3072]{2,1,0:T(8,128)(2,1)S(1)}) custom-call(s32[52]{0:T(128)S(1)} %get-tuple-element.292.refs_0_, bf16[4,256,768]{2,1,0:T(8,128)(2,1)S(1)} %copy-done.26, bf16[4,256,128]{2,1,0:T(8,128)(2,1)S(1)} %copy-done.32, ...), custom_call_target="tpu_custom_call" | custom-call | flops 54000001024 | bytes 180000000 | tf_op jit(solution)/shard_map/fc1/pallas_call | solution.py:579
  77.3 6.6 %gw2.1 = (bf16[16,96,768]{2,1,0:T(8,128)(2,1)S(1)}, bf16[16,96,768]{2,1,0:T(8,128)(2,1)}, f32[1,768]{1,0:T(1,128)S(1)}) custom-call(s32[52]{0:T(128)S(1)} %get-tuple-element.292.refs_0_, bf16[4,256,3072]{2,1,0:T(8,128)(2,1)S(1)} %get-tuple-element.156.refs_1_, bf16[4,128,768]{2,1,0:T(8,128)(2,1)S(1)} %copy-done.38, ...), custom_call_target="tpu_custom_call" | custom-call | flops 24000000000 | bytes 80000000 | tf_op jit(solution)/shard_map/gw2/pallas_call | solution.py:579
  91.4 7.1 %df.1 = (bf16[512,3072]{1,0:T(8,128)(2,1)S(1)}, f32[1,3072]{1,0:T(1,128)S(1)}) custom-call(s32[52]{0:T(128)S(1)} %get-tuple-element.292.refs_0_, bf16[4,128,768]{2,1,0:T(8,128)(2,1)S(1)} %copy-done.39, bf16[4,128,3072]{2,1,0:T(8,128)(2,1)S(1)} %copy-done.36, bf16[768,768]{1,0:T(8,128)(2,1)} %get-tuple-element.153.refs_3_.refs_5_, ...), custom_call_target="tpu_custom_call" | custom-call | flops 20999999488 | bytes 70000000 | tf_op jit(solution)/shard_map/df/pallas_call | solution.py:579
  100.7 7.6 %mlp_back.1 = (f32[4,128,768]{2,1,0:T(8,128)S(1)}, bf16[4,128,768]{2,1,0:T(8,128)(2,1)S(1)}, bf16[4,128,768]{2,1,0:T(8,128)(2,1)S(1)}, f32[8,768]{1,0:T(8,128)S(1)}) custom-call(s32[52]{0:T(128)S(1)} %get-tuple-element.292.refs_0_, bf16[512,3072]{1,0:T(8,128)(2,1)S(1)} %get-tuple-element.165.refs_1_.refs_2_, bf16[4,128,768]{2,1,0:T(8,128)(2,1)S(1)} %copy-done.39, ...), custom_call_target="tpu_custom_call" | custom-call | flops 30000001024 | bytes 100000000 | tf_op jit(solution)/shard_map/mlp_back/pallas_call | solution.py:579
  108.3 6.9 %gw1o.1 = (bf16[16,24,3840]{2,1,0:T(8,128)(2,1)S(1)}, bf16[16,24,3840]{2,1,0:T(8,128)(2,1)S(1)}) custom-call(s32[52]{0:T(128)S(1)} %get-tuple-element.292.refs_0_, bf16[4,256,768]{2,1,0:T(8,128)(2,1)S(1)} %copy-done.44, bf16[512,3072]{1,0:T(8,128)(2,1)S(1)} %get-tuple-element.165.refs_1_.refs_2_, bf16[4,256,768]{2,1,0:T(8,128)(2,1)S(1)} %copy-done.24, ...), custom_call_target="tpu_custom_call" | custom-call | flops 27000000512 | bytes 90000000 | tf_op jit(solution)/shard_map/gw1o/pallas_call | solution.py:579
  119.4 11.3 %attn_back.2 = (bf16[4,128,768]{2,1,0:T(8,128)(2,1)S(1)}, bf16[4,256,1536]{2,1,0:T(8,128)(2,1)S(1)}, f32[8,768]{1,0:T(8,128)S(1)}) custom-call(bf16[4,256,2304]{2,1,0:T(8,128)(2,1)S(1)} %bitcast.31, bf16[4,128,768]{2,1,0:T(8,128)(2,1)S(1)} %get-tuple-element.171.refs_1_, bf16[4,96,768]{2,1,0:T(8,128)(2,1)S(1)} %add_convert_fusion.4.refs_2_, ...), custom_call_target="tpu_custom_call" | custom-call | flops 35999997952 | bytes 120000000 | tf_op jit(solution)/shard_map/attn_back/pallas_call | solution.py:579
  134.4 11.3 %attn_back.3 = (bf16[4,128,768]{2,1,0:T(8,128)(2,1)S(1)}, bf16[4,256,1536]{2,1,0:T(8,128)(2,1)S(1)}, f32[8,768]{1,0:T(8,128)S(1)}) custom-call(bf16[4,256,2304]{2,1,0:T(8,128)(2,1)S(1)} %bitcast.31, bf16[4,128,768]{2,1,0:T(8,128)(2,1)S(1)} %get-tuple-element.171.refs_1_, ...), custom_call_target="tpu_custom_call", output_to_operand_aliasing={{0}: (2, {}), {1}: (3, {})} | custom-call | flops 35999997952 | bytes 120000000 | tf_op jit(solution)/shard_map/attn_back/pallas_call | solution.py:579
  146.8 6.1 %gqkv.1 = (bf16[16,24,2304]{2,1,0:T(8,128)(2,1)S(1)}, bf16[16,24,2304]{2,1,0:T(8,128)(2,1)S(1)}) custom-call(s32[52]{0:T(128)S(1)} %get-tuple-element.292.refs_0_, bf16[4,256,768]{2,1,0:T(8,128)(2,1)S(1)} %copy-done.29, bf16[4,128,768]{2,1,0:T(8,128)(2,1)S(1)} %get-tuple-element.188.refs_2_.refs_4_, ...), custom_call_target="tpu_custom_call" | custom-call | flops 27000000512 | bytes 90000000 | tf_op jit(solution)/shard_map/gqkv/pallas_call | solution.py:579
  153.2 2.5 collective-permute-start.27
  158.6 12.0 %grad_in.1 = (f32[4,256,768]{2,1,0:T(8,128)}, f32[16,768]{1,0:T(8,128)S(1)}) custom-call(s32[52]{0:T(128)S(1)} %get-tuple-element.292.refs_0_, bf16[4,256,768]{2,1,0:T(8,128)(2,1)S(1)} %copy-done.27, bf16[4,256,128]{2,1,0:T(8,128)(2,1)S(1)} %copy-done.33, f32[16,768]{1,0:T(8,128)S(1)} %fusion.12.refs_3_.refs_4_, ...), custom_call_target="tpu_custom_call" | custom-call | flops 44999999488 | bytes 150000000 | tf_op jit(solution)/shard_map/grad_in/pallas_call | solution.py:579
  170.7 2.1 subtract_convert_fusion.1
  172.8 2.4 collective-permute-start.39
  177.2 10.7 %out.1 = bf16[4,256,768]{2,1,0:T(8,128)(2,1)} custom-call(s32[52]{0:T(128)S(1)} %get-tuple-element.292.refs_0_, bf16[4,256,3072]{2,1,0:T(8,128)(2,1)S(1)} %bitcast.33, f32[4,256,768]{2,1,0:T(8,128)S(1)} %copy-done.42, f32[16,768]{1,0:T(8,128)S(1)} %fusion.12.refs_3_.refs_4_, bf16[4,256,256]{2,1,0:T(8,128)(2,1)S(1)} %copy-done.46, ...), custom_call_target="tpu_custom_call" | custom-call | flops 38999998464 | bytes 130000000 | tf_op jit(solution)/shard_map/out/pallas_call | solution.py:579
  193.4 9.1 %collective-permute-done.40 = bf16[2,104,768]{2,1,0:T(8,128)(2,1)S(1)} collective-permute-done((bf16[2,104,768]{2,1,0:T(8,128)(2,1)S(1)}, bf16[2,104,768]{2,1,0:T(8,128)(2,1)S(1)}, u32[]{:S(2)}, u32[]{:S(2)}) %collective-permute-start.40) | collective-permute-done | bytes 319520 | tf_op jit(solution)/shard_map/ppermute | solution.py:112
  202.7 2.1 collective-permute-start.44
  208.6 2.4 collective-permute-start.36
  213.6 2.5 collective-permute-done.36
  221.6 4.2 %collective-permute-start.37 = (bf16[2,24,3840]{2,1,0:T(8,128)(2,1)S(1)}, bf16[2,24,3840]{2,1,0:T(8,128)(2,1)S(1)}, u32[]{:S(2)}, u32[]{:S(2)}) collective-permute-start(bf16[2,24,3840]{2,1,0:T(8,128)(2,1)S(1)} %constant_dynamic-update-slice_fusion.4), channel_id=1, source_target_pairs={{0,8},{1,5},{2,10},{3,7},{4,12},{5,1},{6,14},{7,3},{8,0},{9,13},{1... | collective-permute-start | bytes 1105928 | tf_op jit(solution)/shard_map/ppermute | solution.py:112
  225.9 3.0 %collective-permute-start.46 = (f32[16,768]{1,0:T(8,128)S(1)}, f32[16,768]{1,0:T(8,128)S(1)}, u32[]{:S(2)}, u32[]{:S(2)}) collective-permute-start(f32[16,768]{1,0:T(8,128)S(1)} %add.349), channel_id=1, source_target_pairs={{0,24},{1,25},{2,26},{3,27},{4,28},{5,29},{6,30},{7,31},{8,16},{9,... | collective-permute-start | bytes 147464 | tf_op jit(solution)/shard_map/ppermute | solution.py:112
  230.6 8.6 %collective-permute-done.46 = f32[16,768]{1,0:T(8,128)S(1)} collective-permute-done((f32[16,768]{1,0:T(8,128)S(1)}, f32[16,768]{1,0:T(8,128)S(1)}, u32[]{:S(2)}, u32[]{:S(2)}) %collective-permute-start.46) | collective-permute-done | bytes 49184 | tf_op jit(solution)/shard_map/ppermute | solution.py:112
  245.2 2.5 place.3.refs_3_
  247.7 3.9 %collective-permute-done.38.refs_2_ = bf16[4,24,3840]{2,1,0:T(8,128)(2,1)S(1)} collective-permute-done((bf16[4,24,3840]{2,1,0:T(8,128)(2,1)S(1)}, bf16[4,24,3840]{2,1,0:T(8,128)(2,1)S(1)}, u32[]{:S(2)}, u32[]{:S(2)}) %collective-permute-start.38) | collective-permute-done | bytes 737312 | tf_op jit(solution)/shard_map/ppermute | solution.py:112
  253.2 3.5 %place.4 = (f32[192,3072]{1,0:T(8,128)}, f32[192,768]{1,0:T(8,128)}) custom-call(s32[52]{0:T(128)S(1)} %get-tuple-element.292.refs_0_, bf16[4,24,3840]{2,1,0:T(8,128)(2,1)S(1)} %constant_dynamic-update-slice_fusion.6.refs_1_, bf16[4,24,3840]{2,1,0:T(8,128)(2,1)S(1)} %collective-permute-done.38.refs_2_, f32[768,768]{1,0:T(8,128)S(1)} %copy-done.20), custom_call_target="tpu_custom_call" | custom-call | flops 3000000000 | bytes 10000000 | tf_op jit(solution)/shard_map/place/pallas_call | solution.py:579
  257.8 2.4 place.5
  (277 shorter events, 76.6 us)
Async XLA Ops:
  1.4 13.0 %collective-permute-start = (bf16[14,192]{1,0:T(8,128)(2,1)S(1)}, bf16[14,192]{1,0:T(8,128)(2,1)S(1)}, u32[]{:S(2)}, u32[]{:S(2)}) collective-permute-start(bf16[14,192]{1,0:T(8,128)(2,1)S(1)} %convert_element_type.251), channel_id=1, source_target_pairs={{0,1},{1,0},{2,3},{3,2},{4,5},{5,4},{6,7},{7,6},{8,9},{9,8},{10,11... | collective-permute-start | bytes 16136 | tf_op jit(solution)/shard_map/ppermute | solution.py:112
  1.9 14.9 %collective-permute-start.2 = (bf16[14,192]{1,0:T(8,128)(2,1)S(1)}, bf16[14,192]{1,0:T(8,128)(2,1)S(1)}, u32[]{:S(2)}, u32[]{:S(2)}) collective-permute-start(bf16[14,192]{1,0:T(8,128)(2,1)S(1)} %convert_element_type.251), channel_id=1, source_target_pairs={{0,2},{1,3},{2,0},{3,1},{4,6},{5,7},{6,4},{7,5},{8,10},{9,11},{10,... | collective-permute-start | bytes 16136 | tf_op jit(solution)/shard_map/ppermute | solution.py:112
  7.8 12.6 %collective-permute-start.4 = (bf16[96,2304]{1,0:T(8,128)(2,1)S(1)}, bf16[96,2304]{1,0:T(8,128)(2,1)}, u32[]{:S(2)}, u32[]{:S(2)}) collective-permute-start(bf16[96,2304]{1,0:T(8,128)(2,1)S(1)} %get-tuple-element.143.refs_4_), channel_id=1, source_target_pairs={{0,2},{1,3},{2,0},{3,1},{4,6},{5,7},{6,4},{7,5},{8,10},{9,11},{10,... | collective-permute-start | bytes 1327112 | tf_op jit(solution)/shard_map/ppermute | solution.py:112
  29.0 19.2 %collective-permute-start.8 = (bf16[96,3840]{1,0:T(8,128)(2,1)}, bf16[96,3840]{1,0:T(8,128)(2,1)}, u32[]{:S(2)}, u32[]{:S(2)}) collective-permute-start(bf16[96,3840]{1,0:T(8,128)(2,1)} %get-tuple-element.150.refs_10_), channel_id=1, source_target_pairs={{0,2},{1,3},{2,0},{3,1},{4,6},{5,7},{6,4},{7,5},{8,10},{9,11},{10,... | collective-permute-start | bytes 2211848 | tf_op jit(solution)/shard_map/ppermute | solution.py:112
  48.2 11.7 %collective-permute-start.10 = (bf16[96,3840]{1,0:T(8,128)(2,1)}, bf16[96,3840]{1,0:T(8,128)(2,1)S(1)}, u32[]{:S(2)}, u32[]{:S(2)}) collective-permute-start(bf16[96,3840]{1,0:T(8,128)(2,1)} %collective-permute-done.8.refs_1_.refs_7_), channel_id=1, source_target_pairs={{0,4},{1,9},{2,6},{3,11},{4,0},{5,13},{6,2},{7,15},{8,12},{9,1},{1... | collective-permute-start | bytes 2211848 | tf_op jit(solution)/shard_map/ppermute | solution.py:112
  59.9 15.8 %collective-permute-start.14 = (bf16[384,768]{1,0:T(8,128)(2,1)S(1)}, bf16[384,768]{1,0:T(8,128)(2,1)}, u32[]{:S(2)}, u32[]{:S(2)}) collective-permute-start(bf16[384,768]{1,0:T(8,128)(2,1)S(1)} %get-tuple-element.152.refs_2_), channel_id=1, source_target_pairs={{0,2},{1,3},{2,0},{3,1},{4,6},{5,7},{6,4},{7,5},{8,10},{9,11},{10,... | collective-permute-start | bytes 1769480 | tf_op jit(solution)/shard_map/ppermute | solution.py:112
  60.2 27.0 %collective-permute-start.13 = (bf16[768,768]{1,0:T(8,128)(2,1)}, bf16[768,768]{1,0:T(8,128)(2,1)}, u32[]{:S(2)}, u32[]{:S(2)}) collective-permute-start(bf16[768,768]{1,0:T(8,128)(2,1)} %get-tuple-element.153.refs_3_.refs_5_), channel_id=1, source_target_pairs={{0,1},{1,0},{2,3},{3,2},{4,5},{5,4},{6,7},{7,6},{8,9},{9,8},{10,11... | collective-permute-start | bytes 3538952 | tf_op jit(solution)/shard_map/ppermute | solution.py:112
  86.0 12.5 %collective-permute-start.18 = (bf16[16,96,768]{2,1,0:T(8,128)(2,1)}, bf16[16,96,768]{2,1,0:T(8,128)(2,1)}, u32[]{:S(2)}, u32[]{:S(2)}) collective-permute-start(bf16[16,96,768]{2,1,0:T(8,128)(2,1)} %get-tuple-element.167), channel_id=1, source_target_pairs={{0,1},{1,0},{2,3},{3,2},{4,5},{5,4},{6,7},{7,6},{8,9},{9,8},{10,11... | collective-permute-start | bytes 7077896 | tf_op jit(solution)/shard_map/ppermute | solution.py:112
  100.2 16.3 %collective-permute-start.19 = (bf16[8,96,768]{2,1,0:T(8,128)(2,1)S(1)}, bf16[8,96,768]{2,1,0:T(8,128)(2,1)S(1)}, u32[]{:S(2)}, u32[]{:S(2)}) collective-permute-start(bf16[8,96,768]{2,1,0:T(8,128)(2,1)S(1)} %add_convert_fusion.1.refs_11_), channel_id=1, source_target_pairs={{0,2},{1,5},{2,0},{3,7},{4,6},{5,1},{6,4},{7,3},{8,10},{9,13},{10,... | collective-permute-start | bytes 3538952 | tf_op jit(solution)/shard_map/ppermute | solution.py:112
  115.2 18.2 %collective-permute-start.20 = (bf16[16,24,3840]{2,1,0:T(8,128)(2,1)S(1)}, bf16[16,24,3840]{2,1,0:T(8,128)(2,1)S(1)}, u32[]{:S(2)}, u32[]{:S(2)}) collective-permute-start(bf16[16,24,3840]{2,1,0:T(8,128)(2,1)S(1)} %get-tuple-element.174.refs_3_), channel_id=1, source_target_pairs={{0,1},{1,0},{2,3},{3,2},{4,5},{5,4},{6,7},{7,6},{8,9},{9,8},{10,11... | collective-permute-start | bytes 8847368 | tf_op jit(solution)/shard_map/ppermute | solution.py:112
  117.8 13.0 %collective-permute-start.21 = (bf16[4,96,768]{2,1,0:T(8,128)(2,1)S(1)}, bf16[4,96,768]{2,1,0:T(8,128)(2,1)S(1)}, u32[]{:S(2)}, u32[]{:S(2)}) collective-permute-start(bf16[4,96,768]{2,1,0:T(8,128)(2,1)S(1)} %add_convert_fusion.4.refs_2_), channel_id=1, source_target_pairs={{0,8},{1,3},{2,10},{3,1},{4,12},{5,7},{6,14},{7,5},{8,0},{9,11},{1... | collective-permute-start | bytes 1769480 | tf_op jit(solution)/shard_map/ppermute | solution.py:112
  131.9 13.9 %collective-permute-start.22 = (bf16[2,96,768]{2,1,0:T(8,128)(2,1)S(1)}, bf16[2,96,768]{2,1,0:T(8,128)(2,1)S(1)}, u32[]{:S(2)}, u32[]{:S(2)}) collective-permute-start(bf16[2,96,768]{2,1,0:T(8,128)(2,1)S(1)} %add_convert_fusion.7.refs_6_), channel_id=1, source_target_pairs={{0,4},{1,9},{2,6},{3,11},{4,0},{5,13},{6,2},{7,15},{8,12},{9,1},{1... | collective-permute-start | bytes 884744 | tf_op jit(solution)/shard_map/ppermute | solution.py:112
  133.8 21.9 %collective-permute-start.25 = (bf16[8,24,3840]{2,1,0:T(8,128)(2,1)S(1)}, bf16[8,24,3840]{2,1,0:T(8,128)(2,1)S(1)}, u32[]{:S(2)}, u32[]{:S(2)}) collective-permute-start(bf16[8,24,3840]{2,1,0:T(8,128)(2,1)S(1)} %add_convert_fusion.refs_5_), channel_id=1, source_target_pairs={{0,2},{1,5},{2,0},{3,7},{4,6},{5,1},{6,4},{7,3},{8,10},{9,13},{10,... | collective-permute-start | bytes 4423688 | tf_op jit(solution)/shard_map/ppermute | solution.py:112
  153.2 17.4 %collective-permute-start.27 = (bf16[1,96,768]{2,1,0:T(8,128)(2,1)S(1)}, bf16[1,96,768]{2,1,0:T(8,128)(2,1)S(1)}, u32[]{:S(2)}, u32[]{:S(2)}) collective-permute-start(bf16[1,96,768]{2,1,0:T(8,128)(2,1)S(1)} %add_convert_fusion.10.refs_4_), channel_id=1, source_target_pairs={{0,24},{1,25},{2,26},{3,27},{4,28},{5,29},{6,30},{7,31},{8,16},{9,... | collective-permute-start | bytes 442376 | tf_op jit(solution)/shard_map/ppermute | solution.py:112
  156.0 19.3 %collective-permute-start.26 = (bf16[4,24,3840]{2,1,0:T(8,128)(2,1)S(1)}, bf16[4,24,3840]{2,1,0:T(8,128)(2,1)S(1)}, u32[]{:S(2)}, u32[]{:S(2)}) collective-permute-start(bf16[4,24,3840]{2,1,0:T(8,128)(2,1)S(1)} %add_convert_fusion.3.refs_18_), channel_id=1, source_target_pairs={{0,8},{1,3},{2,10},{3,1},{4,12},{5,7},{6,14},{7,5},{8,0},{9,11},{1... | collective-permute-start | bytes 2211848 | tf_op jit(solution)/shard_map/ppermute | solution.py:112
  156.9 19.3 %collective-permute-start.24 = (bf16[8,24,2304]{2,1,0:T(8,128)(2,1)S(1)}, bf16[8,24,2304]{2,1,0:T(8,128)(2,1)S(1)}, u32[]{:S(2)}, u32[]{:S(2)}) collective-permute-start(bf16[8,24,2304]{2,1,0:T(8,128)(2,1)S(1)} %add_convert_fusion.2.refs_19_), channel_id=1, source_target_pairs={{0,2},{1,5},{2,0},{3,7},{4,6},{5,1},{6,4},{7,3},{8,10},{9,13},{10,... | collective-permute-start | bytes 2654216 | tf_op jit(solution)/shard_map/ppermute | solution.py:112
  170.6 17.3 %collective-permute-start.42 = (f32[16,768]{1,0:T(8,128)S(1)}, f32[16,768]{1,0:T(8,128)S(1)}, u32[]{:S(2)}, u32[]{:S(2)}) collective-permute-start(f32[16,768]{1,0:T(8,128)S(1)} %get-tuple-element.259.refs_14_), channel_id=1, source_target_pairs={{0,1},{1,0},{2,3},{3,2},{4,5},{5,4},{6,7},{7,6},{8,9},{9,8},{10,11... | collective-permute-start | bytes 147464 | tf_op jit(solution)/shard_map/ppermute | solution.py:112
  172.8 16.6 %collective-permute-start.39 = (bf16[1,104,768]{2,1,0:T(8,128)(2,1)S(1)}, bf16[1,104,768]{2,1,0:T(8,128)(2,1)S(1)}, u32[]{:S(2)}, u32[]{:S(2)}) collective-permute-start(bf16[1,104,768]{2,1,0:T(8,128)(2,1)S(1)} %maximum_bitcast_fusion.1.refs_13_), channel_id=1, source_target_pairs={{0,24},{1,25},{2,26},{3,27},{4,28},{5,29},{6,30},{7,31},{8,16},{9,... | collective-permute-start | bytes 479240 | tf_op jit(solution)/shard_map/ppermute | solution.py:112
  175.5 15.4 %collective-permute-start.34 = (bf16[2,24,3840]{2,1,0:T(8,128)(2,1)S(1)}, bf16[2,24,3840]{2,1,0:T(8,128)(2,1)S(1)}, u32[]{:S(2)}, u32[]{:S(2)}) collective-permute-start(bf16[2,24,3840]{2,1,0:T(8,128)(2,1)S(1)} %add_convert_fusion.6.refs_12_), channel_id=1, source_target_pairs={{0,4},{1,9},{2,6},{3,11},{4,0},{5,13},{6,2},{7,15},{8,12},{9,1},{1... | collective-permute-start | bytes 1105928 | tf_op jit(solution)/shard_map/ppermute | solution.py:112
  176.4 16.0 %collective-permute-start.28 = (bf16[4,24,2304]{2,1,0:T(8,128)(2,1)S(1)}, bf16[4,24,2304]{2,1,0:T(8,128)(2,1)S(1)}, u32[]{:S(2)}, u32[]{:S(2)}) collective-permute-start(bf16[4,24,2304]{2,1,0:T(8,128)(2,1)S(1)} %add_convert_fusion.5.refs_11_), channel_id=1, source_target_pairs={{0,8},{1,3},{2,10},{3,1},{4,12},{5,7},{6,14},{7,5},{8,0},{9,11},{1... | collective-permute-start | bytes 1327112 | tf_op jit(solution)/shard_map/ppermute | solution.py:112
  187.9 14.8 %collective-permute-start.43 = (f32[16,768]{1,0:T(8,128)S(1)}, f32[16,768]{1,0:T(8,128)S(1)}, u32[]{:S(2)}, u32[]{:S(2)}) collective-permute-start(f32[16,768]{1,0:T(8,128)S(1)} %add.346), channel_id=1, source_target_pairs={{0,2},{1,3},{2,0},{3,1},{4,6},{5,7},{6,4},{7,5},{8,10},{9,11},{10,... | collective-permute-start | bytes 147464 | tf_op jit(solution)/shard_map/ppermute | solution.py:112
  189.5 13.0 %collective-permute-start.40 = (bf16[2,104,768]{2,1,0:T(8,128)(2,1)S(1)}, bf16[2,104,768]{2,1,0:T(8,128)(2,1)S(1)}, u32[]{:S(2)}, u32[]{:S(2)}) collective-permute-start(bf16[2,104,768]{2,1,0:T(8,128)(2,1)S(1)} %constant_dynamic-update-slice_fusion.8), channel_id=1, source_target_pairs={{0,8},{1,5},{2,10},{3,7},{4,12},{5,1},{6,14},{7,3},{8,0},{9,13},{1... | collective-permute-start | bytes 958472 | tf_op jit(solution)/shard_map/ppermute | solution.py:112
  191.0 13.7 %collective-permute-start.35 = (bf16[1,24,3840]{2,1,0:T(8,128)(2,1)S(1)}, bf16[1,24,3840]{2,1,0:T(8,128)(2,1)S(1)}, u32[]{:S(2)}, u32[]{:S(2)}) collective-permute-start(bf16[1,24,3840]{2,1,0:T(8,128)(2,1)S(1)} %add_convert_fusion.9), channel_id=1, source_target_pairs={{0,24},{1,25},{2,26},{3,27},{4,28},{5,29},{6,30},{7,31},{8,16},{9,... | collective-permute-start | bytes 552968 | tf_op jit(solution)/shard_map/ppermute | solution.py:112
  192.6 18.4 %collective-permute-start.29 = (bf16[2,24,2304]{2,1,0:T(8,128)(2,1)S(1)}, bf16[2,24,2304]{2,1,0:T(8,128)(2,1)S(1)}, u32[]{:S(2)}, u32[]{:S(2)}) collective-permute-start(bf16[2,24,2304]{2,1,0:T(8,128)(2,1)S(1)} %add_convert_fusion.8), channel_id=1, source_target_pairs={{0,4},{1,9},{2,6},{3,11},{4,0},{5,13},{6,2},{7,15},{8,12},{9,1},{1... | collective-permute-start | bytes 663560 | tf_op jit(solution)/shard_map/ppermute | solution.py:112
  202.5 38.2 %collective-permute-start.41 = (bf16[4,104,768]{2,1,0:T(8,128)(2,1)S(1)}, bf16[4,104,768]{2,1,0:T(8,128)(2,1)S(1)}, u32[]{:S(2)}, u32[]{:S(2)}) collective-permute-start(bf16[4,104,768]{2,1,0:T(8,128)(2,1)S(1)} %constant_dynamic-update-slice_fusion.10.refs_1_), channel_id=1, source_target_pairs={{0,4},{1,9},{2,6},{3,11},{4,0},{5,13},{6,2},{7,15},{8,12},{9,1},{1... | collective-permute-start | bytes 1916936 | tf_op jit(solution)/shard_map/ppermute | solution.py:112
  202.7 10.9 %collective-permute-start.44 = (f32[16,768]{1,0:T(8,128)S(1)}, f32[16,768]{1,0:T(8,128)S(1)}, u32[]{:S(2)}, u32[]{:S(2)}) collective-permute-start(f32[16,768]{1,0:T(8,128)S(1)} %add.347), channel_id=1, source_target_pairs={{0,4},{1,5},{2,6},{3,7},{4,0},{5,1},{6,2},{7,3},{8,12},{9,13},{10,... | collective-permute-start | bytes 147464 | tf_op jit(solution)/shard_map/ppermute | solution.py:112
  213.5 12.3 %collective-permute-start.45 = (f32[16,768]{1,0:T(8,128)S(1)}, f32[16,768]{1,0:T(8,128)S(1)}, u32[]{:S(2)}, u32[]{:S(2)}) collective-permute-start(f32[16,768]{1,0:T(8,128)S(1)} %add.348), channel_id=1, source_target_pairs={{0,8},{1,9},{2,10},{3,11},{4,12},{5,13},{6,14},{7,15},{8,0},{9,1},... | collective-permute-start | bytes 147464 | tf_op jit(solution)/shard_map/ppermute | solution.py:112
  221.6 18.3 %collective-permute-start.37 = (bf16[2,24,3840]{2,1,0:T(8,128)(2,1)S(1)}, bf16[2,24,3840]{2,1,0:T(8,128)(2,1)S(1)}, u32[]{:S(2)}, u32[]{:S(2)}) collective-permute-start(bf16[2,24,3840]{2,1,0:T(8,128)(2,1)S(1)} %constant_dynamic-update-slice_fusion.4), channel_id=1, source_target_pairs={{0,8},{1,5},{2,10},{3,7},{4,12},{5,1},{6,14},{7,3},{8,0},{9,13},{1... | collective-permute-start | bytes 1105928 | tf_op jit(solution)/shard_map/ppermute | solution.py:112
  225.9 13.4 %collective-permute-start.46 = (f32[16,768]{1,0:T(8,128)S(1)}, f32[16,768]{1,0:T(8,128)S(1)}, u32[]{:S(2)}, u32[]{:S(2)}) collective-permute-start(f32[16,768]{1,0:T(8,128)S(1)} %add.349), channel_id=1, source_target_pairs={{0,24},{1,25},{2,26},{3,27},{4,28},{5,29},{6,30},{7,31},{8,16},{9,... | collective-permute-start | bytes 147464 | tf_op jit(solution)/shard_map/ppermute | solution.py:112
  228.9 13.8 %collective-permute-start.32 = (bf16[2,24,2304]{2,1,0:T(8,128)(2,1)S(1)}, bf16[2,24,2304]{2,1,0:T(8,128)(2,1)}, u32[]{:S(2)}, u32[]{:S(2)}) collective-permute-start(bf16[2,24,2304]{2,1,0:T(8,128)(2,1)S(1)} %constant_dynamic-update-slice_fusion), channel_id=1, source_target_pairs={{0,8},{1,5},{2,10},{3,7},{4,12},{5,1},{6,14},{7,3},{8,0},{9,13},{1... | collective-permute-start | bytes 663560 | tf_op jit(solution)/shard_map/ppermute | solution.py:112
  240.0 11.5 %collective-permute-start.38 = (bf16[4,24,3840]{2,1,0:T(8,128)(2,1)S(1)}, bf16[4,24,3840]{2,1,0:T(8,128)(2,1)S(1)}, u32[]{:S(2)}, u32[]{:S(2)}) collective-permute-start(bf16[4,24,3840]{2,1,0:T(8,128)(2,1)S(1)} %constant_dynamic-update-slice_fusion.6.refs_1_), channel_id=1, source_target_pairs={{0,4},{1,9},{2,6},{3,11},{4,0},{5,13},{6,2},{7,15},{8,12},{9,1},{1... | collective-permute-start | bytes 2211848 | tf_op jit(solution)/shard_map/ppermute | solution.py:112
  243.7 13.1 %collective-permute-start.33 = (bf16[4,24,2304]{2,1,0:T(8,128)(2,1)S(1)}, bf16[4,24,2304]{2,1,0:T(8,128)(2,1)S(1)}, u32[]{:S(2)}, u32[]{:S(2)}) collective-permute-start(bf16[4,24,2304]{2,1,0:T(8,128)(2,1)S(1)} %constant_dynamic-update-slice_fusion.2.refs_3_.refs_1_), channel_id=1, source_target_pairs={{0,4},{1,9},{2,6},{3,11},{4,0},{5,13},{6,2},{7,15},{8,12},{9,1},{1... | collective-permute-start | bytes 1327112 | tf_op jit(solution)/shard_map/ppermute | solution.py:112
  (82 other events, 721.3 us)
where the time goes:
time: 261 us; the launch traced here: 260 us
  Pallas kernels  126 us (48%)
  starting transfers between devices  49.1 us (19%)
  waiting for transfers between devices  48.4 us (19%)
  local copies, waits for them, and re-layouts  18.3 us (7%)
  other arithmetic  17.2 us (7%)
    pallas_call x19, Pallas kernels, __call__(): pl.pallas_call(body, grid_spec=pltpu.PrefetchScalarGridSpec(num_scalar_pr...  126 us
    ppermute x47, starting transfers between devices, exchange(): return lax.ppermute(value, ('batch', 'fsdp'), pairs)  49.1 us
    ppermute x47, waiting for transfers between devices, exchange(): return lax.ppermute(value, ('batch', 'fsdp'), pairs)  48.4 us
    unnamed x140, local copies, waits for them, and re-layouts  14.3 us
    convert_element_type x12, other arithmetic, add(): self.sent = self.call.hold(total.astype(BF16))  6.62 us
    convert_element_type x3, other arithmetic, finish(): news.append(new_w.astype(BF16))  5.77 us
  transfers between devices with their start and end apart: 47, of which 16 were waited for; matrix products, arithmetic and copies ran while one was open for 7% of the time, Pallas kernels for 47%

commit v1 on v0

--- a/solution.py
+++ b/solution.py
@@ -102,7 +102,7 @@
         near = [1, 2, 6] if self.bbits == 3 else [1 << k for k in range(self.bbits)]
         self.batch = [mask * self.nf for mask in near]
         first, second, *rest = self.batch
-        self.scatter = ([1, 2, second, first] + rest, [1, first, 2, second] + rest)
+        self.scatter = ([1, first, second] + rest + [2], [1, second, first, 2] + rest)
         self.gather = (rest[::-1] + [second, first], rest[::-1] + [first, second])
         self.helper = (first, second)
 
@@ -238,21 +238,30 @@
     qkv_ref[0, :, 2 * D :] = (dot(n1, w_ref[:, 2 * D :]) + vec_ref[5:6, :]).astype(BF16)
 
 
+def lane_slab(slab):
+    return pl.ds(pl.multiple_of(slab * LANES, LANES), LANES)
+
+
 def mix_kernel(qkv_ref, a_ref):
     low = lax.broadcasted_iota(jnp.int32, (1, LANES), 1) < HDIM
-    for slab in range(SLABS):
-        cols = slice(slab * LANES, (slab + 1) * LANES)
-        q = qkv_ref[0, :, cols] * jnp.asarray(HDIM**-0.5, BF16)
-        k = qkv_ref[0, :, D + slab * LANES : D + (slab + 1) * LANES]
-        v = qkv_ref[0, :, 2 * D + slab * LANES : 2 * D + (slab + 1) * LANES]
-        outs = []
-        for head in range(2):
-            mine = low if head == 0 else jnp.logical_not(low)
-            scores = dot_last(jnp.where(mine, q, jnp.zeros_like(q)), k)
-            e = jnp.exp(scores - jnp.max(scores, axis=-1, keepdims=True))
-            p = (e * (1.0 / jnp.sum(e, axis=-1, keepdims=True))).astype(BF16)
-            outs.append(dot(p, v))
-        a_ref[0, :, cols] = jnp.where(low, outs[0], outs[1]).astype(BF16)
+
+    def some_slabs(turn, _):
+        for slab in [3 * turn + k for k in range(3)]:
+            cols = lane_slab(slab)
+            q = qkv_ref[0, :, cols] * jnp.asarray(HDIM**-0.5, BF16)
+            k = qkv_ref[0, :, lane_slab(slab + SLABS)]
+            v = qkv_ref[0, :, lane_slab(slab + 2 * SLABS)]
+            outs = []
+            for head in range(2):
+                mine = low if head == 0 else jnp.logical_not(low)
+                scores = dot_last(jnp.where(mine, q, jnp.zeros_like(q)), k)
+                e = jnp.exp(scores - jnp.max(scores, axis=-1, keepdims=True))
+                p = (e * (1.0 / jnp.sum(e, axis=-1, keepdims=True))).astype(BF16)
+                outs.append(dot(p, v))
+            a_ref[0, :, cols] = jnp.where(low, outs[0], outs[1]).astype(BF16)
+        return 0
+
+    lax.fori_loop(0, SLABS // 3, some_slabs, 0)
 
 
 def fc1_kernel(rows, place_ref, tok_ref, img_ref, a_ref, vec_ref, *refs):
@@ -701,8 +710,8 @@
     rows_d, rows_f = D // nf, FF // nf
 
     low_vec = vectors.astype(BF16)
-    vec_parts = [low_vec, plan.exchange(low_vec, 1)]
-    vec_parts += [plan.exchange(part, 2) for part in vec_parts]
+    vec_far = plan.exchange(low_vec, 2)
+    vec_parts = [low_vec, plan.exchange(low_vec, 1), vec_far, plan.exchange(vec_far, 1)]
     columns = []
     for spot in range(nf):
         chosen = vec_parts[0]
@@ -728,7 +737,7 @@
                 (pl.BlockSpec((half, cols), lambda i, *_: (0, 0)), (half, cols), BF16),
             ],
             [],
-            spent(rows * cols / 2e5),
+            spent(0.1),
             "cast",
             after,
         )
@@ -779,7 +788,7 @@
             (pair_spec(length, 3 * D), (pairs, length, 3 * D), BF16),
         ],
         [pltpu.VMEM((D, 3 * D), BF16), sems],
-        spent(1),
+        spent(0.1),
         "qkv",
     )
 
@@ -1011,6 +1020,10 @@
 
     sum_3.add()
 
+    paced, call.last = call.last, sum_3.sent
+    moved_2, (new_m2, new_v2) = finish(sum_2, (3,), (w_fc2,), ((m_fc2, v_fc2),), riders)
+    call.last = paced
+
     grad_tokens, vec_sum = call(
         functools.partial(grad_in_kernel, rows_d),
         (pairs,),
@@ -1038,15 +1051,25 @@
         "grad_in",
     )
 
-    vec_gens = [1, 2] + plan.batch
+    vec_gens = [1] + plan.batch[1:] + plan.batch[:1] + [2]
     vec_got = plan.exchange(vec_sum, vec_gens[0])
+
+    vec_place = 1
+
+    def vec_step():
+        nonlocal vec_sum, vec_got, vec_place
+        if vec_place > len(vec_gens):
+            return
+        one, two = call.pin([vec_sum, vec_got])
+        vec_sum = one + two
+        if vec_place < len(vec_gens):
+            vec_got = plan.exchange(vec_sum, vec_gens[vec_place])
+        vec_place += 1
 
     last = plan.bbits
     sum_3.add()
     sum_1.add()
-    while sum_2.count > 1:
-        sum_2.add()
-    moved_2, (new_m2, new_v2) = finish(sum_2, (3,), (w_fc2,), ((m_fc2, v_fc2),), riders)
+    moved_2.join()
 
     (layer_out,) = call(
         functools.partial(out_kernel, rows_f),
@@ -1064,18 +1087,6 @@
         spent(13),
         "out",
     )
-
-    vec_place = 1
-
-    def vec_step():
-        nonlocal vec_sum, vec_got, vec_place
-        if vec_place > len(vec_gens):
-            return
-        one, two = call.pin([vec_sum, vec_got])
-        vec_sum = one + two
-        if vec_place < len(vec_gens):
-            vec_got = plan.exchange(vec_sum, vec_gens[vec_place])
-        vec_place += 1
 
     moved_1 = moved_3 = None
     while moved_3 is None or moved_3.place < last:
@@ -1108,12 +1119,13 @@
     while moved_2.place < last:
         moved_2.join()
     call.waiting = []
+    tail = call.pin([moved_2.blocks, moved_2.got])
     (new_2,) = put(moved_2, (D,), FF // nd)
     new_1, new_o = put(moved_1, (FF, D), D // nd)
     (new_q,) = put(moved_3, (3 * D,), D // nd)
 
     own_cols = D // nd
-    got = jnp.concatenate([moved_2.blocks[:, FF // nd :], moved_2.got[:, FF // nd :]], axis=0)
+    got = jnp.concatenate([part[:, FF // nd :] for part in tail], axis=0)
     half = rider_cols // 2
     held = got[:, :, :half].astype(F32) + got[:, :, half:rider_cols].astype(F32)
     held = held.reshape(nb, -1)[:, : 2 * NVEC * own_cols].reshape(nb, 2 * NVEC, own_cols)

time: 261 us -> 249 us (0.954)
  waiting for transfers between devices: 48.4 us -> 38.8 us
  starting transfers between devices: 49.1 us -> 44 us
  Pallas kernels: 126 us -> 129 us
    ppermute x47, waiting for transfers between devices: 48.4 us -> 38.8 us  [exchange(): return lax.ppermute(value, ('batch', 'fsdp'), pairs)]
    ppermute x47, starting transfers between devices: 49.1 us -> 44 us  [exchange(): return lax.ppermute(value, ('batch', 'fsdp'), pairs)]
    pallas_call x19, Pallas kernels: 126 us -> 129 us  [__call__(): pl.pallas_call(body, grid_spec=pltpu.PrefetchScalarGridSpec(num_scalar_pr...]
    unnamed x140 -> x146, local copies, waits for them, and re-layouts: 14.3 us -> 13 us
  transfers between devices with their start and end apart: 47 -> 47, of which waited for: 16 -> 17; matrix products, arithmetic and copies ran while one was open for 7% -> 8% of each run, Pallas kernels for 47% -> 51%
where the time goes in v1:
time: 249 us; the launch traced here: 247 us
  Pallas kernels  129 us (52%)
  starting transfers between devices  44 us (18%)
  waiting for transfers between devices  38.8 us (16%)
  other arithmetic  17.9 us (7%)
  local copies, waits for them, and re-layouts  16.1 us (6%)
    pallas_call x19, Pallas kernels, __call__(): pl.pallas_call(body, grid_spec=pltpu.PrefetchScalarGridSpec(num_scalar_pr...  129 us
    ppermute x47, starting transfers between devices, exchange(): return lax.ppermute(value, ('batch', 'fsdp'), pairs)  44 us
    ppermute x47, waiting for transfers between devices, exchange(): return lax.ppermute(value, ('batch', 'fsdp'), pairs)  38.8 us
    unnamed x146, local copies, waits for them, and re-layouts  13 us
    convert_element_type x12, other arithmetic, add(): self.sent = self.call.hold(total.astype(BF16))  6.63 us
    convert_element_type x3, other arithmetic, finish(): news.append(new_w.astype(BF16))  5.77 us
  transfers between devices with their start and end apart: 47, of which 17 were waited for; matrix products, arithmetic and copies ran while one was open for 8% of the time, Pallas kernels for 51%

profile of v1, /device:TPU:0, one launch (start us, length us, event | category | flops | bytes accessed | tf_op | source)
XLA Modules:
  0.0 247.3 jit_solution(650658028903362154)
XLA Ops:
  1.4 3.0 %collective-permute-start = (bf16[14,192]{1,0:T(8,128)(2,1)S(1)}, bf16[14,192]{1,0:T(8,128)(2,1)S(1)}, u32[]{:S(2)}, u32[]{:S(2)}) collective-permute-start(bf16[14,192]{1,0:T(8,128)(2,1)S(1)} %convert_element_type.251), channel_id=1, source_target_pairs={{0,2},{1,3},{2,0},{3,1},{4,6},{5,7},{6,4},{7,5},{8,10},{9,11},{10,... | collective-permute-start | bytes 16136 | tf_op jit(solution)/shard_map/ppermute | solution.py:112
  9.9 3.3 %order.1 = (bf16[4,256,256]{2,1,0:T(8,128)(2,1)S(1)}, bf16[4,256,768]{2,1,0:T(8,128)(2,1)S(1)}, bf16[4,256,128]{2,1,0:T(8,128)(2,1)S(1)}, bf16[4,128,768]{2,1,0:T(8,128)(2,1)S(1)}) custom-call(s32[4]{0:T(128)S(1)} %copy-done.32, s32[4,1,128]{2,1,0:T(1,128)S(1)} %bitcast.31, bf16[4,256,768]{2,1,0:T(8,128)(2,1)S(1)} %copy-done.16, ...), custom_call_target="tpu_custom_call" | custom-call | flops 17999998976 | bytes 60000000 | tf_op jit(solution)/shard_map/order/pallas_call | solution.py:588
  17.3 3.4 %collective-permute-done.4.refs_6_.refs_14_ = bf16[96,2304]{1,0:T(8,128)(2,1)} collective-permute-done((bf16[96,2304]{1,0:T(8,128)(2,1)S(1)}, bf16[96,2304]{1,0:T(8,128)(2,1)}, u32[]{:S(2)}, u32[]{:S(2)}) %collective-permute-start.4) | collective-permute-done | bytes 442400 | tf_op jit(solution)/shard_map/ppermute | solution.py:112
  22.7 6.6 %collective-permute-done.5.refs_7_.refs_15_ = bf16[96,2304]{1,0:T(8,128)(2,1)} collective-permute-done((bf16[96,2304]{1,0:T(8,128)(2,1)}, bf16[96,2304]{1,0:T(8,128)(2,1)}, u32[]{:S(2)}, u32[]{:S(2)}) %collective-permute-start.5) | collective-permute-done | bytes 442400 | tf_op jit(solution)/shard_map/ppermute | solution.py:112
  32.3 8.0 %qkv.1 = (bf16[4,256,768]{2,1,0:T(8,128)(2,1)S(1)}, bf16[4,256,2304]{2,1,0:T(8,128)(2,1)S(1)}) custom-call(s32[52]{0:T(128)S(1)} %get-tuple-element.296.refs_0_, bf16[4,256,768]{2,1,0:T(8,128)(2,1)S(1)} %get-tuple-element.146.refs_1_, bf16[4,256,128]{2,1,0:T(8,128)(2,1)S(1)} %copy-done.13, f32[16,768]{1,0:T(8,128)S(1)} %fusion.12.refs_3_.refs_4_, ...), custom_call_target="tpu_custom_call" | custom-call | flops 300000000 | bytes 1000000 | tf_op jit(solution)/shard_map/qkv/pallas_call | solution.py:588
  45.3 10.9 %mix.1.refs_3_.refs_11_ = bf16[4,256,768]{2,1,0:T(8,128)(2,1)S(1)} custom-call(bf16[4,256,2304]{2,1,0:T(8,128)(2,1)S(1)} %get-tuple-element.153.refs_2_.refs_0_, bf16[96,3840]{1,0:T(8,128)(2,1)} %collective-permute-done.8.refs_1_.refs_7_, bf16[384,768]{1,0:T(8,128)(2,1)S(1)} %get-tuple-element.154.refs_2_), custom_call_target="tpu_custom_call" | custom-call | flops 3000000000 | bytes 10000000 | tf_op jit(solution)/shard_map/mix/pallas_call | solution.py:588
  58.5 13.6 %fc1.1 = (f32[4,256,768]{2,1,0:T(8,128)S(1)}, bf16[4,256,768]{2,1,0:T(8,128)(2,1)S(1)}, bf16[4,256,3072]{2,1,0:T(8,128)(2,1)S(1)}, bf16[4,128,3072]{2,1,0:T(8,128)(2,1)S(1)}) custom-call(s32[52]{0:T(128)S(1)} %get-tuple-element.296.refs_0_, bf16[4,256,768]{2,1,0:T(8,128)(2,1)S(1)} %get-tuple-element.146.refs_1_, bf16[4,256,128]{2,1,0:T(8,128)(2,1)S(1)} %copy-done.14, ...), custom_call_target="tpu_custom_call" | custom-call | flops 54000001024 | bytes 180000000 | tf_op jit(solution)/shard_map/fc1/pallas_call | solution.py:588
  73.7 6.6 %gw2.1 = (bf16[16,96,768]{2,1,0:T(8,128)(2,1)S(1)}, bf16[16,96,768]{2,1,0:T(8,128)(2,1)}, f32[1,768]{1,0:T(1,128)S(1)}) custom-call(s32[52]{0:T(128)S(1)} %get-tuple-element.296.refs_0_, bf16[4,256,3072]{2,1,0:T(8,128)(2,1)S(1)} %get-tuple-element.158.refs_1_, bf16[4,128,768]{2,1,0:T(8,128)(2,1)S(1)} %copy-done.9, ...), custom_call_target="tpu_custom_call" | custom-call | flops 24000000000 | bytes 80000000 | tf_op jit(solution)/shard_map/gw2/pallas_call | solution.py:588
  80.4 2.1 collective-permute-done.15.refs_6_.refs_8_
  87.9 7.1 %df.1 = (bf16[512,3072]{1,0:T(8,128)(2,1)S(1)}, f32[1,3072]{1,0:T(1,128)S(1)}) custom-call(s32[52]{0:T(128)S(1)} %get-tuple-element.296.refs_0_, bf16[4,128,768]{2,1,0:T(8,128)(2,1)S(1)} %copy-done.10, bf16[4,128,3072]{2,1,0:T(8,128)(2,1)S(1)} %copy-done.39, bf16[768,768]{1,0:T(8,128)(2,1)} %get-tuple-element.155.refs_3_.refs_5_, ...), custom_call_target="tpu_custom_call" | custom-call | flops 20999999488 | bytes 70000000 | tf_op jit(solution)/shard_map/df/pallas_call | solution.py:588
  98.2 7.6 %mlp_back.1 = (f32[4,128,768]{2,1,0:T(8,128)S(1)}, bf16[4,128,768]{2,1,0:T(8,128)(2,1)S(1)}, bf16[4,128,768]{2,1,0:T(8,128)(2,1)S(1)}, f32[8,768]{1,0:T(8,128)S(1)}) custom-call(s32[52]{0:T(128)S(1)} %get-tuple-element.296.refs_0_, bf16[512,3072]{1,0:T(8,128)(2,1)S(1)} %get-tuple-element.167.refs_1_.refs_2_, bf16[4,128,768]{2,1,0:T(8,128)(2,1)S(1)} %copy-done.10, ...), custom_call_target="tpu_custom_call" | custom-call | flops 30000001024 | bytes 100000000 | tf_op jit(solution)/shard_map/mlp_back/pallas_call | solution.py:588
  105.8 6.9 %gw1o.1 = (bf16[16,24,3840]{2,1,0:T(8,128)(2,1)S(1)}, bf16[16,24,3840]{2,1,0:T(8,128)(2,1)S(1)}) custom-call(s32[52]{0:T(128)S(1)} %get-tuple-element.296.refs_0_, bf16[4,256,768]{2,1,0:T(8,128)(2,1)S(1)} %copy-done.44, bf16[512,3072]{1,0:T(8,128)(2,1)S(1)} %get-tuple-element.167.refs_1_.refs_2_, bf16[4,256,768]{2,1,0:T(8,128)(2,1)S(1)} %copy-done.36, ...), custom_call_target="tpu_custom_call" | custom-call | flops 27000000512 | bytes 90000000 | tf_op jit(solution)/shard_map/gw1o/pallas_call | solution.py:588
  115.9 11.3 %attn_back.2 = (bf16[4,128,768]{2,1,0:T(8,128)(2,1)S(1)}, bf16[4,256,1536]{2,1,0:T(8,128)(2,1)S(1)}, f32[8,768]{1,0:T(8,128)S(1)}) custom-call(bf16[4,256,2304]{2,1,0:T(8,128)(2,1)S(1)} %bitcast.30, bf16[4,128,768]{2,1,0:T(8,128)(2,1)S(1)} %get-tuple-element.173.refs_1_, bf16[4,96,768]{2,1,0:T(8,128)(2,1)S(1)} %add_convert_fusion.4.refs_2_, ...), custom_call_target="tpu_custom_call" | custom-call | flops 35999997952 | bytes 120000000 | tf_op jit(solution)/shard_map/attn_back/pallas_call | solution.py:588
  128.4 2.5 %collective-permute-start.22 = (bf16[2,96,768]{2,1,0:T(8,128)(2,1)S(1)}, bf16[2,96,768]{2,1,0:T(8,128)(2,1)S(1)}, u32[]{:S(2)}, u32[]{:S(2)}) collective-permute-start(bf16[2,96,768]{2,1,0:T(8,128)(2,1)S(1)} %add_convert_fusion.7.refs_6_), channel_id=1, source_target_pairs={{0,24},{1,3},{2,26},{3,1},{4,28},{5,7},{6,30},{7,5},{8,16},{9,11},... | collective-permute-start | bytes 884744 | tf_op jit(solution)/shard_map/ppermute | solution.py:112
  132.7 11.3 %attn_back.3 = (bf16[4,128,768]{2,1,0:T(8,128)(2,1)S(1)}, bf16[4,256,1536]{2,1,0:T(8,128)(2,1)S(1)}, f32[8,768]{1,0:T(8,128)S(1)}) custom-call(bf16[4,256,2304]{2,1,0:T(8,128)(2,1)S(1)} %bitcast.30, bf16[4,128,768]{2,1,0:T(8,128)(2,1)S(1)} %get-tuple-element.173.refs_1_, ...), custom_call_target="tpu_custom_call", output_to_operand_aliasing={{0}: (2, {}), {1}: (3, {})} | custom-call | flops 35999997952 | bytes 120000000 | tf_op jit(solution)/shard_map/attn_back/pallas_call | solution.py:588
  145.0 6.1 %gqkv.1 = (bf16[16,24,2304]{2,1,0:T(8,128)(2,1)S(1)}, bf16[16,24,2304]{2,1,0:T(8,128)(2,1)S(1)}) custom-call(s32[52]{0:T(128)S(1)} %get-tuple-element.296.refs_0_, bf16[4,256,768]{2,1,0:T(8,128)(2,1)S(1)} %copy-done.19, bf16[4,128,768]{2,1,0:T(8,128)(2,1)S(1)} %get-tuple-element.190.refs_2_.refs_4_, ...), custom_call_target="tpu_custom_call" | custom-call | flops 27000000512 | bytes 90000000 | tf_op jit(solution)/shard_map/gqkv/pallas_call | solution.py:588
  152.6 2.3 collective-permute-done.23
  156.6 2.1 subtract_convert_fusion.1
  159.6 12.0 %grad_in.1 = (f32[4,256,768]{2,1,0:T(8,128)}, f32[16,768]{1,0:T(8,128)S(1)}) custom-call(s32[52]{0:T(128)S(1)} %get-tuple-element.296.refs_0_, bf16[4,256,768]{2,1,0:T(8,128)(2,1)S(1)} %copy-done.5, bf16[4,256,128]{2,1,0:T(8,128)(2,1)S(1)} %copy-done.15, f32[16,768]{1,0:T(8,128)S(1)} %fusion.12.refs_3_.refs_4_, ...), custom_call_target="tpu_custom_call" | custom-call | flops 44999999488 | bytes 150000000 | tf_op jit(solution)/shard_map/grad_in/pallas_call | solution.py:588
  171.7 2.0 collective-permute-start.42
  174.8 2.8 %collective-permute-start.35 = (bf16[2,24,3840]{2,1,0:T(8,128)(2,1)S(1)}, bf16[2,24,3840]{2,1,0:T(8,128)(2,1)S(1)}, u32[]{:S(2)}, u32[]{:S(2)}) collective-permute-start(bf16[2,24,3840]{2,1,0:T(8,128)(2,1)S(1)} %add_convert_fusion.6.refs_12_), channel_id=1, source_target_pairs={{0,24},{1,3},{2,26},{3,1},{4,28},{5,7},{6,30},{7,5},{8,16},{9,11},... | collective-permute-start | bytes 1105928 | tf_op jit(solution)/shard_map/ppermute | solution.py:112
  178.9 10.6 %out.1 = bf16[4,256,768]{2,1,0:T(8,128)(2,1)} custom-call(s32[52]{0:T(128)S(1)} %get-tuple-element.296.refs_0_, bf16[4,256,3072]{2,1,0:T(8,128)(2,1)S(1)} %bitcast.33, f32[4,256,768]{2,1,0:T(8,128)S(1)} %copy-done.42, f32[16,768]{1,0:T(8,128)S(1)} %fusion.12.refs_3_.refs_4_, bf16[4,256,256]{2,1,0:T(8,128)(2,1)S(1)} %copy-done.46, ...), custom_call_target="tpu_custom_call" | custom-call | flops 38999998464 | bytes 130000000 | tf_op jit(solution)/shard_map/out/pallas_call | solution.py:588
  192.6 2.0 collective-permute-start.30
  197.1 2.0 subtract_convert_fusion
  200.4 2.7 %collective-permute-start.44 = (f32[16,768]{1,0:T(8,128)S(1)}, f32[16,768]{1,0:T(8,128)S(1)}, u32[]{:S(2)}, u32[]{:S(2)}) collective-permute-start(f32[16,768]{1,0:T(8,128)S(1)} %add.347), channel_id=1, source_target_pairs={{0,24},{1,25},{2,26},{3,27},{4,28},{5,29},{6,30},{7,31},{8,16},{9,... | collective-permute-start | bytes 147464 | tf_op jit(solution)/shard_map/ppermute | solution.py:112
  204.3 4.3 %collective-permute-done.37 = bf16[1,24,3840]{2,1,0:T(8,128)(2,1)S(1)} collective-permute-done((bf16[1,24,3840]{2,1,0:T(8,128)(2,1)S(1)}, bf16[1,24,3840]{2,1,0:T(8,128)(2,1)S(1)}, u32[]{:S(2)}, u32[]{:S(2)}) %collective-permute-start.37) | collective-permute-done | bytes 184352 | tf_op jit(solution)/shard_map/ppermute | solution.py:112
  215.5 3.6 %collective-permute-done.32 = bf16[1,24,2304]{2,1,0:T(8,128)(2,1)S(1)} collective-permute-done((bf16[1,24,2304]{2,1,0:T(8,128)(2,1)S(1)}, bf16[1,24,2304]{2,1,0:T(8,128)(2,1)S(1)}, u32[]{:S(2)}, u32[]{:S(2)}) %collective-permute-start.32) | collective-permute-done | bytes 110624 | tf_op jit(solution)/shard_map/ppermute | solution.py:112
  223.8 2.6 %collective-permute-done.33 = bf16[2,24,2304]{2,1,0:T(8,128)(2,1)S(1)} collective-permute-done((bf16[2,24,2304]{2,1,0:T(8,128)(2,1)S(1)}, bf16[2,24,2304]{2,1,0:T(8,128)(2,1)S(1)}, u32[]{:S(2)}, u32[]{:S(2)}) %collective-permute-start.33) | collective-permute-done | bytes 221216 | tf_op jit(solution)/shard_map/ppermute | solution.py:112
  228.9 2.6 %place.3.refs_3_ = f32[768,768]{1,0:T(8,128)} custom-call(s32[52]{0:T(128)S(1)} %get-tuple-element.296.refs_0_, bf16[4,104,768]{2,1,0:T(8,128)(2,1)S(1)} %constant_dynamic-update-slice_fusion.10.refs_1_, bf16[4,104,768]{2,1,0:T(8,128)(2,1)S(1)} %collective-permute-done.41.refs_2_, bf16[4,24,2304]{2,1,0:T(8,128)(2,1)S(1)} %constant_dynamic-update-slice_fusion.4.refs_3_.refs_1_), custom_call_target="tpu_custom_call" | custom-call | flops 3000000000 | bytes 10000000 | tf_op jit(solution)/shard_map/place/pallas_call | solution.py:588
  232.9 4.6 %collective-permute-done.39.refs_2_ = bf16[4,24,3840]{2,1,0:T(8,128)(2,1)S(1)} collective-permute-done((bf16[4,24,3840]{2,1,0:T(8,128)(2,1)S(1)}, bf16[4,24,3840]{2,1,0:T(8,128)(2,1)S(1)}, u32[]{:S(2)}, u32[]{:S(2)}) %collective-permute-start.39) | collective-permute-done | bytes 737312 | tf_op jit(solution)/shard_map/ppermute | solution.py:112
  239.2 3.5 %place.4 = (f32[192,3072]{1,0:T(8,128)}, f32[192,768]{1,0:T(8,128)}) custom-call(s32[52]{0:T(128)S(1)} %get-tuple-element.296.refs_0_, bf16[4,24,3840]{2,1,0:T(8,128)(2,1)S(1)} %constant_dynamic-update-slice_fusion.8.refs_1_, bf16[4,24,3840]{2,1,0:T(8,128)(2,1)S(1)} %collective-permute-done.39.refs_2_, f32[768,768]{1,0:T(8,128)S(1)} %copy-done.33), custom_call_target="tpu_custom_call" | custom-call | flops 3000000000 | bytes 10000000 | tf_op jit(solution)/shard_map/place/pallas_call | solution.py:588
  243.8 3.5 %place.5 = f32[192,2304]{1,0:T(8,128)} custom-call(s32[52]{0:T(128)S(1)} %get-tuple-element.296.refs_0_, bf16[4,24,2304]{2,1,0:T(8,128)(2,1)S(1)} %constant_dynamic-update-slice_fusion.4.refs_3_.refs_1_, bf16[4,24,2304]{2,1,0:T(8,128)(2,1)} %collective-permute-done.34.refs_2_, f32[192,768]{1,0:T(8,128)S(1)} %copy-done.34), custom_call_target="tpu_custom_call" | custom-call | flops 3000000000 | bytes 10000000 | tf_op jit(solution)/shard_map/place/pallas_call | solution.py:588
  (283 shorter events, 72.2 us)
Async XLA Ops:
  1.4 12.5 %collective-permute-start = (bf16[14,192]{1,0:T(8,128)(2,1)S(1)}, bf16[14,192]{1,0:T(8,128)(2,1)S(1)}, u32[]{:S(2)}, u32[]{:S(2)}) collective-permute-start(bf16[14,192]{1,0:T(8,128)(2,1)S(1)} %convert_element_type.251), channel_id=1, source_target_pairs={{0,2},{1,3},{2,0},{3,1},{4,6},{5,7},{6,4},{7,5},{8,10},{9,11},{10,... | collective-permute-start | bytes 16136 | tf_op jit(solution)/shard_map/ppermute | solution.py:112
  4.4 12.9 %collective-permute-start.2 = (bf16[14,192]{1,0:T(8,128)(2,1)S(1)}, bf16[14,192]{1,0:T(8,128)(2,1)S(1)}, u32[]{:S(2)}, u32[]{:S(2)}) collective-permute-start(bf16[14,192]{1,0:T(8,128)(2,1)S(1)} %convert_element_type.251), channel_id=1, source_target_pairs={{0,1},{1,0},{2,3},{3,2},{4,5},{5,4},{6,7},{7,6},{8,9},{9,8},{10,11... | collective-permute-start | bytes 16136 | tf_op jit(solution)/shard_map/ppermute | solution.py:112
  7.8 21.6 %collective-permute-start.3 = (bf16[192,2304]{1,0:T(8,128)(2,1)S(1)}, bf16[192,2304]{1,0:T(8,128)(2,1)S(1)}, u32[]{:S(2)}, u32[]{:S(2)}) collective-permute-start(bf16[192,2304]{1,0:T(8,128)(2,1)S(1)} %get-tuple-element.148.refs_4_.refs_12_), channel_id=1, source_target_pairs={{0,1},{1,0},{2,3},{3,2},{4,5},{5,4},{6,7},{7,6},{8,9},{9,8},{10,11... | collective-permute-start | bytes 2654216 | tf_op jit(solution)/shard_map/ppermute | solution.py:112
  8.4 12.3 %collective-permute-start.4 = (bf16[96,2304]{1,0:T(8,128)(2,1)S(1)}, bf16[96,2304]{1,0:T(8,128)(2,1)}, u32[]{:S(2)}, u32[]{:S(2)}) collective-permute-start(bf16[96,2304]{1,0:T(8,128)(2,1)S(1)} %get-tuple-element.145.refs_4_), channel_id=1, source_target_pairs={{0,2},{1,3},{2,0},{3,1},{4,6},{5,7},{6,4},{7,5},{8,10},{9,11},{10,... | collective-permute-start | bytes 1327112 | tf_op jit(solution)/shard_map/ppermute | solution.py:112
  22.2 21.1 %collective-permute-start.8 = (bf16[96,3840]{1,0:T(8,128)(2,1)}, bf16[96,3840]{1,0:T(8,128)(2,1)}, u32[]{:S(2)}, u32[]{:S(2)}) collective-permute-start(bf16[96,3840]{1,0:T(8,128)(2,1)} %get-tuple-element.152.refs_10_), channel_id=1, source_target_pairs={{0,2},{1,3},{2,0},{3,1},{4,6},{5,7},{6,4},{7,5},{8,10},{9,11},{10,... | collective-permute-start | bytes 2211848 | tf_op jit(solution)/shard_map/ppermute | solution.py:112
  43.2 13.0 %collective-permute-start.10 = (bf16[96,3840]{1,0:T(8,128)(2,1)}, bf16[96,3840]{1,0:T(8,128)(2,1)S(1)}, u32[]{:S(2)}, u32[]{:S(2)}) collective-permute-start(bf16[96,3840]{1,0:T(8,128)(2,1)} %collective-permute-done.8.refs_1_.refs_7_), channel_id=1, source_target_pairs={{0,4},{1,9},{2,6},{3,11},{4,0},{5,13},{6,2},{7,15},{8,12},{9,1},{1... | collective-permute-start | bytes 2211848 | tf_op jit(solution)/shard_map/ppermute | solution.py:112
  44.8 12.6 %collective-permute-start.9 = (bf16[192,3840]{1,0:T(8,128)(2,1)S(1)}, bf16[192,3840]{1,0:T(8,128)(2,1)S(1)}, u32[]{:S(2)}, u32[]{:S(2)}) collective-permute-start(bf16[192,3840]{1,0:T(8,128)(2,1)S(1)} %copy-done.21), channel_id=1, source_target_pairs={{0,1},{1,0},{2,3},{3,2},{4,5},{5,4},{6,7},{7,6},{8,9},{9,8},{10,11... | collective-permute-start | bytes 4423688 | tf_op jit(solution)/shard_map/ppermute | solution.py:112
  44.8 12.6 %collective-permute-start.11 = (bf16[96,3840]{1,0:T(8,128)(2,1)}, bf16[96,3840]{1,0:T(8,128)(2,1)S(1)}, u32[]{:S(2)}, u32[]{:S(2)}) collective-permute-start(bf16[96,3840]{1,0:T(8,128)(2,1)} %collective-permute-done.8.refs_1_.refs_7_), channel_id=1, source_target_pairs={{0,1},{1,0},{2,3},{3,2},{4,5},{5,4},{6,7},{7,6},{8,9},{9,8},{10,11... | collective-permute-start | bytes 2211848 | tf_op jit(solution)/shard_map/ppermute | solution.py:112
  56.3 27.3 %collective-permute-start.13 = (bf16[768,768]{1,0:T(8,128)(2,1)}, bf16[768,768]{1,0:T(8,128)(2,1)}, u32[]{:S(2)}, u32[]{:S(2)}) collective-permute-start(bf16[768,768]{1,0:T(8,128)(2,1)} %get-tuple-element.155.refs_3_.refs_5_), channel_id=1, source_target_pairs={{0,1},{1,0},{2,3},{3,2},{4,5},{5,4},{6,7},{7,6},{8,9},{9,8},{10,11... | collective-permute-start | bytes 3538952 | tf_op jit(solution)/shard_map/ppermute | solution.py:112
  56.8 15.4 %collective-permute-start.14 = (bf16[384,768]{1,0:T(8,128)(2,1)S(1)}, bf16[384,768]{1,0:T(8,128)(2,1)}, u32[]{:S(2)}, u32[]{:S(2)}) collective-permute-start(bf16[384,768]{1,0:T(8,128)(2,1)S(1)} %get-tuple-element.154.refs_2_), channel_id=1, source_target_pairs={{0,2},{1,3},{2,0},{3,1},{4,6},{5,7},{6,4},{7,5},{8,10},{9,11},{10,... | collective-permute-start | bytes 1769480 | tf_op jit(solution)/shard_map/ppermute | solution.py:112
  72.2 10.2 %collective-permute-start.15 = (bf16[384,768]{1,0:T(8,128)(2,1)}, bf16[384,768]{1,0:T(8,128)(2,1)}, u32[]{:S(2)}, u32[]{:S(2)}) collective-permute-start(bf16[384,768]{1,0:T(8,128)(2,1)} %collective-permute-done.14.refs_5_.refs_7_), channel_id=1, source_target_pairs={{0,4},{1,9},{2,6},{3,11},{4,0},{5,13},{6,2},{7,15},{8,12},{9,1},{1... | collective-permute-start | bytes 1769480 | tf_op jit(solution)/shard_map/ppermute | solution.py:112
  73.6 10.1 %collective-permute-start.16 = (bf16[384,768]{1,0:T(8,128)(2,1)}, bf16[384,768]{1,0:T(8,128)(2,1)}, u32[]{:S(2)}, u32[]{:S(2)}) collective-permute-start(bf16[384,768]{1,0:T(8,128)(2,1)} %collective-permute-done.14.refs_5_.refs_7_), channel_id=1, source_target_pairs={{0,1},{1,0},{2,3},{3,2},{4,5},{5,4},{6,7},{7,6},{8,9},{9,8},{10,11... | collective-permute-start | bytes 1769480 | tf_op jit(solution)/shard_map/ppermute | solution.py:112
  82.5 12.5 %collective-permute-start.18 = (bf16[16,96,768]{2,1,0:T(8,128)(2,1)}, bf16[16,96,768]{2,1,0:T(8,128)(2,1)}, u32[]{:S(2)}, u32[]{:S(2)}) collective-permute-start(bf16[16,96,768]{2,1,0:T(8,128)(2,1)} %get-tuple-element.169), channel_id=1, source_target_pairs={{0,1},{1,0},{2,3},{3,2},{4,5},{5,4},{6,7},{7,6},{8,9},{9,8},{10,11... | collective-permute-start | bytes 7077896 | tf_op jit(solution)/shard_map/ppermute | solution.py:112
  96.7 16.3 %collective-permute-start.19 = (bf16[8,96,768]{2,1,0:T(8,128)(2,1)S(1)}, bf16[8,96,768]{2,1,0:T(8,128)(2,1)S(1)}, u32[]{:S(2)}, u32[]{:S(2)}) collective-permute-start(bf16[8,96,768]{2,1,0:T(8,128)(2,1)S(1)} %add_convert_fusion.1.refs_11_), channel_id=1, source_target_pairs={{0,4},{1,9},{2,6},{3,11},{4,0},{5,13},{6,2},{7,15},{8,12},{9,1},{1... | collective-permute-start | bytes 3538952 | tf_op jit(solution)/shard_map/ppermute | solution.py:112
  112.7 18.2 %collective-permute-start.20 = (bf16[16,24,3840]{2,1,0:T(8,128)(2,1)S(1)}, bf16[16,24,3840]{2,1,0:T(8,128)(2,1)S(1)}, u32[]{:S(2)}, u32[]{:S(2)}) collective-permute-start(bf16[16,24,3840]{2,1,0:T(8,128)(2,1)S(1)} %get-tuple-element.176.refs_3_), channel_id=1, source_target_pairs={{0,1},{1,0},{2,3},{3,2},{4,5},{5,4},{6,7},{7,6},{8,9},{9,8},{10,11... | collective-permute-start | bytes 8847368 | tf_op jit(solution)/shard_map/ppermute | solution.py:112
  114.3 12.9 %collective-permute-start.21 = (bf16[4,96,768]{2,1,0:T(8,128)(2,1)S(1)}, bf16[4,96,768]{2,1,0:T(8,128)(2,1)S(1)}, u32[]{:S(2)}, u32[]{:S(2)}) collective-permute-start(bf16[4,96,768]{2,1,0:T(8,128)(2,1)S(1)} %add_convert_fusion.4.refs_2_), channel_id=1, source_target_pairs={{0,8},{1,5},{2,10},{3,7},{4,12},{5,1},{6,14},{7,3},{8,0},{9,13},{1... | collective-permute-start | bytes 1769480 | tf_op jit(solution)/shard_map/ppermute | solution.py:112
  128.4 15.6 %collective-permute-start.22 = (bf16[2,96,768]{2,1,0:T(8,128)(2,1)S(1)}, bf16[2,96,768]{2,1,0:T(8,128)(2,1)S(1)}, u32[]{:S(2)}, u32[]{:S(2)}) collective-permute-start(bf16[2,96,768]{2,1,0:T(8,128)(2,1)S(1)} %add_convert_fusion.7.refs_6_), channel_id=1, source_target_pairs={{0,24},{1,3},{2,26},{3,1},{4,28},{5,7},{6,30},{7,5},{8,16},{9,11},... | collective-permute-start | bytes 884744 | tf_op jit(solution)/shard_map/ppermute | solution.py:112
  131.3 20.7 %collective-permute-start.25 = (bf16[8,24,3840]{2,1,0:T(8,128)(2,1)S(1)}, bf16[8,24,3840]{2,1,0:T(8,128)(2,1)S(1)}, u32[]{:S(2)}, u32[]{:S(2)}) collective-permute-start(bf16[8,24,3840]{2,1,0:T(8,128)(2,1)S(1)} %add_convert_fusion.refs_5_), channel_id=1, source_target_pairs={{0,4},{1,9},{2,6},{3,11},{4,0},{5,13},{6,2},{7,15},{8,12},{9,1},{1... | collective-permute-start | bytes 4423688 | tf_op jit(solution)/shard_map/ppermute | solution.py:112
  152.3 22.3 %collective-permute-start.27 = (bf16[4,24,3840]{2,1,0:T(8,128)(2,1)S(1)}, bf16[4,24,3840]{2,1,0:T(8,128)(2,1)S(1)}, u32[]{:S(2)}, u32[]{:S(2)}) collective-permute-start(bf16[4,24,3840]{2,1,0:T(8,128)(2,1)S(1)} %add_convert_fusion.3.refs_18_), channel_id=1, source_target_pairs={{0,8},{1,5},{2,10},{3,7},{4,12},{5,1},{6,14},{7,3},{8,0},{9,13},{1... | collective-permute-start | bytes 2211848 | tf_op jit(solution)/shard_map/ppermute | solution.py:112
  155.1 22.5 %collective-permute-start.24 = (bf16[8,24,2304]{2,1,0:T(8,128)(2,1)S(1)}, bf16[8,24,2304]{2,1,0:T(8,128)(2,1)S(1)}, u32[]{:S(2)}, u32[]{:S(2)}) collective-permute-start(bf16[8,24,2304]{2,1,0:T(8,128)(2,1)S(1)} %add_convert_fusion.2.refs_19_), channel_id=1, source_target_pairs={{0,4},{1,9},{2,6},{3,11},{4,0},{5,13},{6,2},{7,15},{8,12},{9,1},{1... | collective-permute-start | bytes 2654216 | tf_op jit(solution)/shard_map/ppermute | solution.py:112
  158.8 15.7 %collective-permute-start.28 = (bf16[1,104,768]{2,1,0:T(8,128)(2,1)S(1)}, bf16[1,104,768]{2,1,0:T(8,128)(2,1)S(1)}, u32[]{:S(2)}, u32[]{:S(2)}) collective-permute-start(bf16[1,104,768]{2,1,0:T(8,128)(2,1)S(1)} %maximum_bitcast_fusion.1.refs_20_), channel_id=1, source_target_pairs={{0,24},{1,25},{2,26},{3,27},{4,28},{5,29},{6,30},{7,31},{8,16},{9,... | collective-permute-start | bytes 479240 | tf_op jit(solution)/shard_map/ppermute | solution.py:112
  171.7 19.8 %collective-permute-start.42 = (f32[16,768]{1,0:T(8,128)S(1)}, f32[16,768]{1,0:T(8,128)S(1)}, u32[]{:S(2)}, u32[]{:S(2)}) collective-permute-start(f32[16,768]{1,0:T(8,128)S(1)} %get-tuple-element.263.refs_14_), channel_id=1, source_target_pairs={{0,1},{1,0},{2,3},{3,2},{4,5},{5,4},{6,7},{7,6},{8,9},{9,8},{10,11... | collective-permute-start | bytes 147464 | tf_op jit(solution)/shard_map/ppermute | solution.py:112
  174.5 15.8 %collective-permute-start.40 = (bf16[2,104,768]{2,1,0:T(8,128)(2,1)S(1)}, bf16[2,104,768]{2,1,0:T(8,128)(2,1)S(1)}, u32[]{:S(2)}, u32[]{:S(2)}) collective-permute-start(bf16[2,104,768]{2,1,0:T(8,128)(2,1)S(1)} %constant_dynamic-update-slice_fusion.refs_13_), channel_id=1, source_target_pairs={{0,8},{1,5},{2,10},{3,7},{4,12},{5,1},{6,14},{7,3},{8,0},{9,13},{1... | collective-permute-start | bytes 958472 | tf_op jit(solution)/shard_map/ppermute | solution.py:112
  174.8 14.8 %collective-permute-start.35 = (bf16[2,24,3840]{2,1,0:T(8,128)(2,1)S(1)}, bf16[2,24,3840]{2,1,0:T(8,128)(2,1)S(1)}, u32[]{:S(2)}, u32[]{:S(2)}) collective-permute-start(bf16[2,24,3840]{2,1,0:T(8,128)(2,1)S(1)} %add_convert_fusion.6.refs_12_), channel_id=1, source_target_pairs={{0,24},{1,3},{2,26},{3,1},{4,28},{5,7},{6,30},{7,5},{8,16},{9,11},... | collective-permute-start | bytes 1105928 | tf_op jit(solution)/shard_map/ppermute | solution.py:112
  177.8 14.7 %collective-permute-start.29 = (bf16[4,24,2304]{2,1,0:T(8,128)(2,1)S(1)}, bf16[4,24,2304]{2,1,0:T(8,128)(2,1)S(1)}, u32[]{:S(2)}, u32[]{:S(2)}) collective-permute-start(bf16[4,24,2304]{2,1,0:T(8,128)(2,1)S(1)} %add_convert_fusion.5.refs_11_), channel_id=1, source_target_pairs={{0,8},{1,5},{2,10},{3,7},{4,12},{5,1},{6,14},{7,3},{8,0},{9,13},{1... | collective-permute-start | bytes 1327112 | tf_op jit(solution)/shard_map/ppermute | solution.py:112
  190.4 37.2 %collective-permute-start.41 = (bf16[4,104,768]{2,1,0:T(8,128)(2,1)S(1)}, bf16[4,104,768]{2,1,0:T(8,128)(2,1)S(1)}, u32[]{:S(2)}, u32[]{:S(2)}) collective-permute-start(bf16[4,104,768]{2,1,0:T(8,128)(2,1)S(1)} %constant_dynamic-update-slice_fusion.10.refs_1_), channel_id=1, source_target_pairs={{0,4},{1,9},{2,6},{3,11},{4,0},{5,13},{6,2},{7,15},{8,12},{9,1},{1... | collective-permute-start | bytes 1916936 | tf_op jit(solution)/shard_map/ppermute | solution.py:112
  191.5 8.9 %collective-permute-start.43 = (f32[16,768]{1,0:T(8,128)S(1)}, f32[16,768]{1,0:T(8,128)S(1)}, u32[]{:S(2)}, u32[]{:S(2)}) collective-permute-start(f32[16,768]{1,0:T(8,128)S(1)} %add.346), channel_id=1, source_target_pairs={{0,8},{1,9},{2,10},{3,11},{4,12},{5,13},{6,14},{7,15},{8,0},{9,1},... | collective-permute-start | bytes 147464 | tf_op jit(solution)/shard_map/ppermute | solution.py:112
  192.6 10.5 %collective-permute-start.30 = (bf16[2,24,2304]{2,1,0:T(8,128)(2,1)S(1)}, bf16[2,24,2304]{2,1,0:T(8,128)(2,1)S(1)}, u32[]{:S(2)}, u32[]{:S(2)}) collective-permute-start(bf16[2,24,2304]{2,1,0:T(8,128)(2,1)S(1)} %add_convert_fusion.8), channel_id=1, source_target_pairs={{0,24},{1,3},{2,26},{3,1},{4,28},{5,7},{6,30},{7,5},{8,16},{9,11},... | collective-permute-start | bytes 663560 | tf_op jit(solution)/shard_map/ppermute | solution.py:112
  199.2 9.4 %collective-permute-start.37 = (bf16[1,24,3840]{2,1,0:T(8,128)(2,1)S(1)}, bf16[1,24,3840]{2,1,0:T(8,128)(2,1)S(1)}, u32[]{:S(2)}, u32[]{:S(2)}) collective-permute-start(bf16[1,24,3840]{2,1,0:T(8,128)(2,1)S(1)} %maximum_bitcast_fusion), channel_id=1, source_target_pairs={{0,24},{1,25},{2,26},{3,27},{4,28},{5,29},{6,30},{7,31},{8,16},{9,... | collective-permute-start | bytes 552968 | tf_op jit(solution)/shard_map/ppermute | solution.py:112
  200.4 9.2 %collective-permute-start.44 = (f32[16,768]{1,0:T(8,128)S(1)}, f32[16,768]{1,0:T(8,128)S(1)}, u32[]{:S(2)}, u32[]{:S(2)}) collective-permute-start(f32[16,768]{1,0:T(8,128)S(1)} %add.347), channel_id=1, source_target_pairs={{0,24},{1,25},{2,26},{3,27},{4,28},{5,29},{6,30},{7,31},{8,16},{9,... | collective-permute-start | bytes 147464 | tf_op jit(solution)/shard_map/ppermute | solution.py:112
  222.7 14.9 %collective-permute-start.39 = (bf16[4,24,3840]{2,1,0:T(8,128)(2,1)S(1)}, bf16[4,24,3840]{2,1,0:T(8,128)(2,1)S(1)}, u32[]{:S(2)}, u32[]{:S(2)}) collective-permute-start(bf16[4,24,3840]{2,1,0:T(8,128)(2,1)S(1)} %constant_dynamic-update-slice_fusion.8.refs_1_), channel_id=1, source_target_pairs={{0,4},{1,9},{2,6},{3,11},{4,0},{5,13},{6,2},{7,15},{8,12},{9,1},{1... | collective-permute-start | bytes 2211848 | tf_op jit(solution)/shard_map/ppermute | solution.py:112
  226.4 16.4 %collective-permute-start.34 = (bf16[4,24,2304]{2,1,0:T(8,128)(2,1)S(1)}, bf16[4,24,2304]{2,1,0:T(8,128)(2,1)}, u32[]{:S(2)}, u32[]{:S(2)}) collective-permute-start(bf16[4,24,2304]{2,1,0:T(8,128)(2,1)S(1)} %constant_dynamic-update-slice_fusion.4.refs_3_.refs_1_), channel_id=1, source_target_pairs={{0,4},{1,9},{2,6},{3,11},{4,0},{5,13},{6,2},{7,15},{8,12},{9,1},{1... | collective-permute-start | bytes 1327112 | tf_op jit(solution)/shard_map/ppermute | solution.py:112
  (85 other events, 680.4 us)

commit v2 on v1

--- a/solution.py
+++ b/solution.py
@@ -238,30 +238,21 @@
     qkv_ref[0, :, 2 * D :] = (dot(n1, w_ref[:, 2 * D :]) + vec_ref[5:6, :]).astype(BF16)
 
 
-def lane_slab(slab):
-    return pl.ds(pl.multiple_of(slab * LANES, LANES), LANES)
-
-
 def mix_kernel(qkv_ref, a_ref):
     low = lax.broadcasted_iota(jnp.int32, (1, LANES), 1) < HDIM
-
-    def some_slabs(turn, _):
-        for slab in [3 * turn + k for k in range(3)]:
-            cols = lane_slab(slab)
-            q = qkv_ref[0, :, cols] * jnp.asarray(HDIM**-0.5, BF16)
-            k = qkv_ref[0, :, lane_slab(slab + SLABS)]
-            v = qkv_ref[0, :, lane_slab(slab + 2 * SLABS)]
-            outs = []
-            for head in range(2):
-                mine = low if head == 0 else jnp.logical_not(low)
-                scores = dot_last(jnp.where(mine, q, jnp.zeros_like(q)), k)
-                e = jnp.exp(scores - jnp.max(scores, axis=-1, keepdims=True))
-                p = (e * (1.0 / jnp.sum(e, axis=-1, keepdims=True))).astype(BF16)
-                outs.append(dot(p, v))
-            a_ref[0, :, cols] = jnp.where(low, outs[0], outs[1]).astype(BF16)
-        return 0
-
-    lax.fori_loop(0, SLABS // 3, some_slabs, 0)
+    for slab in range(SLABS):
+        cols = slice(slab * LANES, (slab + 1) * LANES)
+        q = qkv_ref[0, :, cols] * jnp.asarray(HDIM**-0.5, BF16)
+        k = qkv_ref[0, :, D + slab * LANES : D + (slab + 1) * LANES]
+        v = qkv_ref[0, :, 2 * D + slab * LANES : 2 * D + (slab + 1) * LANES]
+        outs = []
+        for head in range(2):
+            mine = low if head == 0 else jnp.logical_not(low)
+            scores = dot_last(jnp.where(mine, q, jnp.zeros_like(q)), k)
+            e = jnp.exp(scores - jnp.max(scores, axis=-1, keepdims=True))
+            inverse = 1.0 / jnp.sum(e, axis=-1, keepdims=True)
+            outs.append(dot(e.astype(BF16), v) * inverse)
+        a_ref[0, :, cols] = jnp.where(low, outs[0], outs[1]).astype(BF16)
 
 
 def fc1_kernel(rows, place_ref, tok_ref, img_ref, a_ref, vec_ref, *refs):
@@ -422,14 +413,14 @@
         for head in range(2):
             mine = low if head == 0 else jnp.logical_not(low)
             zero = jnp.zeros_like(q)
-            scores = dot_last(jnp.where(mine, q, zero), k)
-            e = jnp.exp(scores - jnp.max(scores, axis=-1, keepdims=True))
-            p = e * (1.0 / jnp.sum(e, axis=-1, keepdims=True))
-            gvs.append(dot_first(p.astype(BF16), da))
-            dp = dot_last(jnp.where(mine, da, zero), v)
-            ds = (p * (dp - jnp.sum(p * dp, axis=-1, keepdims=True))).astype(BF16)
-            gqs.append(dot(ds, k))
-            gks.append(dot_first(ds, q))
+            scores = dot_last(k, jnp.where(mine, q, zero))
+            e = jnp.exp(scores - jnp.max(scores, axis=0, keepdims=True))
+            p = e * (1.0 / jnp.sum(e, axis=0, keepdims=True))
+            gvs.append(dot(p.astype(BF16), da))
+            dp = dot_last(v, jnp.where(mine, da, zero))
+            ds = (p * (dp - jnp.sum(p * dp, axis=0, keepdims=True))).astype(BF16)
+            gqs.append(dot_first(ds, k))
+            gks.append(dot(ds, q))
         gq = jnp.where(low, gqs[0], gqs[1]) * (HDIM**-0.5)
         gk = jnp.where(low, gks[0], gks[1])
         gv = jnp.where(low, gvs[0], gvs[1])
@@ -624,7 +615,19 @@
             total = total + part[low:high].astype(F32)
         return total
 
+    def last_moves(self, sends):
+        pairs = list(zip(*(order[self.place :] for order in self.plan.scatter)))
+        (far, far_odd), (near, near_odd) = pairs
+        moves = [(near, near_odd), (far, far_odd), (far ^ near, far_odd ^ near_odd)]
+        for spot, masks in enumerate(moves):
+            self.parts.append(self.plan.exchange(sends[spot : spot + 1], *masks))
+        self.count, self.place = 1, self.place + 2
+
     def add(self):
+        if self.count == 4:
+            self.sent = self.call.hold(self.total(1, 4).astype(BF16))
+            self.last_moves(self.sent)
+            return
         self.count //= 2
         total = self.total(self.count, 2 * self.count)
         self.sent = self.call.hold(total.astype(BF16))
@@ -776,7 +779,9 @@
     )
 
     set_b = cast([w_out, w_fc1])
+    near_a = set_a[2]
     set_a = last_piece(spread_pieces(set_a, [set_b[0]] + vec_parts))
+    set_c = cast([w_fc2], [near_a])
 
     n1, qkv = call(
         functools.partial(qkv_kernel, rows_d),
@@ -792,9 +797,8 @@
         "qkv",
     )
 
-    set_c = cast([w_fc2])
     near_b = set_b[2]
-    set_b = spread_pieces(set_b, set_c[0])
+    set_b = spread_pieces(set_b, n1)
     (mixed,) = call(
         mix_kernel,
         (pairs,),
@@ -953,28 +957,8 @@
         )
         if number == 0:
             sum_1.add()
-        sum_2.add()
+            sum_2.add()
     dq, dkv, attn_sum = back
-
-    got = call(
-        gqkv_kernel,
-        (3,),
-        [owners],
-        [
-            (n1, full((pairs, length, D))),
-            (dq, full((pairs, slots, D))),
-            (
-                dkv,
-                pl.BlockSpec((pairs, length, D), lambda i, *_: (0, 0, jnp.where(i == 2, 1, 0))),
-            ),
-        ],
-        grad_outs(D, 3 * D, D),
-        [pltpu.VMEM((D, pairs * length), BF16), pltpu.VMEM((D, D), F32)],
-        spent(9),
-        "gqkv",
-    )
-    sum_3 = grad_sum(got)
-    sum_1.add()
 
     fallback = (D // nd) % 8 != 0 or (FF // nd) % 8 != 0
     places = OWN + nd
@@ -1018,10 +1002,33 @@
         cuts = np.cumsum([0] + list(widths))
         return [blocks[:, a:b] for a, b in zip(cuts[:-1], cuts[1:])]
 
+    while sum_2.count > 1:
+        sum_2.add()
+    moved_2, (new_m2, new_v2) = finish(sum_2, (3,), (w_fc2,), ((m_fc2, v_fc2),), riders)
+
+    got = call(
+        gqkv_kernel,
+        (3,),
+        [owners],
+        [
+            (n1, full((pairs, length, D))),
+            (dq, full((pairs, slots, D))),
+            (
+                dkv,
+                pl.BlockSpec((pairs, length, D), lambda i, *_: (0, 0, jnp.where(i == 2, 1, 0))),
+            ),
+        ],
+        grad_outs(D, 3 * D, D),
+        [pltpu.VMEM((D, pairs * length), BF16), pltpu.VMEM((D, D), F32)],
+        spent(9),
+        "gqkv",
+    )
+    sum_3 = grad_sum(got)
+    sum_1.add()
+
     sum_3.add()
-
     paced, call.last = call.last, sum_3.sent
-    moved_2, (new_m2, new_v2) = finish(sum_2, (3,), (w_fc2,), ((m_fc2, v_fc2),), riders)
+    moved_2.join()
     call.last = paced
 
     grad_tokens, vec_sum = call(
@@ -1088,12 +1095,13 @@
         "out",
     )
 
-    moved_1 = moved_3 = None
+    moved_1 = moved_3 = put_2 = None
     while moved_3 is None or moved_3.place < last:
         token = None
         if sum_3.count > 1:
             sum_3.add()
             token = sum_3.sent
+            call.last = token
         elif moved_3 is None:
             moved_3, (new_mq, new_vq) = finish(sum_3, (0,), (w_qkv,), ((m_qkv, v_qkv),))
             token = moved_3.blocks
@@ -1112,15 +1120,20 @@
             moved_2.join()
         vec_step()
         call.last = token
+        if put_2 is None and moved_2.place == last:
+            tail = call.pin([moved_2.blocks, moved_2.got])
+            (put_2,) = put(moved_2, (D,), FF // nd)
     while len(vec_gens) >= vec_place:
         vec_step()
     while moved_1.place < last:
         moved_1.join()
-    while moved_2.place < last:
-        moved_2.join()
     call.waiting = []
-    tail = call.pin([moved_2.blocks, moved_2.got])
-    (new_2,) = put(moved_2, (D,), FF // nd)
+    if put_2 is None:
+        while moved_2.place < last:
+            moved_2.join()
+        tail = call.pin([moved_2.blocks, moved_2.got])
+        (put_2,) = put(moved_2, (D,), FF // nd)
+    new_2 = put_2
     new_1, new_o = put(moved_1, (FF, D), D // nd)
     (new_q,) = put(moved_3, (3 * D,), D // nd)
 

time: 249 us -> 280 us (1.12)
  other arithmetic: 17.9 us -> 29.2 us
  local copies, waits for them, and re-layouts: 16.1 us -> 26.2 us
  waiting for transfers between devices: 38.8 us -> 48.7 us
  starting transfers between devices: 44 us -> 53.2 us
  Pallas kernels: 129 us -> 120 us
    unnamed x146 -> x178, local copies, waits for them, and re-layouts: 13 us -> 23 us
    ppermute x47 -> x50, waiting for transfers between devices: 38.8 us -> 48.7 us  [exchange(): return lax.ppermute(value, ('batch', 'fsdp'), pairs)]
    pallas_call x19, Pallas kernels: 129 us -> 120 us  [__call__(): pl.pallas_call(body, grid_spec=pltpu.PrefetchScalarGridSpec(num_scalar_pr...]
    ppermute x47 -> x50, starting transfers between devices: 44 us -> 53.2 us  [exchange(): return lax.ppermute(value, ('batch', 'fsdp'), pairs)]
    convert_element_type x0 -> x3, other arithmetic: none -> 4.06 us  [add(): self.sent = self.call.hold(self.total(1, 4).astype(BF16))]
    convert_element_type x12 -> x6, other arithmetic: 6.63 us -> 9.98 us  [add(): self.sent = self.call.hold(total.astype(BF16))]
  transfers between devices with their start and end apart: 47 -> 50, of which waited for: 17 -> 13; matrix products, arithmetic and copies ran while one was open for 8% -> 11% of each run, Pallas kernels for 51% -> 42%
where the time goes in v2:
time: 280 us; the launch traced here: 279 us
  Pallas kernels  120 us (43%)
  starting transfers between devices  53.2 us (19%)
  waiting for transfers between devices  48.7 us (17%)
  other arithmetic  29.2 us (10%)
  local copies, waits for them, and re-layouts  26.2 us (9%)
    pallas_call x19, Pallas kernels, __call__(): pl.pallas_call(body, grid_spec=pltpu.PrefetchScalarGridSpec(num_scalar_pr...  120 us
    ppermute x50, starting transfers between devices, exchange(): return lax.ppermute(value, ('batch', 'fsdp'), pairs)  53.2 us
    ppermute x50, waiting for transfers between devices, exchange(): return lax.ppermute(value, ('batch', 'fsdp'), pairs)  48.7 us
    unnamed x178, local copies, waits for them, and re-layouts  23 us
    convert_element_type x6, other arithmetic, add(): self.sent = self.call.hold(total.astype(BF16))  9.98 us
    convert_element_type x3, other arithmetic, finish(): news.append(new_w.astype(BF16))  6.23 us
  transfers between devices with their start and end apart: 50, of which 13 were waited for; matrix products, arithmetic and copies ran while one was open for 11% of the time, Pallas kernels for 42%

profile of v2, /device:TPU:0, one launch (start us, length us, event | category | flops | bytes accessed | tf_op | source)
XLA Modules:
  0.0 278.7 jit_solution(8822225726676967023)
XLA Ops:
  2.0 3.0 %collective-permute-start = (bf16[14,192]{1,0:T(8,128)(2,1)}, bf16[14,192]{1,0:T(8,128)(2,1)S(1)}, u32[]{:S(2)}, u32[]{:S(2)}) collective-permute-start(bf16[14,192]{1,0:T(8,128)(2,1)} %convert_element_type.206), channel_id=1, source_target_pairs={{0,2},{1,3},{2,0},{3,1},{4,6},{5,7},{6,4},{7,5},{8,10},{9,11},{10,... | collective-permute-start | bytes 16136 | tf_op jit(solution)/shard_map/ppermute | solution.py:112
  11.2 3.3 %order.1 = (bf16[4,256,256]{2,1,0:T(8,128)(2,1)S(1)}, bf16[4,256,768]{2,1,0:T(8,128)(2,1)S(1)}, bf16[4,256,128]{2,1,0:T(8,128)(2,1)S(1)}, bf16[4,128,768]{2,1,0:T(8,128)(2,1)S(1)}) custom-call(s32[4]{0:T(128)S(1)} %copy-done.45, s32[4,1,128]{2,1,0:T(1,128)S(1)} %bitcast.31, bf16[4,256,768]{2,1,0:T(8,128)(2,1)S(1)} %copy-done.29, ...), custom_call_target="tpu_custom_call" | custom-call | flops 17999998976 | bytes 60000000 | tf_op jit(solution)/shard_map/order/pallas_call | solution.py:579
  17.9 4.0 %collective-permute-done.4.refs_2_.refs_6_.refs_14_ = bf16[96,2304]{1,0:T(8,128)(2,1)S(1)} collective-permute-done((bf16[96,2304]{1,0:T(8,128)(2,1)S(1)}, bf16[96,2304]{1,0:T(8,128)(2,1)S(1)}, u32[]{:S(2)}, u32[]{:S(2)}) %collective-permute-start.4) | collective-permute-done | bytes 442400 | tf_op jit(solution)/shard_map/ppermute | solution.py:112
  23.9 6.3 %collective-permute-done.5.refs_7_.refs_15_ = bf16[96,2304]{1,0:T(8,128)(2,1)} collective-permute-done((bf16[96,2304]{1,0:T(8,128)(2,1)S(1)}, bf16[96,2304]{1,0:T(8,128)(2,1)}, u32[]{:S(2)}, u32[]{:S(2)}) %collective-permute-start.5) | collective-permute-done | bytes 442400 | tf_op jit(solution)/shard_map/ppermute | solution.py:112
  32.9 8.1 %qkv.1 = (bf16[4,256,768]{2,1,0:T(8,128)(2,1)S(1)}, bf16[4,256,2304]{2,1,0:T(8,128)(2,1)S(1)}) custom-call(s32[52]{0:T(128)S(1)} %get-tuple-element.281.refs_0_, bf16[4,256,768]{2,1,0:T(8,128)(2,1)S(1)} %copy-done.13, bf16[4,256,128]{2,1,0:T(8,128)(2,1)S(1)} %copy-done.21, f32[16,768]{1,0:T(8,128)S(1)} %fusion.12.refs_3_.refs_4_, ...), custom_call_target="tpu_custom_call" | custom-call | flops 300000000 | bytes 1000000 | tf_op jit(solution)/shard_map/qkv/pallas_call | solution.py:579
  43.2 5.9 %mix.1.refs_3_.refs_11_ = bf16[4,256,768]{2,1,0:T(8,128)(2,1)S(1)} custom-call(bf16[4,256,2304]{2,1,0:T(8,128)(2,1)S(1)} %get-tuple-element.142.refs_0_.refs_2_, bf16[96,3840]{1,0:T(8,128)(2,1)} %collective-permute-done.8.refs_1_.refs_7_, bf16[4,256,2304]{2,1,0:T(8,128)(2,1)S(1)} %get-tuple-element.142.refs_0_.refs_2_), custom_call_target="tpu_custom_call" | custom-call | flops 3000000000 | bytes 10000000 | tf_op jit(solution)/shard_map/mix/pallas_call | solution.py:579
  49.1 3.7 %collective-permute-done.10.refs_8_ = bf16[96,3840]{1,0:T(8,128)(2,1)S(1)} collective-permute-done((bf16[96,3840]{1,0:T(8,128)(2,1)}, bf16[96,3840]{1,0:T(8,128)(2,1)S(1)}, u32[]{:S(2)}, u32[]{:S(2)}) %collective-permute-start.10) | collective-permute-done | bytes 737312 | tf_op jit(solution)/shard_map/ppermute | solution.py:112
  55.1 13.6 %fc1.1 = (f32[4,256,768]{2,1,0:T(8,128)S(1)}, bf16[4,256,768]{2,1,0:T(8,128)(2,1)S(1)}, bf16[4,256,3072]{2,1,0:T(8,128)(2,1)S(1)}, bf16[4,128,3072]{2,1,0:T(8,128)(2,1)S(1)}) custom-call(s32[52]{0:T(128)S(1)} %get-tuple-element.281.refs_0_, bf16[4,256,768]{2,1,0:T(8,128)(2,1)S(1)} %copy-done.13, bf16[4,256,128]{2,1,0:T(8,128)(2,1)S(1)} %copy-done.21, ...), custom_call_target="tpu_custom_call" | custom-call | flops 54000001024 | bytes 180000000 | tf_op jit(solution)/shard_map/fc1/pallas_call | solution.py:579
  71.9 6.6 %gw2.1 = (bf16[16,96,768]{2,1,0:T(8,128)(2,1)S(1)}, bf16[16,96,768]{2,1,0:T(8,128)(2,1)}, f32[1,768]{1,0:T(1,128)S(1)}) custom-call(s32[52]{0:T(128)S(1)} %get-tuple-element.281.refs_0_, bf16[4,256,3072]{2,1,0:T(8,128)(2,1)S(1)} %get-tuple-element.146.refs_1_, bf16[4,128,768]{2,1,0:T(8,128)(2,1)S(1)} %copy-done.18, ...), custom_call_target="tpu_custom_call" | custom-call | flops 24000000000 | bytes 80000000 | tf_op jit(solution)/shard_map/gw2/pallas_call | solution.py:579
  84.9 7.1 %df.1 = (bf16[512,3072]{1,0:T(8,128)(2,1)S(1)}, f32[1,3072]{1,0:T(1,128)S(1)}) custom-call(s32[52]{0:T(128)S(1)} %get-tuple-element.281.refs_0_, bf16[4,128,768]{2,1,0:T(8,128)(2,1)S(1)} %copy-done.18, bf16[4,128,3072]{2,1,0:T(8,128)(2,1)S(1)} %copy-done.50, bf16[768,768]{1,0:T(8,128)(2,1)} %get-tuple-element.149.refs_3_.refs_5_, ...), custom_call_target="tpu_custom_call" | custom-call | flops 20999999488 | bytes 70000000 | tf_op jit(solution)/shard_map/df/pallas_call | solution.py:579
  95.4 7.6 %mlp_back.1 = (f32[4,128,768]{2,1,0:T(8,128)S(1)}, bf16[4,128,768]{2,1,0:T(8,128)(2,1)S(1)}, bf16[4,128,768]{2,1,0:T(8,128)(2,1)S(1)}, f32[8,768]{1,0:T(8,128)S(1)}) custom-call(s32[52]{0:T(128)S(1)} %get-tuple-element.281.refs_0_, bf16[512,3072]{1,0:T(8,128)(2,1)S(1)} %get-tuple-element.155.refs_1_.refs_2_, bf16[4,128,768]{2,1,0:T(8,128)(2,1)S(1)} %copy-done.18, ...), custom_call_target="tpu_custom_call" | custom-call | flops 30000001024 | bytes 100000000 | tf_op jit(solution)/shard_map/mlp_back/pallas_call | solution.py:579
  104.1 6.9 %gw1o.1 = (bf16[16,24,3840]{2,1,0:T(8,128)(2,1)S(1)}, bf16[16,24,3840]{2,1,0:T(8,128)(2,1)S(1)}) custom-call(s32[52]{0:T(128)S(1)} %get-tuple-element.281.refs_0_, bf16[4,256,768]{2,1,0:T(8,128)(2,1)S(1)} %copy-done.57, bf16[512,3072]{1,0:T(8,128)(2,1)S(1)} %get-tuple-element.155.refs_1_.refs_2_, bf16[4,256,768]{2,1,0:T(8,128)(2,1)S(1)} %copy-done.16, ...), custom_call_target="tpu_custom_call" | custom-call | flops 27000000512 | bytes 90000000 | tf_op jit(solution)/shard_map/gw1o/pallas_call | solution.py:579
  114.5 9.2 %attn_back.2 = (bf16[4,128,768]{2,1,0:T(8,128)(2,1)S(1)}, bf16[4,256,1536]{2,1,0:T(8,128)(2,1)S(1)}, f32[8,768]{1,0:T(8,128)S(1)}) custom-call(bf16[4,256,2304]{2,1,0:T(8,128)(2,1)S(1)} %bitcast.30, bf16[4,128,768]{2,1,0:T(8,128)(2,1)S(1)} %get-tuple-element.161.refs_1_, bf16[4,96,768]{2,1,0:T(8,128)(2,1)S(1)} %add_convert_fusion.4.refs_2_, ...), custom_call_target="tpu_custom_call" | custom-call | flops 35999997952 | bytes 120000000 | tf_op jit(solution)/shard_map/attn_back/pallas_call | solution.py:579
  125.5 2.7 collective-permute-start.23
  132.7 9.2 %attn_back.3 = (bf16[4,128,768]{2,1,0:T(8,128)(2,1)S(1)}, bf16[4,256,1536]{2,1,0:T(8,128)(2,1)S(1)}, f32[8,768]{1,0:T(8,128)S(1)}) custom-call(bf16[4,256,2304]{2,1,0:T(8,128)(2,1)S(1)} %bitcast.30, bf16[4,128,768]{2,1,0:T(8,128)(2,1)S(1)} %get-tuple-element.161.refs_1_, ...), custom_call_target="tpu_custom_call", output_to_operand_aliasing={{0}: (2, {}), {1}: (3, {})} | custom-call | flops 35999997952 | bytes 120000000 | tf_op jit(solution)/shard_map/attn_back/pallas_call | solution.py:579
  141.9 2.6 subtract_convert_fusion.1
  144.7 7.0 %gqkv.1 = (bf16[16,24,2304]{2,1,0:T(8,128)(2,1)S(1)}, bf16[16,24,2304]{2,1,0:T(8,128)(2,1)}) custom-call(s32[52]{0:T(128)S(1)} %get-tuple-element.281.refs_0_, bf16[4,256,768]{2,1,0:T(8,128)(2,1)S(1)} %copy-done.32, bf16[4,128,768]{2,1,0:T(8,128)(2,1)S(1)} %get-tuple-element.178.refs_2_.refs_4_, ...), custom_call_target="tpu_custom_call" | custom-call | flops 27000000512 | bytes 90000000 | tf_op jit(solution)/shard_map/gqkv/pallas_call | solution.py:579
  153.1 2.9 %collective-permute-start.28 = (bf16[1,104,768]{2,1,0:T(8,128)(2,1)S(1)}, bf16[1,104,768]{2,1,0:T(8,128)(2,1)S(1)}, u32[]{:S(2)}, u32[]{:S(2)}) collective-permute-start(bf16[1,104,768]{2,1,0:T(8,128)(2,1)S(1)} %maximum_bitcast_fusion.1.refs_4_), channel_id=1, source_target_pairs={{0,24},{1,25},{2,26},{3,27},{4,28},{5,29},{6,30},{7,31},{8,16},{9,... | collective-permute-start | bytes 479240 | tf_op jit(solution)/shard_map/ppermute | solution.py:112
  166.1 12.1 %grad_in.1 = (f32[4,256,768]{2,1,0:T(8,128)}, f32[16,768]{1,0:T(8,128)S(1)}) custom-call(s32[52]{0:T(128)S(1)} %get-tuple-element.281.refs_0_, bf16[4,256,768]{2,1,0:T(8,128)(2,1)S(1)} %copy-done.14, bf16[4,256,128]{2,1,0:T(8,128)(2,1)S(1)} %copy-done.22, f32[16,768]{1,0:T(8,128)S(1)} %copy-done.26, bf16[4,128,768]{2,1,0:T(8,128)(2,1)S(1)} %copy-done.63, ...), custom_call_target="tpu_custom_call" | custom-call | flops 44999999488 | bytes 150000000 | tf_op jit(solution)/shard_map/grad_in/pallas_call | solution.py:579
  178.2 4.1 %collective-permute-done.30 = bf16[2,104,768]{2,1,0:T(8,128)(2,1)S(1)} collective-permute-done((bf16[2,104,768]{2,1,0:T(8,128)(2,1)S(1)}, bf16[2,104,768]{2,1,0:T(8,128)(2,1)S(1)}, u32[]{:S(2)}, u32[]{:S(2)}) %collective-permute-start.30) | collective-permute-done | bytes 319520 | tf_op jit(solution)/shard_map/ppermute | solution.py:112
  186.2 3.3 %collective-permute-start.37 = (bf16[1,24,3840]{2,1,0:T(8,128)(2,1)S(1)}, bf16[1,24,3840]{2,1,0:T(8,128)(2,1)S(1)}, u32[]{:S(2)}, u32[]{:S(2)}) collective-permute-start(bf16[1,24,3840]{2,1,0:T(8,128)(2,1)S(1)} %get-tuple-element.264), channel_id=1, source_target_pairs={{0,24},{1,3},{2,26},{3,1},{4,28},{5,7},{6,30},{7,5},{8,16},{9,11},... | collective-permute-start | bytes 552968 | tf_op jit(solution)/shard_map/ppermute | solution.py:112
  191.2 2.8 copy-done.48
  193.9 10.6 %out.1 = bf16[4,256,768]{2,1,0:T(8,128)(2,1)} custom-call(s32[52]{0:T(128)S(1)} %get-tuple-element.281.refs_0_, bf16[4,256,3072]{2,1,0:T(8,128)(2,1)S(1)} %copy-done.48, f32[4,256,768]{2,1,0:T(8,128)S(1)} %copy-done.55, f32[16,768]{1,0:T(8,128)S(1)} %copy-done.26, bf16[4,256,256]{2,1,0:T(8,128)(2,1)S(1)} %copy-done.61, ...), custom_call_target="tpu_custom_call" | custom-call | flops 38999998464 | bytes 130000000 | tf_op jit(solution)/shard_map/out/pallas_call | solution.py:579
  208.8 3.1 %collective-permute-start.33 = (bf16[1,24,2304]{2,1,0:T(8,128)(2,1)}, bf16[1,24,2304]{2,1,0:T(8,128)(2,1)}, u32[]{:S(2)}, u32[]{:S(2)}) collective-permute-start(bf16[1,24,2304]{2,1,0:T(8,128)(2,1)} %get-tuple-element.270), channel_id=1, source_target_pairs={{0,24},{1,3},{2,26},{3,1},{4,28},{5,7},{6,30},{7,5},{8,16},{9,11},... | collective-permute-start | bytes 331784 | tf_op jit(solution)/shard_map/ppermute | solution.py:112
  220.1 3.7 %collective-permute-start.42 = (bf16[1,24,3840]{2,1,0:T(8,128)(2,1)S(1)}, bf16[1,24,3840]{2,1,0:T(8,128)(2,1)S(1)}, u32[]{:S(2)}, u32[]{:S(2)}) collective-permute-start(bf16[1,24,3840]{2,1,0:T(8,128)(2,1)S(1)} %maximum_bitcast_fusion.refs_4_), channel_id=1, source_target_pairs={{0,24},{1,25},{2,26},{3,27},{4,28},{5,29},{6,30},{7,31},{8,16},{9,... | collective-permute-start | bytes 552968 | tf_op jit(solution)/shard_map/ppermute | solution.py:112
  226.4 4.1 %collective-permute-start.46 = (f32[16,768]{1,0:T(8,128)S(1)}, f32[16,768]{1,0:T(8,128)S(1)}, u32[]{:S(2)}, u32[]{:S(2)}) collective-permute-start(f32[16,768]{1,0:T(8,128)S(1)} %add.310), channel_id=1, source_target_pairs={{0,8},{1,9},{2,10},{3,11},{4,12},{5,13},{6,14},{7,15},{8,0},{9,1},... | collective-permute-start | bytes 147464 | tf_op jit(solution)/shard_map/ppermute | solution.py:112
  232.6 2.5 place.3
  238.9 2.6 collective-permute-start.39
  242.4 4.2 %collective-permute-done.39 = bf16[1,24,2304]{2,1,0:T(8,128)(2,1)S(1)} collective-permute-done((bf16[1,24,2304]{2,1,0:T(8,128)(2,1)S(1)}, bf16[1,24,2304]{2,1,0:T(8,128)(2,1)S(1)}, u32[]{:S(2)}, u32[]{:S(2)}) %collective-permute-start.39) | collective-permute-done | bytes 110624 | tf_op jit(solution)/shard_map/ppermute | solution.py:112
  247.8 11.2 %collective-permute-done.40 = bf16[2,24,2304]{2,1,0:T(8,128)(2,1)S(1)} collective-permute-done((bf16[2,24,2304]{2,1,0:T(8,128)(2,1)S(1)}, bf16[2,24,2304]{2,1,0:T(8,128)(2,1)S(1)}, u32[]{:S(2)}, u32[]{:S(2)}) %collective-permute-start.40) | collective-permute-done | bytes 221216 | tf_op jit(solution)/shard_map/ppermute | solution.py:112
  262.6 7.9 %collective-permute-done.44.refs_2_ = bf16[4,24,3840]{2,1,0:T(8,128)(2,1)S(1)} collective-permute-done((bf16[4,24,3840]{2,1,0:T(8,128)(2,1)S(1)}, bf16[4,24,3840]{2,1,0:T(8,128)(2,1)S(1)}, u32[]{:S(2)}, u32[]{:S(2)}) %collective-permute-start.44) | collective-permute-done | bytes 737312 | tf_op jit(solution)/shard_map/ppermute | solution.py:112
  270.5 3.5 %place.4 = (f32[192,3072]{1,0:T(8,128)}, f32[192,768]{1,0:T(8,128)}) custom-call(s32[52]{0:T(128)S(1)} %get-tuple-element.281.refs_0_, bf16[4,24,3840]{2,1,0:T(8,128)(2,1)S(1)} %constant_dynamic-update-slice_fusion.10.refs_1_, bf16[4,24,3840]{2,1,0:T(8,128)(2,1)S(1)} %collective-permute-done.44.refs_2_, ...), custom_call_target="tpu_custom_call" | custom-call | flops 3000000000 | bytes 10000000 | tf_op jit(solution)/shard_map/place/pallas_call | solution.py:579
  (320 shorter events, 91.6 us)
Async XLA Ops:
  2.0 13.6 %collective-permute-start = (bf16[14,192]{1,0:T(8,128)(2,1)}, bf16[14,192]{1,0:T(8,128)(2,1)S(1)}, u32[]{:S(2)}, u32[]{:S(2)}) collective-permute-start(bf16[14,192]{1,0:T(8,128)(2,1)} %convert_element_type.206), channel_id=1, source_target_pairs={{0,2},{1,3},{2,0},{3,1},{4,6},{5,7},{6,4},{7,5},{8,10},{9,11},{10,... | collective-permute-start | bytes 16136 | tf_op jit(solution)/shard_map/ppermute | solution.py:112
  5.0 12.9 %collective-permute-start.2 = (bf16[14,192]{1,0:T(8,128)(2,1)}, bf16[14,192]{1,0:T(8,128)(2,1)}, u32[]{:S(2)}, u32[]{:S(2)}) collective-permute-start(bf16[14,192]{1,0:T(8,128)(2,1)} %convert_element_type.206), channel_id=1, source_target_pairs={{0,1},{1,0},{2,3},{3,2},{4,5},{5,4},{6,7},{7,6},{8,9},{9,8},{10,11... | collective-permute-start | bytes 16136 | tf_op jit(solution)/shard_map/ppermute | solution.py:112
  9.2 23.6 %collective-permute-start.3 = (bf16[192,2304]{1,0:T(8,128)(2,1)}, bf16[192,2304]{1,0:T(8,128)(2,1)}, u32[]{:S(2)}, u32[]{:S(2)}) collective-permute-start(bf16[192,2304]{1,0:T(8,128)(2,1)} %get-tuple-element.136.refs_4_.refs_12_), channel_id=1, source_target_pairs={{0,1},{1,0},{2,3},{3,2},{4,5},{5,4},{6,7},{7,6},{8,9},{9,8},{10,11... | collective-permute-start | bytes 2654216 | tf_op jit(solution)/shard_map/ppermute | solution.py:112
  9.7 12.1 %collective-permute-start.4 = (bf16[96,2304]{1,0:T(8,128)(2,1)S(1)}, bf16[96,2304]{1,0:T(8,128)(2,1)S(1)}, u32[]{:S(2)}, u32[]{:S(2)}) collective-permute-start(bf16[96,2304]{1,0:T(8,128)(2,1)S(1)} %get-tuple-element.133.refs_4_), channel_id=1, source_target_pairs={{0,2},{1,3},{2,0},{3,1},{4,6},{5,7},{6,4},{7,5},{8,10},{9,11},{10,... | collective-permute-start | bytes 1327112 | tf_op jit(solution)/shard_map/ppermute | solution.py:112
  23.4 17.7 %collective-permute-start.8 = (bf16[96,3840]{1,0:T(8,128)(2,1)S(1)}, bf16[96,3840]{1,0:T(8,128)(2,1)}, u32[]{:S(2)}, u32[]{:S(2)}) collective-permute-start(bf16[96,3840]{1,0:T(8,128)(2,1)S(1)} %get-tuple-element.140.refs_3_), channel_id=1, source_target_pairs={{0,2},{1,3},{2,0},{3,1},{4,6},{5,7},{6,4},{7,5},{8,10},{9,11},{10,... | collective-permute-start | bytes 2211848 | tf_op jit(solution)/shard_map/ppermute | solution.py:112
  41.1 11.7 %collective-permute-start.10 = (bf16[96,3840]{1,0:T(8,128)(2,1)}, bf16[96,3840]{1,0:T(8,128)(2,1)S(1)}, u32[]{:S(2)}, u32[]{:S(2)}) collective-permute-start(bf16[96,3840]{1,0:T(8,128)(2,1)} %collective-permute-done.8.refs_1_.refs_7_), channel_id=1, source_target_pairs={{0,4},{1,9},{2,6},{3,11},{4,0},{5,13},{6,2},{7,15},{8,12},{9,1},{1... | collective-permute-start | bytes 2211848 | tf_op jit(solution)/shard_map/ppermute | solution.py:112
  52.8 17.5 %collective-permute-start.14 = (bf16[384,768]{1,0:T(8,128)(2,1)S(1)}, bf16[384,768]{1,0:T(8,128)(2,1)}, u32[]{:S(2)}, u32[]{:S(2)}) collective-permute-start(bf16[384,768]{1,0:T(8,128)(2,1)S(1)} %get-tuple-element.141.refs_10_), channel_id=1, source_target_pairs={{0,2},{1,3},{2,0},{3,1},{4,6},{5,7},{6,4},{7,5},{8,10},{9,11},{10,... | collective-permute-start | bytes 1769480 | tf_op jit(solution)/shard_map/ppermute | solution.py:112
  53.1 28.8 %collective-permute-start.13 = (bf16[768,768]{1,0:T(8,128)(2,1)}, bf16[768,768]{1,0:T(8,128)(2,1)}, u32[]{:S(2)}, u32[]{:S(2)}) collective-permute-start(bf16[768,768]{1,0:T(8,128)(2,1)} %get-tuple-element.149.refs_3_.refs_5_), channel_id=1, source_target_pairs={{0,1},{1,0},{2,3},{3,2},{4,5},{5,4},{6,7},{7,6},{8,9},{9,8},{10,11... | collective-permute-start | bytes 3538952 | tf_op jit(solution)/shard_map/ppermute | solution.py:112
  80.6 11.4 %collective-permute-start.18 = (bf16[16,96,768]{2,1,0:T(8,128)(2,1)}, bf16[16,96,768]{2,1,0:T(8,128)(2,1)}, u32[]{:S(2)}, u32[]{:S(2)}) collective-permute-start(bf16[16,96,768]{2,1,0:T(8,128)(2,1)} %get-tuple-element.157), channel_id=1, source_target_pairs={{0,1},{1,0},{2,3},{3,2},{4,5},{5,4},{6,7},{7,6},{8,9},{9,8},{10,11... | collective-permute-start | bytes 7077896 | tf_op jit(solution)/shard_map/ppermute | solution.py:112
  93.8 17.3 %collective-permute-start.19 = (bf16[8,96,768]{2,1,0:T(8,128)(2,1)S(1)}, bf16[8,96,768]{2,1,0:T(8,128)(2,1)S(1)}, u32[]{:S(2)}, u32[]{:S(2)}) collective-permute-start(bf16[8,96,768]{2,1,0:T(8,128)(2,1)S(1)} %add_convert_fusion.1.refs_11_), channel_id=1, source_target_pairs={{0,4},{1,9},{2,6},{3,11},{4,0},{5,13},{6,2},{7,15},{8,12},{9,1},{1... | collective-permute-start | bytes 3538952 | tf_op jit(solution)/shard_map/ppermute | solution.py:112
  111.0 19.3 %collective-permute-start.20 = (bf16[16,24,3840]{2,1,0:T(8,128)(2,1)S(1)}, bf16[16,24,3840]{2,1,0:T(8,128)(2,1)S(1)}, u32[]{:S(2)}, u32[]{:S(2)}) collective-permute-start(bf16[16,24,3840]{2,1,0:T(8,128)(2,1)S(1)} %get-tuple-element.164.refs_3_), channel_id=1, source_target_pairs={{0,1},{1,0},{2,3},{3,2},{4,5},{5,4},{6,7},{7,6},{8,9},{9,8},{10,11... | collective-permute-start | bytes 8847368 | tf_op jit(solution)/shard_map/ppermute | solution.py:112
  125.0 16.9 %collective-permute-start.22 = (bf16[1,96,768]{2,1,0:T(8,128)(2,1)S(1)}, bf16[1,96,768]{2,1,0:T(8,128)(2,1)S(1)}, u32[]{:S(2)}, u32[]{:S(2)}) collective-permute-start(bf16[1,96,768]{2,1,0:T(8,128)(2,1)S(1)} %get-tuple-element.268), channel_id=1, source_target_pairs={{0,2},{1,25},{2,0},{3,27},{4,6},{5,29},{6,4},{7,31},{8,10},{9,17},... | collective-permute-start | bytes 442376 | tf_op jit(solution)/shard_map/ppermute | solution.py:112
  125.5 16.3 %collective-permute-start.23 = (bf16[1,96,768]{2,1,0:T(8,128)(2,1)S(1)}, bf16[1,96,768]{2,1,0:T(8,128)(2,1)S(1)}, u32[]{:S(2)}, u32[]{:S(2)}) collective-permute-start(bf16[1,96,768]{2,1,0:T(8,128)(2,1)S(1)} %get-tuple-element.267), channel_id=1, source_target_pairs={{0,24},{1,3},{2,26},{3,1},{4,28},{5,7},{6,30},{7,5},{8,16},{9,11},... | collective-permute-start | bytes 442376 | tf_op jit(solution)/shard_map/ppermute | solution.py:112
  128.3 13.6 %collective-permute-start.24 = (bf16[1,96,768]{2,1,0:T(8,128)(2,1)S(1)}, bf16[1,96,768]{2,1,0:T(8,128)(2,1)S(1)}, u32[]{:S(2)}, u32[]{:S(2)}) collective-permute-start(bf16[1,96,768]{2,1,0:T(8,128)(2,1)S(1)} %get-tuple-element.266), channel_id=1, source_target_pairs={{0,26},{1,27},{2,24},{3,25},{4,30},{5,31},{6,28},{7,29},{8,18},{9,... | collective-permute-start | bytes 442376 | tf_op jit(solution)/shard_map/ppermute | solution.py:112
  132.1 23.9 %collective-permute-start.27 = (bf16[8,24,3840]{2,1,0:T(8,128)(2,1)}, bf16[8,24,3840]{2,1,0:T(8,128)(2,1)}, u32[]{:S(2)}, u32[]{:S(2)}) collective-permute-start(bf16[8,24,3840]{2,1,0:T(8,128)(2,1)} %add_convert_fusion.refs_5_), channel_id=1, source_target_pairs={{0,4},{1,9},{2,6},{3,11},{4,0},{5,13},{6,2},{7,15},{8,12},{9,1},{1... | collective-permute-start | bytes 4423688 | tf_op jit(solution)/shard_map/ppermute | solution.py:112
  157.8 26.1 %collective-permute-start.29 = (bf16[4,24,3840]{2,1,0:T(8,128)(2,1)S(1)}, bf16[4,24,3840]{2,1,0:T(8,128)(2,1)S(1)}, u32[]{:S(2)}, u32[]{:S(2)}) collective-permute-start(bf16[4,24,3840]{2,1,0:T(8,128)(2,1)S(1)} %add_convert_fusion.3.refs_18_), channel_id=1, source_target_pairs={{0,8},{1,5},{2,10},{3,7},{4,12},{5,1},{6,14},{7,3},{8,0},{9,13},{1... | collective-permute-start | bytes 2211848 | tf_op jit(solution)/shard_map/ppermute | solution.py:112
  159.4 30.2 %collective-permute-start.26 = (bf16[8,24,2304]{2,1,0:T(8,128)(2,1)S(1)}, bf16[8,24,2304]{2,1,0:T(8,128)(2,1)S(1)}, u32[]{:S(2)}, u32[]{:S(2)}) collective-permute-start(bf16[8,24,2304]{2,1,0:T(8,128)(2,1)S(1)} %add_convert_fusion.2.refs_19_), channel_id=1, source_target_pairs={{0,4},{1,9},{2,6},{3,11},{4,0},{5,13},{6,2},{7,15},{8,12},{9,1},{1... | collective-permute-start | bytes 2654216 | tf_op jit(solution)/shard_map/ppermute | solution.py:112
  161.6 20.8 %collective-permute-start.30 = (bf16[2,104,768]{2,1,0:T(8,128)(2,1)S(1)}, bf16[2,104,768]{2,1,0:T(8,128)(2,1)S(1)}, u32[]{:S(2)}, u32[]{:S(2)}) collective-permute-start(bf16[2,104,768]{2,1,0:T(8,128)(2,1)S(1)} %constant_dynamic-update-slice_fusion.refs_20_), channel_id=1, source_target_pairs={{0,8},{1,5},{2,10},{3,7},{4,12},{5,1},{6,14},{7,3},{8,0},{9,13},{1... | collective-permute-start | bytes 958472 | tf_op jit(solution)/shard_map/ppermute | solution.py:112
  178.2 47.4 %collective-permute-start.45 = (f32[16,768]{1,0:T(8,128)S(1)}, f32[16,768]{1,0:T(8,128)}, u32[]{:S(2)}, u32[]{:S(2)}) collective-permute-start(f32[16,768]{1,0:T(8,128)S(1)} %get-tuple-element.239.refs_14_), channel_id=1, source_target_pairs={{0,1},{1,0},{2,3},{3,2},{4,5},{5,4},{6,7},{7,6},{8,9},{9,8},{10,11... | collective-permute-start | bytes 147464 | tf_op jit(solution)/shard_map/ppermute | solution.py:112
  182.4 37.7 %collective-permute-start.35 = (bf16[4,104,768]{2,1,0:T(8,128)(2,1)S(1)}, bf16[4,104,768]{2,1,0:T(8,128)(2,1)S(1)}, u32[]{:S(2)}, u32[]{:S(2)}) collective-permute-start(bf16[4,104,768]{2,1,0:T(8,128)(2,1)S(1)} %constant_dynamic-update-slice_fusion.2.refs_13_.refs_1_), channel_id=1, source_target_pairs={{0,4},{1,9},{2,6},{3,11},{4,0},{5,13},{6,2},{7,15},{8,12},{9,1},{1... | collective-permute-start | bytes 1916936 | tf_op jit(solution)/shard_map/ppermute | solution.py:112
  185.7 22.4 %collective-permute-start.36 = (bf16[1,24,3840]{2,1,0:T(8,128)(2,1)S(1)}, bf16[1,24,3840]{2,1,0:T(8,128)(2,1)S(1)}, u32[]{:S(2)}, u32[]{:S(2)}) collective-permute-start(bf16[1,24,3840]{2,1,0:T(8,128)(2,1)S(1)} %get-tuple-element.265), channel_id=1, source_target_pairs={{0,2},{1,25},{2,0},{3,27},{4,6},{5,29},{6,4},{7,31},{8,10},{9,17},... | collective-permute-start | bytes 552968 | tf_op jit(solution)/shard_map/ppermute | solution.py:112
  186.2 22.6 %collective-permute-start.37 = (bf16[1,24,3840]{2,1,0:T(8,128)(2,1)S(1)}, bf16[1,24,3840]{2,1,0:T(8,128)(2,1)S(1)}, u32[]{:S(2)}, u32[]{:S(2)}) collective-permute-start(bf16[1,24,3840]{2,1,0:T(8,128)(2,1)S(1)} %get-tuple-element.264), channel_id=1, source_target_pairs={{0,24},{1,3},{2,26},{3,1},{4,28},{5,7},{6,30},{7,5},{8,16},{9,11},... | collective-permute-start | bytes 552968 | tf_op jit(solution)/shard_map/ppermute | solution.py:112
  191.1 13.5 %collective-permute-start.31 = (bf16[4,24,2304]{2,1,0:T(8,128)(2,1)S(1)}, bf16[4,24,2304]{2,1,0:T(8,128)(2,1)S(1)}, u32[]{:S(2)}, u32[]{:S(2)}) collective-permute-start(bf16[4,24,2304]{2,1,0:T(8,128)(2,1)S(1)} %add_convert_fusion.6.refs_11_), channel_id=1, source_target_pairs={{0,8},{1,5},{2,10},{3,7},{4,12},{5,1},{6,14},{7,3},{8,0},{9,13},{1... | collective-permute-start | bytes 1327112 | tf_op jit(solution)/shard_map/ppermute | solution.py:112
  208.0 28.5 %collective-permute-start.32 = (bf16[1,24,2304]{2,1,0:T(8,128)(2,1)}, bf16[1,24,2304]{2,1,0:T(8,128)(2,1)}, u32[]{:S(2)}, u32[]{:S(2)}) collective-permute-start(bf16[1,24,2304]{2,1,0:T(8,128)(2,1)} %get-tuple-element.271), channel_id=1, source_target_pairs={{0,2},{1,25},{2,0},{3,27},{4,6},{5,29},{6,4},{7,31},{8,10},{9,17},... | collective-permute-start | bytes 331784 | tf_op jit(solution)/shard_map/ppermute | solution.py:112
  208.8 27.7 %collective-permute-start.33 = (bf16[1,24,2304]{2,1,0:T(8,128)(2,1)}, bf16[1,24,2304]{2,1,0:T(8,128)(2,1)}, u32[]{:S(2)}, u32[]{:S(2)}) collective-permute-start(bf16[1,24,2304]{2,1,0:T(8,128)(2,1)} %get-tuple-element.270), channel_id=1, source_target_pairs={{0,24},{1,3},{2,26},{3,1},{4,28},{5,7},{6,30},{7,5},{8,16},{9,11},... | collective-permute-start | bytes 331784 | tf_op jit(solution)/shard_map/ppermute | solution.py:112
  213.8 22.8 %collective-permute-start.34 = (bf16[1,24,2304]{2,1,0:T(8,128)(2,1)}, bf16[1,24,2304]{2,1,0:T(8,128)(2,1)}, u32[]{:S(2)}, u32[]{:S(2)}) collective-permute-start(bf16[1,24,2304]{2,1,0:T(8,128)(2,1)} %get-tuple-element.269), channel_id=1, source_target_pairs={{0,26},{1,27},{2,24},{3,25},{4,30},{5,31},{6,28},{7,29},{8,18},{9,... | collective-permute-start | bytes 331784 | tf_op jit(solution)/shard_map/ppermute | solution.py:112
  220.1 22.2 %collective-permute-start.42 = (bf16[1,24,3840]{2,1,0:T(8,128)(2,1)S(1)}, bf16[1,24,3840]{2,1,0:T(8,128)(2,1)S(1)}, u32[]{:S(2)}, u32[]{:S(2)}) collective-permute-start(bf16[1,24,3840]{2,1,0:T(8,128)(2,1)S(1)} %maximum_bitcast_fusion.refs_4_), channel_id=1, source_target_pairs={{0,24},{1,25},{2,26},{3,27},{4,28},{5,29},{6,30},{7,31},{8,16},{9,... | collective-permute-start | bytes 552968 | tf_op jit(solution)/shard_map/ppermute | solution.py:112
  242.3 16.6 %collective-permute-start.43 = (bf16[2,24,3840]{2,1,0:T(8,128)(2,1)S(1)}, bf16[2,24,3840]{2,1,0:T(8,128)(2,1)S(1)}, u32[]{:S(2)}, u32[]{:S(2)}) collective-permute-start(bf16[2,24,3840]{2,1,0:T(8,128)(2,1)S(1)} %constant_dynamic-update-slice_fusion.8), channel_id=1, source_target_pairs={{0,8},{1,5},{2,10},{3,7},{4,12},{5,1},{6,14},{7,3},{8,0},{9,13},{1... | collective-permute-start | bytes 1105928 | tf_op jit(solution)/shard_map/ppermute | solution.py:112
  246.6 12.3 %collective-permute-start.40 = (bf16[2,24,2304]{2,1,0:T(8,128)(2,1)S(1)}, bf16[2,24,2304]{2,1,0:T(8,128)(2,1)S(1)}, u32[]{:S(2)}, u32[]{:S(2)}) collective-permute-start(bf16[2,24,2304]{2,1,0:T(8,128)(2,1)S(1)} %constant_dynamic-update-slice_fusion.4), channel_id=1, source_target_pairs={{0,8},{1,5},{2,10},{3,7},{4,12},{5,1},{6,14},{7,3},{8,0},{9,13},{1... | collective-permute-start | bytes 663560 | tf_op jit(solution)/shard_map/ppermute | solution.py:112
  246.9 14.3 %collective-permute-start.49 = (f32[16,768]{1,0:T(8,128)S(1)}, f32[16,768]{1,0:T(8,128)S(1)}, u32[]{:S(2)}, u32[]{:S(2)}) collective-permute-start(f32[16,768]{1,0:T(8,128)S(1)} %add.313), channel_id=1, source_target_pairs={{0,2},{1,3},{2,0},{3,1},{4,6},{5,7},{6,4},{7,5},{8,10},{9,11},{10,... | collective-permute-start | bytes 147464 | tf_op jit(solution)/shard_map/ppermute | solution.py:112
  259.0 11.5 %collective-permute-start.44 = (bf16[4,24,3840]{2,1,0:T(8,128)(2,1)S(1)}, bf16[4,24,3840]{2,1,0:T(8,128)(2,1)S(1)}, u32[]{:S(2)}, u32[]{:S(2)}) collective-permute-start(bf16[4,24,3840]{2,1,0:T(8,128)(2,1)S(1)} %constant_dynamic-update-slice_fusion.10.refs_1_), channel_id=1, source_target_pairs={{0,4},{1,9},{2,6},{3,11},{4,0},{5,13},{6,2},{7,15},{8,12},{9,1},{1... | collective-permute-start | bytes 2211848 | tf_op jit(solution)/shard_map/ppermute | solution.py:112
  260.2 15.1 %collective-permute-start.41 = (bf16[4,24,2304]{2,1,0:T(8,128)(2,1)S(1)}, bf16[4,24,2304]{2,1,0:T(8,128)(2,1)S(1)}, u32[]{:S(2)}, u32[]{:S(2)}) collective-permute-start(bf16[4,24,2304]{2,1,0:T(8,128)(2,1)S(1)} %constant_dynamic-update-slice_fusion.6.refs_3_.refs_1_), channel_id=1, source_target_pairs={{0,4},{1,9},{2,6},{3,11},{4,0},{5,13},{6,2},{7,15},{8,12},{9,1},{1... | collective-permute-start | bytes 1327112 | tf_op jit(solution)/shard_map/ppermute | solution.py:112
  (104 other events, 817.3 us)

commit v3 on v1

--- a/solution.py
+++ b/solution.py
@@ -238,30 +238,21 @@
     qkv_ref[0, :, 2 * D :] = (dot(n1, w_ref[:, 2 * D :]) + vec_ref[5:6, :]).astype(BF16)
 
 
-def lane_slab(slab):
-    return pl.ds(pl.multiple_of(slab * LANES, LANES), LANES)
-
-
 def mix_kernel(qkv_ref, a_ref):
     low = lax.broadcasted_iota(jnp.int32, (1, LANES), 1) < HDIM
-
-    def some_slabs(turn, _):
-        for slab in [3 * turn + k for k in range(3)]:
-            cols = lane_slab(slab)
-            q = qkv_ref[0, :, cols] * jnp.asarray(HDIM**-0.5, BF16)
-            k = qkv_ref[0, :, lane_slab(slab + SLABS)]
-            v = qkv_ref[0, :, lane_slab(slab + 2 * SLABS)]
-            outs = []
-            for head in range(2):
-                mine = low if head == 0 else jnp.logical_not(low)
-                scores = dot_last(jnp.where(mine, q, jnp.zeros_like(q)), k)
-                e = jnp.exp(scores - jnp.max(scores, axis=-1, keepdims=True))
-                p = (e * (1.0 / jnp.sum(e, axis=-1, keepdims=True))).astype(BF16)
-                outs.append(dot(p, v))
-            a_ref[0, :, cols] = jnp.where(low, outs[0], outs[1]).astype(BF16)
-        return 0
-
-    lax.fori_loop(0, SLABS // 3, some_slabs, 0)
+    for slab in range(SLABS):
+        cols = slice(slab * LANES, (slab + 1) * LANES)
+        q = qkv_ref[0, :, cols] * jnp.asarray(HDIM**-0.5, BF16)
+        k = qkv_ref[0, :, D + slab * LANES : D + (slab + 1) * LANES]
+        v = qkv_ref[0, :, 2 * D + slab * LANES : 2 * D + (slab + 1) * LANES]
+        outs = []
+        for head in range(2):
+            mine = low if head == 0 else jnp.logical_not(low)
+            scores = dot_last(jnp.where(mine, q, jnp.zeros_like(q)), k)
+            e = jnp.exp(scores - jnp.max(scores, axis=-1, keepdims=True))
+            inverse = 1.0 / jnp.sum(e, axis=-1, keepdims=True)
+            outs.append(dot(e.astype(BF16), v) * inverse)
+        a_ref[0, :, cols] = jnp.where(low, outs[0], outs[1]).astype(BF16)
 
 
 def fc1_kernel(rows, place_ref, tok_ref, img_ref, a_ref, vec_ref, *refs):
@@ -422,14 +413,14 @@
         for head in range(2):
             mine = low if head == 0 else jnp.logical_not(low)
             zero = jnp.zeros_like(q)
-            scores = dot_last(jnp.where(mine, q, zero), k)
-            e = jnp.exp(scores - jnp.max(scores, axis=-1, keepdims=True))
-            p = e * (1.0 / jnp.sum(e, axis=-1, keepdims=True))
-            gvs.append(dot_first(p.astype(BF16), da))
-            dp = dot_last(jnp.where(mine, da, zero), v)
-            ds = (p * (dp - jnp.sum(p * dp, axis=-1, keepdims=True))).astype(BF16)
-            gqs.append(dot(ds, k))
-            gks.append(dot_first(ds, q))
+            scores = dot_last(k, jnp.where(mine, q, zero))
+            e = jnp.exp(scores - jnp.max(scores, axis=0, keepdims=True))
+            p = e * (1.0 / jnp.sum(e, axis=0, keepdims=True))
+            gvs.append(dot(p.astype(BF16), da))
+            dp = dot_last(v, jnp.where(mine, da, zero))
+            ds = (p * (dp - jnp.sum(p * dp, axis=0, keepdims=True))).astype(BF16)
+            gqs.append(dot_first(ds, k))
+            gks.append(dot(ds, q))
         gq = jnp.where(low, gqs[0], gqs[1]) * (HDIM**-0.5)
         gk = jnp.where(low, gks[0], gks[1])
         gv = jnp.where(low, gvs[0], gvs[1])
@@ -776,7 +767,9 @@
     )
 
     set_b = cast([w_out, w_fc1])
+    near_a = set_a[2]
     set_a = last_piece(spread_pieces(set_a, [set_b[0]] + vec_parts))
+    set_c = cast([w_fc2], [near_a])
 
     n1, qkv = call(
         functools.partial(qkv_kernel, rows_d),
@@ -792,9 +785,8 @@
         "qkv",
     )
 
-    set_c = cast([w_fc2])
     near_b = set_b[2]
-    set_b = spread_pieces(set_b, set_c[0])
+    set_b = spread_pieces(set_b, n1)
     (mixed,) = call(
         mix_kernel,
         (pairs,),

time: 249 us -> 244 us (0.980)
  Pallas kernels: 129 us -> 120 us
  local copies, waits for them, and re-layouts: 16.1 us -> 18.9 us
    pallas_call x19, Pallas kernels: 129 us -> 120 us  [__call__(): pl.pallas_call(body, grid_spec=pltpu.PrefetchScalarGridSpec(num_scalar_pr...]
  transfers between devices with their start and end apart: 47 -> 47, of which waited for: 17 -> 19; matrix products, arithmetic and copies ran while one was open for 8% -> 9% of each run, Pallas kernels for 51% -> 48%
where the time goes in v3:
time: 244 us; the launch traced here: 242 us
  Pallas kernels  120 us (49%)
  starting transfers between devices  42.2 us (17%)
  waiting for transfers between devices  39.5 us (16%)
  other arithmetic  19.9 us (8%)
  local copies, waits for them, and re-layouts  18.9 us (8%)
    pallas_call x19, Pallas kernels, __call__(): pl.pallas_call(body, grid_spec=pltpu.PrefetchScalarGridSpec(num_scalar_pr...  120 us
    ppermute x47, starting transfers between devices, exchange(): return lax.ppermute(value, ('batch', 'fsdp'), pairs)  42.2 us
    ppermute x47, waiting for transfers between devices, exchange(): return lax.ppermute(value, ('batch', 'fsdp'), pairs)  39.5 us
    unnamed x146, local copies, waits for them, and re-layouts  15.2 us
    convert_element_type x12, other arithmetic, add(): self.sent = self.call.hold(total.astype(BF16))  6.66 us
    convert_element_type x3, other arithmetic, finish(): news.append(new_w.astype(BF16))  5.67 us
  transfers between devices with their start and end apart: 47, of which 19 were waited for; matrix products, arithmetic and copies ran while one was open for 9% of the time, Pallas kernels for 48%

profile of v3, /device:TPU:0, one launch (start us, length us, event | category | flops | bytes accessed | tf_op | source)
XLA Modules:
  0.0 241.8 jit_solution(15499588512521890464)
XLA Ops:
  1.4 3.0 %collective-permute-start = (bf16[14,192]{1,0:T(8,128)(2,1)S(1)}, bf16[14,192]{1,0:T(8,128)(2,1)S(1)}, u32[]{:S(2)}, u32[]{:S(2)}) collective-permute-start(bf16[14,192]{1,0:T(8,128)(2,1)S(1)} %convert_element_type.251), channel_id=1, source_target_pairs={{0,2},{1,3},{2,0},{3,1},{4,6},{5,7},{6,4},{7,5},{8,10},{9,11},{10,... | collective-permute-start | bytes 16136 | tf_op jit(solution)/shard_map/ppermute | solution.py:112
  10.6 3.3 %order.1 = (bf16[4,256,256]{2,1,0:T(8,128)(2,1)S(1)}, bf16[4,256,768]{2,1,0:T(8,128)(2,1)S(1)}, bf16[4,256,128]{2,1,0:T(8,128)(2,1)S(1)}, bf16[4,128,768]{2,1,0:T(8,128)(2,1)S(1)}) custom-call(s32[4]{0:T(128)S(1)} %copy-done.36, s32[4,1,128]{2,1,0:T(1,128)S(1)} %bitcast.31, bf16[4,256,768]{2,1,0:T(8,128)(2,1)S(1)} %copy-done.20, ...), custom_call_target="tpu_custom_call" | custom-call | flops 17999998976 | bytes 60000000 | tf_op jit(solution)/shard_map/order/pallas_call | solution.py:579
  18.6 2.6 %collective-permute-done.4.refs_2_.refs_6_.refs_14_ = bf16[96,2304]{1,0:T(8,128)(2,1)S(1)} collective-permute-done((bf16[96,2304]{1,0:T(8,128)(2,1)S(1)}, bf16[96,2304]{1,0:T(8,128)(2,1)S(1)}, u32[]{:S(2)}, u32[]{:S(2)}) %collective-permute-start.4) | collective-permute-done | bytes 442400 | tf_op jit(solution)/shard_map/ppermute | solution.py:112
  23.3 6.3 %collective-permute-done.5.refs_7_.refs_15_ = bf16[96,2304]{1,0:T(8,128)(2,1)} collective-permute-done((bf16[96,2304]{1,0:T(8,128)(2,1)S(1)}, bf16[96,2304]{1,0:T(8,128)(2,1)}, u32[]{:S(2)}, u32[]{:S(2)}) %collective-permute-start.5) | collective-permute-done | bytes 442400 | tf_op jit(solution)/shard_map/ppermute | solution.py:112
  32.3 8.1 %qkv.1 = (bf16[4,256,768]{2,1,0:T(8,128)(2,1)S(1)}, bf16[4,256,2304]{2,1,0:T(8,128)(2,1)S(1)}) custom-call(s32[52]{0:T(128)S(1)} %get-tuple-element.296.refs_0_, bf16[4,256,768]{2,1,0:T(8,128)(2,1)S(1)} %copy-done.7, bf16[4,256,128]{2,1,0:T(8,128)(2,1)S(1)} %copy-done.16, f32[16,768]{1,0:T(8,128)S(1)} %fusion.12.refs_3_.refs_4_, ...), custom_call_target="tpu_custom_call" | custom-call | flops 300000000 | bytes 1000000 | tf_op jit(solution)/shard_map/qkv/pallas_call | solution.py:579
  42.6 6.0 %mix.1.refs_3_.refs_11_ = bf16[4,256,768]{2,1,0:T(8,128)(2,1)S(1)} custom-call(bf16[4,256,2304]{2,1,0:T(8,128)(2,1)S(1)} %get-tuple-element.154.refs_0_.refs_2_, bf16[96,3840]{1,0:T(8,128)(2,1)S(1)} %collective-permute-done.8.refs_1_.refs_7_, bf16[4,256,2304]{2,1,0:T(8,128)(2,1)S(1)} %get-tuple-element.154.refs_0_.refs_2_), custom_call_target="tpu_custom_call" | custom-call | flops 3000000000 | bytes 10000000 | tf_op jit(solution)/shard_map/mix/pallas_call | solution.py:579
  48.6 3.4 %collective-permute-done.10.refs_8_ = bf16[96,3840]{1,0:T(8,128)(2,1)S(1)} collective-permute-done((bf16[96,3840]{1,0:T(8,128)(2,1)S(1)}, bf16[96,3840]{1,0:T(8,128)(2,1)S(1)}, u32[]{:S(2)}, u32[]{:S(2)}) %collective-permute-start.10) | collective-permute-done | bytes 737312 | tf_op jit(solution)/shard_map/ppermute | solution.py:112
  54.3 13.1 %fc1.1 = (f32[4,256,768]{2,1,0:T(8,128)S(1)}, bf16[4,256,768]{2,1,0:T(8,128)(2,1)S(1)}, bf16[4,256,3072]{2,1,0:T(8,128)(2,1)S(1)}, bf16[4,128,3072]{2,1,0:T(8,128)(2,1)S(1)}) custom-call(s32[52]{0:T(128)S(1)} %get-tuple-element.296.refs_0_, bf16[4,256,768]{2,1,0:T(8,128)(2,1)S(1)} %copy-done.7, bf16[4,256,128]{2,1,0:T(8,128)(2,1)S(1)} %copy-done.16, ...), custom_call_target="tpu_custom_call" | custom-call | flops 54000001024 | bytes 180000000 | tf_op jit(solution)/shard_map/fc1/pallas_call | solution.py:579
  70.6 6.6 %gw2.1 = (bf16[16,96,768]{2,1,0:T(8,128)(2,1)S(1)}, bf16[16,96,768]{2,1,0:T(8,128)(2,1)}, f32[1,768]{1,0:T(1,128)S(1)}) custom-call(s32[52]{0:T(128)S(1)} %get-tuple-element.296.refs_0_, bf16[4,256,3072]{2,1,0:T(8,128)(2,1)S(1)} %get-tuple-element.158.refs_1_, bf16[4,128,768]{2,1,0:T(8,128)(2,1)S(1)} %copy-done.12, ...), custom_call_target="tpu_custom_call" | custom-call | flops 24000000000 | bytes 80000000 | tf_op jit(solution)/shard_map/gw2/pallas_call | solution.py:579
  85.8 7.2 %df.1 = (bf16[512,3072]{1,0:T(8,128)(2,1)S(1)}, f32[1,3072]{1,0:T(1,128)S(1)}) custom-call(s32[52]{0:T(128)S(1)} %get-tuple-element.296.refs_0_, bf16[4,128,768]{2,1,0:T(8,128)(2,1)S(1)} %copy-done.13, bf16[4,128,3072]{2,1,0:T(8,128)(2,1)S(1)} %copy-done.41, bf16[768,768]{1,0:T(8,128)(2,1)} %get-tuple-element.161.refs_3_.refs_5_, ...), custom_call_target="tpu_custom_call" | custom-call | flops 20999999488 | bytes 70000000 | tf_op jit(solution)/shard_map/df/pallas_call | solution.py:579
  96.3 6.7 %mlp_back.1 = (f32[4,128,768]{2,1,0:T(8,128)S(1)}, bf16[4,128,768]{2,1,0:T(8,128)(2,1)S(1)}, bf16[4,128,768]{2,1,0:T(8,128)(2,1)S(1)}, f32[8,768]{1,0:T(8,128)S(1)}) custom-call(s32[52]{0:T(128)S(1)} %get-tuple-element.296.refs_0_, bf16[512,3072]{1,0:T(8,128)(2,1)S(1)} %get-tuple-element.167.refs_1_.refs_2_, bf16[4,128,768]{2,1,0:T(8,128)(2,1)S(1)} %copy-done.13, ...), custom_call_target="tpu_custom_call" | custom-call | flops 30000001024 | bytes 100000000 | tf_op jit(solution)/shard_map/mlp_back/pallas_call | solution.py:579
  103.1 6.9 %gw1o.1 = (bf16[16,24,3840]{2,1,0:T(8,128)(2,1)S(1)}, bf16[16,24,3840]{2,1,0:T(8,128)(2,1)S(1)}) custom-call(s32[52]{0:T(128)S(1)} %get-tuple-element.296.refs_0_, bf16[4,256,768]{2,1,0:T(8,128)(2,1)S(1)} %copy-done.46, bf16[512,3072]{1,0:T(8,128)(2,1)S(1)} %get-tuple-element.167.refs_1_.refs_2_, bf16[4,256,768]{2,1,0:T(8,128)(2,1)S(1)} %copy-done.10, ...), custom_call_target="tpu_custom_call" | custom-call | flops 27000000512 | bytes 90000000 | tf_op jit(solution)/shard_map/gw1o/pallas_call | solution.py:579
  113.9 9.1 %attn_back.2 = (bf16[4,128,768]{2,1,0:T(8,128)(2,1)S(1)}, bf16[4,256,1536]{2,1,0:T(8,128)(2,1)S(1)}, f32[8,768]{1,0:T(8,128)S(1)}) custom-call(bf16[4,256,2304]{2,1,0:T(8,128)(2,1)S(1)} %bitcast.30, bf16[4,128,768]{2,1,0:T(8,128)(2,1)S(1)} %get-tuple-element.173.refs_1_, bf16[4,96,768]{2,1,0:T(8,128)(2,1)S(1)} %add_convert_fusion.4.refs_2_, ...), custom_call_target="tpu_custom_call" | custom-call | flops 35999997952 | bytes 120000000 | tf_op jit(solution)/shard_map/attn_back/pallas_call | solution.py:579
  124.1 2.9 %collective-permute-start.22 = (bf16[2,96,768]{2,1,0:T(8,128)(2,1)S(1)}, bf16[2,96,768]{2,1,0:T(8,128)(2,1)S(1)}, u32[]{:S(2)}, u32[]{:S(2)}) collective-permute-start(bf16[2,96,768]{2,1,0:T(8,128)(2,1)S(1)} %add_convert_fusion.7.refs_6_), channel_id=1, source_target_pairs={{0,24},{1,3},{2,26},{3,1},{4,28},{5,7},{6,30},{7,5},{8,16},{9,11},... | collective-permute-start | bytes 884744 | tf_op jit(solution)/shard_map/ppermute | solution.py:112
  128.9 9.1 %attn_back.3 = (bf16[4,128,768]{2,1,0:T(8,128)(2,1)S(1)}, bf16[4,256,1536]{2,1,0:T(8,128)(2,1)S(1)}, f32[8,768]{1,0:T(8,128)S(1)}) custom-call(bf16[4,256,2304]{2,1,0:T(8,128)(2,1)S(1)} %bitcast.30, bf16[4,128,768]{2,1,0:T(8,128)(2,1)S(1)} %get-tuple-element.173.refs_1_, ...), custom_call_target="tpu_custom_call", output_to_operand_aliasing={{0}: (2, {}), {1}: (3, {})} | custom-call | flops 35999997952 | bytes 120000000 | tf_op jit(solution)/shard_map/attn_back/pallas_call | solution.py:579
  139.1 6.3 %gqkv.1 = (bf16[16,24,2304]{2,1,0:T(8,128)(2,1)S(1)}, bf16[16,24,2304]{2,1,0:T(8,128)(2,1)S(1)}) custom-call(s32[52]{0:T(128)S(1)} %get-tuple-element.296.refs_0_, bf16[4,256,768]{2,1,0:T(8,128)(2,1)S(1)} %copy-done.23, bf16[4,128,768]{2,1,0:T(8,128)(2,1)S(1)} %get-tuple-element.190.refs_2_.refs_4_, ...), custom_call_target="tpu_custom_call" | custom-call | flops 27000000512 | bytes 90000000 | tf_op jit(solution)/shard_map/gqkv/pallas_call | solution.py:579
  150.9 2.0 subtract_convert_fusion.1
  154.0 12.0 %grad_in.1 = (f32[4,256,768]{2,1,0:T(8,128)}, f32[16,768]{1,0:T(8,128)S(1)}) custom-call(s32[52]{0:T(128)S(1)} %get-tuple-element.296.refs_0_, bf16[4,256,768]{2,1,0:T(8,128)(2,1)S(1)} %copy-done.8, bf16[4,256,128]{2,1,0:T(8,128)(2,1)S(1)} %copy-done.17, f32[16,768]{1,0:T(8,128)S(1)} %copy-done.19, ...), custom_call_target="tpu_custom_call" | custom-call | flops 44999999488 | bytes 150000000 | tf_op jit(solution)/shard_map/grad_in/pallas_call | solution.py:579
  169.2 2.5 %collective-permute-start.35 = (bf16[2,24,3840]{2,1,0:T(8,128)(2,1)S(1)}, bf16[2,24,3840]{2,1,0:T(8,128)(2,1)S(1)}, u32[]{:S(2)}, u32[]{:S(2)}) collective-permute-start(bf16[2,24,3840]{2,1,0:T(8,128)(2,1)S(1)} %add_convert_fusion.6.refs_12_), channel_id=1, source_target_pairs={{0,24},{1,3},{2,26},{3,1},{4,28},{5,7},{6,30},{7,5},{8,16},{9,11},... | collective-permute-start | bytes 1105928 | tf_op jit(solution)/shard_map/ppermute | solution.py:112
  173.1 10.6 %out.1 = bf16[4,256,768]{2,1,0:T(8,128)(2,1)} custom-call(s32[52]{0:T(128)S(1)} %get-tuple-element.296.refs_0_, bf16[4,256,3072]{2,1,0:T(8,128)(2,1)S(1)} %bitcast.33, f32[4,256,768]{2,1,0:T(8,128)S(1)} %copy-done.44, f32[16,768]{1,0:T(8,128)S(1)} %copy-done.19, bf16[4,256,256]{2,1,0:T(8,128)(2,1)S(1)} %copy-done.48, ...), custom_call_target="tpu_custom_call" | custom-call | flops 38999998464 | bytes 130000000 | tf_op jit(solution)/shard_map/out/pallas_call | solution.py:579
  191.3 2.0 subtract_convert_fusion
  193.3 2.0 collective-permute-start.37
  195.3 2.0 collective-permute-start.44
  199.3 3.4 %collective-permute-done.37 = bf16[1,24,3840]{2,1,0:T(8,128)(2,1)S(1)} collective-permute-done((bf16[1,24,3840]{2,1,0:T(8,128)(2,1)S(1)}, bf16[1,24,3840]{2,1,0:T(8,128)(2,1)S(1)}, u32[]{:S(2)}, u32[]{:S(2)}) %collective-permute-start.37) | collective-permute-done | bytes 184352 | tf_op jit(solution)/shard_map/ppermute | solution.py:112
  205.5 1.9 fusion.3
  209.7 4.5 %collective-permute-done.32 = bf16[1,24,2304]{2,1,0:T(8,128)(2,1)S(1)} collective-permute-done((bf16[1,24,2304]{2,1,0:T(8,128)(2,1)S(1)}, bf16[1,24,2304]{2,1,0:T(8,128)(2,1)S(1)}, u32[]{:S(2)}, u32[]{:S(2)}) %collective-permute-start.32) | collective-permute-done | bytes 110624 | tf_op jit(solution)/shard_map/ppermute | solution.py:112
  215.0 2.7 %collective-permute-done.38 = bf16[2,24,3840]{2,1,0:T(8,128)(2,1)S(1)} collective-permute-done((bf16[2,24,3840]{2,1,0:T(8,128)(2,1)S(1)}, bf16[2,24,3840]{2,1,0:T(8,128)(2,1)S(1)}, u32[]{:S(2)}, u32[]{:S(2)}) %collective-permute-start.38) | collective-permute-done | bytes 368672 | tf_op jit(solution)/shard_map/ppermute | solution.py:112
  218.5 2.8 %collective-permute-done.33 = bf16[2,24,2304]{2,1,0:T(8,128)(2,1)S(1)} collective-permute-done((bf16[2,24,2304]{2,1,0:T(8,128)(2,1)S(1)}, bf16[2,24,2304]{2,1,0:T(8,128)(2,1)S(1)}, u32[]{:S(2)}, u32[]{:S(2)}) %collective-permute-start.33) | collective-permute-done | bytes 221216 | tf_op jit(solution)/shard_map/ppermute | solution.py:112
  223.3 2.6 %place.3.refs_3_ = f32[768,768]{1,0:T(8,128)} custom-call(s32[52]{0:T(128)S(1)} %get-tuple-element.296.refs_0_, bf16[4,104,768]{2,1,0:T(8,128)(2,1)S(1)} %constant_dynamic-update-slice_fusion.10.refs_1_, bf16[4,104,768]{2,1,0:T(8,128)(2,1)S(1)} %collective-permute-done.41.refs_2_, bf16[4,24,2304]{2,1,0:T(8,128)(2,1)S(1)} %constant_dynamic-update-slice_fusion.4.refs_3_.refs_1_), custom_call_target="tpu_custom_call" | custom-call | flops 3000000000 | bytes 10000000 | tf_op jit(solution)/shard_map/place/pallas_call | solution.py:579
  227.3 4.7 %collective-permute-done.39.refs_2_ = bf16[4,24,3840]{2,1,0:T(8,128)(2,1)S(1)} collective-permute-done((bf16[4,24,3840]{2,1,0:T(8,128)(2,1)S(1)}, bf16[4,24,3840]{2,1,0:T(8,128)(2,1)S(1)}, u32[]{:S(2)}, u32[]{:S(2)}) %collective-permute-start.39) | collective-permute-done | bytes 737312 | tf_op jit(solution)/shard_map/ppermute | solution.py:112
  233.7 3.5 %place.4 = (f32[192,3072]{1,0:T(8,128)}, f32[192,768]{1,0:T(8,128)}) custom-call(s32[52]{0:T(128)S(1)} %get-tuple-element.296.refs_0_, bf16[4,24,3840]{2,1,0:T(8,128)(2,1)S(1)} %constant_dynamic-update-slice_fusion.8.refs_1_, bf16[4,24,3840]{2,1,0:T(8,128)(2,1)S(1)} %collective-permute-done.39.refs_2_, f32[768,768]{1,0:T(8,128)S(1)} %copy-done.37), custom_call_target="tpu_custom_call" | custom-call | flops 3000000000 | bytes 10000000 | tf_op jit(solution)/shard_map/place/pallas_call | solution.py:579
  238.2 3.5 %place.5 = f32[192,2304]{1,0:T(8,128)} custom-call(s32[52]{0:T(128)S(1)} %get-tuple-element.296.refs_0_, bf16[4,24,2304]{2,1,0:T(8,128)(2,1)S(1)} %constant_dynamic-update-slice_fusion.4.refs_3_.refs_1_, bf16[4,24,2304]{2,1,0:T(8,128)(2,1)} %collective-permute-done.34.refs_2_, f32[192,768]{1,0:T(8,128)S(1)} %copy-done.38), custom_call_target="tpu_custom_call" | custom-call | flops 3000000000 | bytes 10000000 | tf_op jit(solution)/shard_map/place/pallas_call | solution.py:579
  (283 shorter events, 76.8 us)
Async XLA Ops:
  1.4 14.3 %collective-permute-start = (bf16[14,192]{1,0:T(8,128)(2,1)S(1)}, bf16[14,192]{1,0:T(8,128)(2,1)S(1)}, u32[]{:S(2)}, u32[]{:S(2)}) collective-permute-start(bf16[14,192]{1,0:T(8,128)(2,1)S(1)} %convert_element_type.251), channel_id=1, source_target_pairs={{0,2},{1,3},{2,0},{3,1},{4,6},{5,7},{6,4},{7,5},{8,10},{9,11},{10,... | collective-permute-start | bytes 16136 | tf_op jit(solution)/shard_map/ppermute | solution.py:112
  4.4 14.2 %collective-permute-start.2 = (bf16[14,192]{1,0:T(8,128)(2,1)S(1)}, bf16[14,192]{1,0:T(8,128)(2,1)S(1)}, u32[]{:S(2)}, u32[]{:S(2)}) collective-permute-start(bf16[14,192]{1,0:T(8,128)(2,1)S(1)} %convert_element_type.251), channel_id=1, source_target_pairs={{0,1},{1,0},{2,3},{3,2},{4,5},{5,4},{6,7},{7,6},{8,9},{9,8},{10,11... | collective-permute-start | bytes 16136 | tf_op jit(solution)/shard_map/ppermute | solution.py:112
  8.6 23.7 %collective-permute-start.3 = (bf16[192,2304]{1,0:T(8,128)(2,1)}, bf16[192,2304]{1,0:T(8,128)(2,1)}, u32[]{:S(2)}, u32[]{:S(2)}) collective-permute-start(bf16[192,2304]{1,0:T(8,128)(2,1)} %get-tuple-element.148.refs_4_.refs_12_), channel_id=1, source_target_pairs={{0,1},{1,0},{2,3},{3,2},{4,5},{5,4},{6,7},{7,6},{8,9},{9,8},{10,11... | collective-permute-start | bytes 2654216 | tf_op jit(solution)/shard_map/ppermute | solution.py:112
  9.1 12.1 %collective-permute-start.4 = (bf16[96,2304]{1,0:T(8,128)(2,1)S(1)}, bf16[96,2304]{1,0:T(8,128)(2,1)S(1)}, u32[]{:S(2)}, u32[]{:S(2)}) collective-permute-start(bf16[96,2304]{1,0:T(8,128)(2,1)S(1)} %get-tuple-element.145.refs_4_), channel_id=1, source_target_pairs={{0,2},{1,3},{2,0},{3,1},{4,6},{5,7},{6,4},{7,5},{8,10},{9,11},{10,... | collective-permute-start | bytes 1327112 | tf_op jit(solution)/shard_map/ppermute | solution.py:112
  22.8 17.8 %collective-permute-start.8 = (bf16[96,3840]{1,0:T(8,128)(2,1)}, bf16[96,3840]{1,0:T(8,128)(2,1)S(1)}, u32[]{:S(2)}, u32[]{:S(2)}) collective-permute-start(bf16[96,3840]{1,0:T(8,128)(2,1)} %get-tuple-element.152.refs_3_), channel_id=1, source_target_pairs={{0,2},{1,3},{2,0},{3,1},{4,6},{5,7},{6,4},{7,5},{8,10},{9,11},{10,... | collective-permute-start | bytes 2211848 | tf_op jit(solution)/shard_map/ppermute | solution.py:112
  23.3 9.0 %collective-permute-start.6 = (bf16[96,2304]{1,0:T(8,128)(2,1)S(1)}, bf16[96,2304]{1,0:T(8,128)(2,1)}, u32[]{:S(2)}, u32[]{:S(2)}) collective-permute-start(bf16[96,2304]{1,0:T(8,128)(2,1)S(1)} %collective-permute-done.4.refs_2_.refs_6_.refs_14_), channel_id=1, source_target_pairs={{0,1},{1,0},{2,3},{3,2},{4,5},{5,4},{6,7},{7,6},{8,9},{9,8},{10,11... | collective-permute-start | bytes 1327112 | tf_op jit(solution)/shard_map/ppermute | solution.py:112
  40.5 11.5 %collective-permute-start.10 = (bf16[96,3840]{1,0:T(8,128)(2,1)S(1)}, bf16[96,3840]{1,0:T(8,128)(2,1)S(1)}, u32[]{:S(2)}, u32[]{:S(2)}) collective-permute-start(bf16[96,3840]{1,0:T(8,128)(2,1)S(1)} %collective-permute-done.8.refs_1_.refs_7_), channel_id=1, source_target_pairs={{0,4},{1,9},{2,6},{3,11},{4,0},{5,13},{6,2},{7,15},{8,12},{9,1},{1... | collective-permute-start | bytes 2211848 | tf_op jit(solution)/shard_map/ppermute | solution.py:112
  42.1 10.7 %collective-permute-start.9 = (bf16[192,3840]{1,0:T(8,128)(2,1)S(1)}, bf16[192,3840]{1,0:T(8,128)(2,1)S(1)}, u32[]{:S(2)}, u32[]{:S(2)}) collective-permute-start(bf16[192,3840]{1,0:T(8,128)(2,1)S(1)} %copy-done.25), channel_id=1, source_target_pairs={{0,1},{1,0},{2,3},{3,2},{4,5},{5,4},{6,7},{7,6},{8,9},{9,8},{10,11... | collective-permute-start | bytes 4423688 | tf_op jit(solution)/shard_map/ppermute | solution.py:112
  42.4 10.4 %collective-permute-start.11 = (bf16[96,3840]{1,0:T(8,128)(2,1)S(1)}, bf16[96,3840]{1,0:T(8,128)(2,1)S(1)}, u32[]{:S(2)}, u32[]{:S(2)}) collective-permute-start(bf16[96,3840]{1,0:T(8,128)(2,1)S(1)} %collective-permute-done.8.refs_1_.refs_7_), channel_id=1, source_target_pairs={{0,1},{1,0},{2,3},{3,2},{4,5},{5,4},{6,7},{7,6},{8,9},{9,8},{10,11... | collective-permute-start | bytes 2211848 | tf_op jit(solution)/shard_map/ppermute | solution.py:112
  52.1 17.0 %collective-permute-start.14 = (bf16[384,768]{1,0:T(8,128)(2,1)S(1)}, bf16[384,768]{1,0:T(8,128)(2,1)}, u32[]{:S(2)}, u32[]{:S(2)}) collective-permute-start(bf16[384,768]{1,0:T(8,128)(2,1)S(1)} %get-tuple-element.153.refs_10_), channel_id=1, source_target_pairs={{0,2},{1,3},{2,0},{3,1},{4,6},{5,7},{6,4},{7,5},{8,10},{9,11},{10,... | collective-permute-start | bytes 1769480 | tf_op jit(solution)/shard_map/ppermute | solution.py:112
  52.6 30.0 %collective-permute-start.13 = (bf16[768,768]{1,0:T(8,128)(2,1)}, bf16[768,768]{1,0:T(8,128)(2,1)}, u32[]{:S(2)}, u32[]{:S(2)}) collective-permute-start(bf16[768,768]{1,0:T(8,128)(2,1)} %get-tuple-element.161.refs_3_.refs_5_), channel_id=1, source_target_pairs={{0,1},{1,0},{2,3},{3,2},{4,5},{5,4},{6,7},{7,6},{8,9},{9,8},{10,11... | collective-permute-start | bytes 3538952 | tf_op jit(solution)/shard_map/ppermute | solution.py:112
  69.1 10.3 %collective-permute-start.15 = (bf16[384,768]{1,0:T(8,128)(2,1)}, bf16[384,768]{1,0:T(8,128)(2,1)}, u32[]{:S(2)}, u32[]{:S(2)}) collective-permute-start(bf16[384,768]{1,0:T(8,128)(2,1)} %collective-permute-done.14.refs_5_.refs_7_), channel_id=1, source_target_pairs={{0,4},{1,9},{2,6},{3,11},{4,0},{5,13},{6,2},{7,15},{8,12},{9,1},{1... | collective-permute-start | bytes 1769480 | tf_op jit(solution)/shard_map/ppermute | solution.py:112
  70.6 11.9 %collective-permute-start.16 = (bf16[384,768]{1,0:T(8,128)(2,1)}, bf16[384,768]{1,0:T(8,128)(2,1)}, u32[]{:S(2)}, u32[]{:S(2)}) collective-permute-start(bf16[384,768]{1,0:T(8,128)(2,1)} %collective-permute-done.14.refs_5_.refs_7_), channel_id=1, source_target_pairs={{0,1},{1,0},{2,3},{3,2},{4,5},{5,4},{6,7},{7,6},{8,9},{9,8},{10,11... | collective-permute-start | bytes 1769480 | tf_op jit(solution)/shard_map/ppermute | solution.py:112
  79.3 13.6 %collective-permute-start.18 = (bf16[16,96,768]{2,1,0:T(8,128)(2,1)}, bf16[16,96,768]{2,1,0:T(8,128)(2,1)}, u32[]{:S(2)}, u32[]{:S(2)}) collective-permute-start(bf16[16,96,768]{2,1,0:T(8,128)(2,1)} %get-tuple-element.169), channel_id=1, source_target_pairs={{0,1},{1,0},{2,3},{3,2},{4,5},{5,4},{6,7},{7,6},{8,9},{9,8},{10,11... | collective-permute-start | bytes 7077896 | tf_op jit(solution)/shard_map/ppermute | solution.py:112
  94.7 16.3 %collective-permute-start.19 = (bf16[8,96,768]{2,1,0:T(8,128)(2,1)S(1)}, bf16[8,96,768]{2,1,0:T(8,128)(2,1)S(1)}, u32[]{:S(2)}, u32[]{:S(2)}) collective-permute-start(bf16[8,96,768]{2,1,0:T(8,128)(2,1)S(1)} %add_convert_fusion.1.refs_11_), channel_id=1, source_target_pairs={{0,4},{1,9},{2,6},{3,11},{4,0},{5,13},{6,2},{7,15},{8,12},{9,1},{1... | collective-permute-start | bytes 3538952 | tf_op jit(solution)/shard_map/ppermute | solution.py:112
  110.0 17.0 %collective-permute-start.20 = (bf16[16,24,3840]{2,1,0:T(8,128)(2,1)S(1)}, bf16[16,24,3840]{2,1,0:T(8,128)(2,1)S(1)}, u32[]{:S(2)}, u32[]{:S(2)}) collective-permute-start(bf16[16,24,3840]{2,1,0:T(8,128)(2,1)S(1)} %get-tuple-element.176.refs_3_), channel_id=1, source_target_pairs={{0,1},{1,0},{2,3},{3,2},{4,5},{5,4},{6,7},{7,6},{8,9},{9,8},{10,11... | collective-permute-start | bytes 8847368 | tf_op jit(solution)/shard_map/ppermute | solution.py:112
  112.3 10.8 %collective-permute-start.21 = (bf16[4,96,768]{2,1,0:T(8,128)(2,1)S(1)}, bf16[4,96,768]{2,1,0:T(8,128)(2,1)S(1)}, u32[]{:S(2)}, u32[]{:S(2)}) collective-permute-start(bf16[4,96,768]{2,1,0:T(8,128)(2,1)S(1)} %add_convert_fusion.4.refs_2_), channel_id=1, source_target_pairs={{0,8},{1,5},{2,10},{3,7},{4,12},{5,1},{6,14},{7,3},{8,0},{9,13},{1... | collective-permute-start | bytes 1769480 | tf_op jit(solution)/shard_map/ppermute | solution.py:112
  124.1 13.9 %collective-permute-start.22 = (bf16[2,96,768]{2,1,0:T(8,128)(2,1)S(1)}, bf16[2,96,768]{2,1,0:T(8,128)(2,1)S(1)}, u32[]{:S(2)}, u32[]{:S(2)}) collective-permute-start(bf16[2,96,768]{2,1,0:T(8,128)(2,1)S(1)} %add_convert_fusion.7.refs_6_), channel_id=1, source_target_pairs={{0,24},{1,3},{2,26},{3,1},{4,28},{5,7},{6,30},{7,5},{8,16},{9,11},... | collective-permute-start | bytes 884744 | tf_op jit(solution)/shard_map/ppermute | solution.py:112
  127.4 19.4 %collective-permute-start.25 = (bf16[8,24,3840]{2,1,0:T(8,128)(2,1)S(1)}, bf16[8,24,3840]{2,1,0:T(8,128)(2,1)S(1)}, u32[]{:S(2)}, u32[]{:S(2)}) collective-permute-start(bf16[8,24,3840]{2,1,0:T(8,128)(2,1)S(1)} %add_convert_fusion.refs_5_), channel_id=1, source_target_pairs={{0,4},{1,9},{2,6},{3,11},{4,0},{5,13},{6,2},{7,15},{8,12},{9,1},{1... | collective-permute-start | bytes 4423688 | tf_op jit(solution)/shard_map/ppermute | solution.py:112
  147.1 21.9 %collective-permute-start.27 = (bf16[4,24,3840]{2,1,0:T(8,128)(2,1)S(1)}, bf16[4,24,3840]{2,1,0:T(8,128)(2,1)S(1)}, u32[]{:S(2)}, u32[]{:S(2)}) collective-permute-start(bf16[4,24,3840]{2,1,0:T(8,128)(2,1)S(1)} %add_convert_fusion.3.refs_18_), channel_id=1, source_target_pairs={{0,8},{1,5},{2,10},{3,7},{4,12},{5,1},{6,14},{7,3},{8,0},{9,13},{1... | collective-permute-start | bytes 2211848 | tf_op jit(solution)/shard_map/ppermute | solution.py:112
  149.4 22.4 %collective-permute-start.24 = (bf16[8,24,2304]{2,1,0:T(8,128)(2,1)S(1)}, bf16[8,24,2304]{2,1,0:T(8,128)(2,1)S(1)}, u32[]{:S(2)}, u32[]{:S(2)}) collective-permute-start(bf16[8,24,2304]{2,1,0:T(8,128)(2,1)S(1)} %add_convert_fusion.2.refs_19_), channel_id=1, source_target_pairs={{0,4},{1,9},{2,6},{3,11},{4,0},{5,13},{6,2},{7,15},{8,12},{9,1},{1... | collective-permute-start | bytes 2654216 | tf_op jit(solution)/shard_map/ppermute | solution.py:112
  152.9 15.6 %collective-permute-start.28 = (bf16[1,104,768]{2,1,0:T(8,128)(2,1)S(1)}, bf16[1,104,768]{2,1,0:T(8,128)(2,1)S(1)}, u32[]{:S(2)}, u32[]{:S(2)}) collective-permute-start(bf16[1,104,768]{2,1,0:T(8,128)(2,1)S(1)} %maximum_bitcast_fusion.1.refs_20_), channel_id=1, source_target_pairs={{0,24},{1,25},{2,26},{3,27},{4,28},{5,29},{6,30},{7,31},{8,16},{9,... | collective-permute-start | bytes 479240 | tf_op jit(solution)/shard_map/ppermute | solution.py:112
  166.0 20.3 %collective-permute-start.42 = (f32[16,768]{1,0:T(8,128)S(1)}, f32[16,768]{1,0:T(8,128)S(1)}, u32[]{:S(2)}, u32[]{:S(2)}) collective-permute-start(f32[16,768]{1,0:T(8,128)S(1)} %get-tuple-element.263.refs_14_), channel_id=1, source_target_pairs={{0,1},{1,0},{2,3},{3,2},{4,5},{5,4},{6,7},{7,6},{8,9},{9,8},{10,11... | collective-permute-start | bytes 147464 | tf_op jit(solution)/shard_map/ppermute | solution.py:112
  168.6 16.0 %collective-permute-start.40 = (bf16[2,104,768]{2,1,0:T(8,128)(2,1)S(1)}, bf16[2,104,768]{2,1,0:T(8,128)(2,1)S(1)}, u32[]{:S(2)}, u32[]{:S(2)}) collective-permute-start(bf16[2,104,768]{2,1,0:T(8,128)(2,1)S(1)} %constant_dynamic-update-slice_fusion.refs_13_), channel_id=1, source_target_pairs={{0,8},{1,5},{2,10},{3,7},{4,12},{5,1},{6,14},{7,3},{8,0},{9,13},{1... | collective-permute-start | bytes 958472 | tf_op jit(solution)/shard_map/ppermute | solution.py:112
  169.2 14.5 %collective-permute-start.35 = (bf16[2,24,3840]{2,1,0:T(8,128)(2,1)S(1)}, bf16[2,24,3840]{2,1,0:T(8,128)(2,1)S(1)}, u32[]{:S(2)}, u32[]{:S(2)}) collective-permute-start(bf16[2,24,3840]{2,1,0:T(8,128)(2,1)S(1)} %add_convert_fusion.6.refs_12_), channel_id=1, source_target_pairs={{0,24},{1,3},{2,26},{3,1},{4,28},{5,7},{6,30},{7,5},{8,16},{9,11},... | collective-permute-start | bytes 1105928 | tf_op jit(solution)/shard_map/ppermute | solution.py:112
  171.9 15.4 %collective-permute-start.29 = (bf16[4,24,2304]{2,1,0:T(8,128)(2,1)S(1)}, bf16[4,24,2304]{2,1,0:T(8,128)(2,1)S(1)}, u32[]{:S(2)}, u32[]{:S(2)}) collective-permute-start(bf16[4,24,2304]{2,1,0:T(8,128)(2,1)S(1)} %add_convert_fusion.5.refs_11_), channel_id=1, source_target_pairs={{0,8},{1,5},{2,10},{3,7},{4,12},{5,1},{6,14},{7,3},{8,0},{9,13},{1... | collective-permute-start | bytes 1327112 | tf_op jit(solution)/shard_map/ppermute | solution.py:112
  184.7 37.3 %collective-permute-start.41 = (bf16[4,104,768]{2,1,0:T(8,128)(2,1)S(1)}, bf16[4,104,768]{2,1,0:T(8,128)(2,1)S(1)}, u32[]{:S(2)}, u32[]{:S(2)}) collective-permute-start(bf16[4,104,768]{2,1,0:T(8,128)(2,1)S(1)} %constant_dynamic-update-slice_fusion.10.refs_1_), channel_id=1, source_target_pairs={{0,4},{1,9},{2,6},{3,11},{4,0},{5,13},{6,2},{7,15},{8,12},{9,1},{1... | collective-permute-start | bytes 1916936 | tf_op jit(solution)/shard_map/ppermute | solution.py:112
  186.4 8.9 %collective-permute-start.43 = (f32[16,768]{1,0:T(8,128)S(1)}, f32[16,768]{1,0:T(8,128)S(1)}, u32[]{:S(2)}, u32[]{:S(2)}) collective-permute-start(f32[16,768]{1,0:T(8,128)S(1)} %add.346), channel_id=1, source_target_pairs={{0,8},{1,9},{2,10},{3,11},{4,12},{5,13},{6,14},{7,15},{8,0},{9,1},... | collective-permute-start | bytes 147464 | tf_op jit(solution)/shard_map/ppermute | solution.py:112
  187.5 10.2 %collective-permute-start.30 = (bf16[2,24,2304]{2,1,0:T(8,128)(2,1)S(1)}, bf16[2,24,2304]{2,1,0:T(8,128)(2,1)S(1)}, u32[]{:S(2)}, u32[]{:S(2)}) collective-permute-start(bf16[2,24,2304]{2,1,0:T(8,128)(2,1)S(1)} %add_convert_fusion.8), channel_id=1, source_target_pairs={{0,24},{1,3},{2,26},{3,1},{4,28},{5,7},{6,30},{7,5},{8,16},{9,11},... | collective-permute-start | bytes 663560 | tf_op jit(solution)/shard_map/ppermute | solution.py:112
  193.3 9.4 %collective-permute-start.37 = (bf16[1,24,3840]{2,1,0:T(8,128)(2,1)S(1)}, bf16[1,24,3840]{2,1,0:T(8,128)(2,1)S(1)}, u32[]{:S(2)}, u32[]{:S(2)}) collective-permute-start(bf16[1,24,3840]{2,1,0:T(8,128)(2,1)S(1)} %maximum_bitcast_fusion), channel_id=1, source_target_pairs={{0,24},{1,25},{2,26},{3,27},{4,28},{5,29},{6,30},{7,31},{8,16},{9,... | collective-permute-start | bytes 552968 | tf_op jit(solution)/shard_map/ppermute | solution.py:112
  217.8 14.3 %collective-permute-start.39 = (bf16[4,24,3840]{2,1,0:T(8,128)(2,1)S(1)}, bf16[4,24,3840]{2,1,0:T(8,128)(2,1)S(1)}, u32[]{:S(2)}, u32[]{:S(2)}) collective-permute-start(bf16[4,24,3840]{2,1,0:T(8,128)(2,1)S(1)} %constant_dynamic-update-slice_fusion.8.refs_1_), channel_id=1, source_target_pairs={{0,4},{1,9},{2,6},{3,11},{4,0},{5,13},{6,2},{7,15},{8,12},{9,1},{1... | collective-permute-start | bytes 2211848 | tf_op jit(solution)/shard_map/ppermute | solution.py:112
  221.4 15.8 %collective-permute-start.34 = (bf16[4,24,2304]{2,1,0:T(8,128)(2,1)S(1)}, bf16[4,24,2304]{2,1,0:T(8,128)(2,1)}, u32[]{:S(2)}, u32[]{:S(2)}) collective-permute-start(bf16[4,24,2304]{2,1,0:T(8,128)(2,1)S(1)} %constant_dynamic-update-slice_fusion.4.refs_3_.refs_1_), channel_id=1, source_target_pairs={{0,4},{1,9},{2,6},{3,11},{4,0},{5,13},{6,2},{7,15},{8,12},{9,1},{1... | collective-permute-start | bytes 1327112 | tf_op jit(solution)/shard_map/ppermute | solution.py:112
  (85 other events, 623.5 us)

commit v4 on v3

--- a/solution.py
+++ b/solution.py
@@ -769,6 +769,12 @@
     set_b = cast([w_out, w_fc1])
     near_a = set_a[2]
     set_a = last_piece(spread_pieces(set_a, [set_b[0]] + vec_parts))
+    held = jnp.concatenate([m_vec, v_vec], axis=0).reshape(-1)
+    held = jnp.pad(held, (0, -held.size % 8)).reshape(8, -1)
+    riders = jnp.concatenate(split_two(held), axis=1)
+    rider_cols = riders.shape[1]
+    riders = jnp.pad(riders, ((0, 0), (0, D - rider_cols)))
+    call.hold(riders)
     set_c = cast([w_fc2], [near_a])
 
     n1, qkv = call(
@@ -971,12 +977,6 @@
     fallback = (D // nd) % 8 != 0 or (FF // nd) % 8 != 0
     places = OWN + nd
     order = tab[places + nb :]
-
-    held = jnp.concatenate([m_vec, v_vec], axis=0).reshape(-1)
-    held = jnp.pad(held, (0, -held.size % 8)).reshape(8, -1)
-    riders = jnp.concatenate(split_two(held), axis=1)
-    rider_cols = riders.shape[1]
-    riders = jnp.pad(riders, ((0, 0), (0, D - rider_cols)))
 
     def finish(total, which, masters, moments, extra=None):
         _, rows, cols = total.parts[0].shape
@@ -1113,8 +1113,10 @@
     call.waiting = []
     tail = call.pin([moved_2.blocks, moved_2.got])
     (new_2,) = put(moved_2, (D,), FF // nd)
+    call.last = None
+    (new_q,) = put(moved_3, (3 * D,), D // nd)
+    call.last = None
     new_1, new_o = put(moved_1, (FF, D), D // nd)
-    (new_q,) = put(moved_3, (3 * D,), D // nd)
 
     own_cols = D // nd
     got = jnp.concatenate([part[:, FF // nd :] for part in tail], axis=0)

time: 244 us -> 247 us (1.012)
  other arithmetic: 19.9 us -> 26.8 us
  starting transfers between devices: 42.2 us -> 47.4 us
  waiting for transfers between devices: 39.5 us -> 34.9 us
  Pallas kernels: 120 us -> 116 us
    convert_element_type x12, other arithmetic: 6.66 us -> 12.3 us  [add(): self.sent = self.call.hold(total.astype(BF16))]
    ppermute x47, starting transfers between devices: 42.2 us -> 47.4 us  [exchange(): return lax.ppermute(value, ('batch', 'fsdp'), pairs)]
    ppermute x47, waiting for transfers between devices: 39.5 us -> 34.9 us  [exchange(): return lax.ppermute(value, ('batch', 'fsdp'), pairs)]
    pallas_call x19, Pallas kernels: 120 us -> 116 us  [__call__(): pl.pallas_call(body, grid_spec=pltpu.PrefetchScalarGridSpec(num_scalar_pr...]
    unnamed x146 -> x170, local copies, waits for them, and re-layouts: 15.2 us -> 15.4 us
  transfers between devices with their start and end apart: 47 -> 47, of which waited for: 19 -> 14; matrix products, arithmetic and copies ran while one was open for 9% -> 12% of each run, Pallas kernels for 48% -> 45%
where the time goes in v4:
time: 247 us; the launch traced here: 246 us
  Pallas kernels  116 us (47%)
  starting transfers between devices  47.4 us (19%)
  waiting for transfers between devices  34.9 us (14%)
  other arithmetic  26.8 us (11%)
  local copies, waits for them, and re-layouts  19.4 us (8%)
    pallas_call x19, Pallas kernels, __call__(): pl.pallas_call(body, grid_spec=pltpu.PrefetchScalarGridSpec(num_scalar_pr...  116 us
    ppermute x47, starting transfers between devices, exchange(): return lax.ppermute(value, ('batch', 'fsdp'), pairs)  47.4 us
    ppermute x47, waiting for transfers between devices, exchange(): return lax.ppermute(value, ('batch', 'fsdp'), pairs)  34.9 us
    unnamed x170, local copies, waits for them, and re-layouts  15.4 us
    convert_element_type x12, other arithmetic, add(): self.sent = self.call.hold(total.astype(BF16))  12.3 us
    convert_element_type x3, other arithmetic, finish(): news.append(new_w.astype(BF16))  6.1 us
  transfers between devices with their start and end apart: 47, of which 14 were waited for; matrix products, arithmetic and copies ran while one was open for 12% of the time, Pallas kernels for 45%

profile of v4, /device:TPU:0, one launch (start us, length us, event | category | flops | bytes accessed | tf_op | source)
XLA Modules:
  0.0 246.0 jit_solution(10557015880385190923)
XLA Ops:
  1.4 3.0 %collective-permute-start = (bf16[14,192]{1,0:T(8,128)(2,1)S(1)}, bf16[14,192]{1,0:T(8,128)(2,1)S(1)}, u32[]{:S(2)}, u32[]{:S(2)}) collective-permute-start(bf16[14,192]{1,0:T(8,128)(2,1)S(1)} %convert_element_type.251), channel_id=1, source_target_pairs={{0,2},{1,3},{2,0},{3,1},{4,6},{5,7},{6,4},{7,5},{8,10},{9,11},{10,... | collective-permute-start | bytes 16136 | tf_op jit(solution)/shard_map/ppermute | solution.py:112
  10.1 3.3 %order.1 = (bf16[4,256,256]{2,1,0:T(8,128)(2,1)S(1)}, bf16[4,256,768]{2,1,0:T(8,128)(2,1)S(1)}, bf16[4,256,128]{2,1,0:T(8,128)(2,1)S(1)}, bf16[4,128,768]{2,1,0:T(8,128)(2,1)S(1)}) custom-call(s32[4]{0:T(128)S(1)} %copy-done.42, s32[4,1,128]{2,1,0:T(1,128)S(1)} %bitcast.31, bf16[4,256,768]{2,1,0:T(8,128)(2,1)S(1)} %copy-done.25, ...), custom_call_target="tpu_custom_call" | custom-call | flops 17999998976 | bytes 60000000 | tf_op jit(solution)/shard_map/order/pallas_call | solution.py:579
  18.0 3.3 %collective-permute-done.4.refs_2_.refs_6_.refs_14_ = bf16[96,2304]{1,0:T(8,128)(2,1)S(1)} collective-permute-done((bf16[96,2304]{1,0:T(8,128)(2,1)S(1)}, bf16[96,2304]{1,0:T(8,128)(2,1)S(1)}, u32[]{:S(2)}, u32[]{:S(2)}) %collective-permute-start.4) | collective-permute-done | bytes 442400 | tf_op jit(solution)/shard_map/ppermute | solution.py:112
  25.0 4.6 %collective-permute-done.5.refs_7_.refs_15_ = bf16[96,2304]{1,0:T(8,128)(2,1)} collective-permute-done((bf16[96,2304]{1,0:T(8,128)(2,1)S(1)}, bf16[96,2304]{1,0:T(8,128)(2,1)}, u32[]{:S(2)}, u32[]{:S(2)}) %collective-permute-start.5) | collective-permute-done | bytes 442400 | tf_op jit(solution)/shard_map/ppermute | solution.py:112
  32.1 7.9 %qkv.1 = (bf16[4,256,768]{2,1,0:T(8,128)(2,1)S(1)}, bf16[4,256,2304]{2,1,0:T(8,128)(2,1)S(1)}) custom-call(s32[52]{0:T(128)S(1)} %get-tuple-element.296.refs_0_, bf16[4,256,768]{2,1,0:T(8,128)(2,1)S(1)} %copy-done.9, bf16[4,256,128]{2,1,0:T(8,128)(2,1)S(1)} %copy-done.19, f32[16,768]{1,0:T(8,128)S(1)} %fusion.12.refs_3_.refs_4_, ...), custom_call_target="tpu_custom_call" | custom-call | flops 300000000 | bytes 1000000 | tf_op jit(solution)/shard_map/qkv/pallas_call | solution.py:579
  42.9 6.0 %mix.1.refs_3_.refs_11_ = bf16[4,256,768]{2,1,0:T(8,128)(2,1)S(1)} custom-call(bf16[4,256,2304]{2,1,0:T(8,128)(2,1)S(1)} %get-tuple-element.154.refs_0_.refs_2_, bf16[96,3840]{1,0:T(8,128)(2,1)S(1)} %collective-permute-done.8.refs_1_.refs_7_, bf16[4,256,2304]{2,1,0:T(8,128)(2,1)S(1)} %get-tuple-element.154.refs_0_.refs_2_), custom_call_target="tpu_custom_call" | custom-call | flops 3000000000 | bytes 10000000 | tf_op jit(solution)/shard_map/mix/pallas_call | solution.py:579
  48.9 4.5 %collective-permute-done.10.refs_8_ = bf16[96,3840]{1,0:T(8,128)(2,1)S(1)} collective-permute-done((bf16[96,3840]{1,0:T(8,128)(2,1)S(1)}, bf16[96,3840]{1,0:T(8,128)(2,1)S(1)}, u32[]{:S(2)}, u32[]{:S(2)}) %collective-permute-start.10) | collective-permute-done | bytes 737312 | tf_op jit(solution)/shard_map/ppermute | solution.py:112
  55.6 13.1 %fc1.1 = (f32[4,256,768]{2,1,0:T(8,128)S(1)}, bf16[4,256,768]{2,1,0:T(8,128)(2,1)S(1)}, bf16[4,256,3072]{2,1,0:T(8,128)(2,1)S(1)}, bf16[4,128,3072]{2,1,0:T(8,128)(2,1)S(1)}) custom-call(s32[52]{0:T(128)S(1)} %get-tuple-element.296.refs_0_, bf16[4,256,768]{2,1,0:T(8,128)(2,1)S(1)} %copy-done.9, bf16[4,256,128]{2,1,0:T(8,128)(2,1)S(1)} %copy-done.19, ...), custom_call_target="tpu_custom_call" | custom-call | flops 54000001024 | bytes 180000000 | tf_op jit(solution)/shard_map/fc1/pallas_call | solution.py:579
  70.2 5.9 %gw2.1 = (bf16[16,96,768]{2,1,0:T(8,128)(2,1)S(1)}, bf16[16,96,768]{2,1,0:T(8,128)(2,1)S(1)}, f32[1,768]{1,0:T(1,128)S(1)}) custom-call(s32[52]{0:T(128)S(1)} %get-tuple-element.296.refs_0_, bf16[4,256,3072]{2,1,0:T(8,128)(2,1)S(1)} %get-tuple-element.158.refs_1_, bf16[4,128,768]{2,1,0:T(8,128)(2,1)S(1)} %copy-done.12, ...), custom_call_target="tpu_custom_call" | custom-call | flops 24000000000 | bytes 80000000 | tf_op jit(solution)/shard_map/gw2/pallas_call | solution.py:579
  76.2 2.8 %collective-permute-done.15.refs_6_.refs_8_ = bf16[384,768]{1,0:T(8,128)(2,1)S(1)} collective-permute-done((bf16[384,768]{1,0:T(8,128)(2,1)S(1)}, bf16[384,768]{1,0:T(8,128)(2,1)S(1)}, u32[]{:S(2)}, u32[]{:S(2)}) %collective-permute-start.15) | collective-permute-done | bytes 589856 | tf_op jit(solution)/shard_map/ppermute | solution.py:112
  81.0 5.4 %df.1 = (bf16[512,3072]{1,0:T(8,128)(2,1)S(1)}, f32[1,3072]{1,0:T(1,128)S(1)}) custom-call(s32[52]{0:T(128)S(1)} %get-tuple-element.296.refs_0_, bf16[4,128,768]{2,1,0:T(8,128)(2,1)S(1)} %copy-done.12, bf16[4,128,3072]{2,1,0:T(8,128)(2,1)S(1)} %get-tuple-element.164.refs_3_.refs_2_, bf16[768,768]{1,0:T(8,128)(2,1)S(1)} %get-tuple-element.161.refs_3_.refs_5_, ...), custom_call_target="tpu_custom_call" | custom-call | flops 20999999488 | bytes 70000000 | tf_op jit(solution)/shard_map/df/pallas_call | solution.py:579
  89.3 6.7 %mlp_back.1 = (f32[4,128,768]{2,1,0:T(8,128)S(1)}, bf16[4,128,768]{2,1,0:T(8,128)(2,1)S(1)}, bf16[4,128,768]{2,1,0:T(8,128)(2,1)S(1)}, f32[8,768]{1,0:T(8,128)S(1)}) custom-call(s32[52]{0:T(128)S(1)} %get-tuple-element.296.refs_0_, bf16[512,3072]{1,0:T(8,128)(2,1)S(1)} %get-tuple-element.167.refs_1_.refs_2_, bf16[4,128,768]{2,1,0:T(8,128)(2,1)S(1)} %copy-done.12, ...), custom_call_target="tpu_custom_call" | custom-call | flops 30000001024 | bytes 100000000 | tf_op jit(solution)/shard_map/mlp_back/pallas_call | solution.py:579
  96.1 6.9 %gw1o.1 = (bf16[16,24,3840]{2,1,0:T(8,128)(2,1)S(1)}, bf16[16,24,3840]{2,1,0:T(8,128)(2,1)S(1)}) custom-call(s32[52]{0:T(128)S(1)} %get-tuple-element.296.refs_0_, bf16[4,256,768]{2,1,0:T(8,128)(2,1)S(1)} %get-tuple-element.162.refs_1_, bf16[512,3072]{1,0:T(8,128)(2,1)S(1)} %get-tuple-element.167.refs_1_.refs_2_, ...), custom_call_target="tpu_custom_call" | custom-call | flops 27000000512 | bytes 90000000 | tf_op jit(solution)/shard_map/gw1o/pallas_call | solution.py:579
  105.1 9.1 %attn_back.2 = (bf16[4,128,768]{2,1,0:T(8,128)(2,1)S(1)}, bf16[4,256,1536]{2,1,0:T(8,128)(2,1)S(1)}, f32[8,768]{1,0:T(8,128)S(1)}) custom-call(bf16[4,256,2304]{2,1,0:T(8,128)(2,1)S(1)} %bitcast.30, bf16[4,128,768]{2,1,0:T(8,128)(2,1)S(1)} %get-tuple-element.173.refs_1_, bf16[4,96,768]{2,1,0:T(8,128)(2,1)S(1)} %add_convert_fusion.4.refs_2_, ...), custom_call_target="tpu_custom_call" | custom-call | flops 35999997952 | bytes 120000000 | tf_op jit(solution)/shard_map/attn_back/pallas_call | solution.py:579
  114.4 2.8 %collective-permute-start.22 = (bf16[2,96,768]{2,1,0:T(8,128)(2,1)S(1)}, bf16[2,96,768]{2,1,0:T(8,128)(2,1)S(1)}, u32[]{:S(2)}, u32[]{:S(2)}) collective-permute-start(bf16[2,96,768]{2,1,0:T(8,128)(2,1)S(1)} %add_convert_fusion.7.refs_6_), channel_id=1, source_target_pairs={{0,24},{1,3},{2,26},{3,1},{4,28},{5,7},{6,30},{7,5},{8,16},{9,11},... | collective-permute-start | bytes 884744 | tf_op jit(solution)/shard_map/ppermute | solution.py:112
  119.8 9.1 %attn_back.3 = (bf16[4,128,768]{2,1,0:T(8,128)(2,1)S(1)}, bf16[4,256,1536]{2,1,0:T(8,128)(2,1)S(1)}, f32[8,768]{1,0:T(8,128)S(1)}) custom-call(bf16[4,256,2304]{2,1,0:T(8,128)(2,1)S(1)} %bitcast.30, bf16[4,128,768]{2,1,0:T(8,128)(2,1)S(1)} %get-tuple-element.173.refs_1_, ...), custom_call_target="tpu_custom_call", output_to_operand_aliasing={{0}: (2, {}), {1}: (3, {})} | custom-call | flops 35999997952 | bytes 120000000 | tf_op jit(solution)/shard_map/attn_back/pallas_call | solution.py:579
  129.2 7.0 %gqkv.1 = (bf16[16,24,2304]{2,1,0:T(8,128)(2,1)S(1)}, bf16[16,24,2304]{2,1,0:T(8,128)(2,1)}) custom-call(s32[52]{0:T(128)S(1)} %get-tuple-element.296.refs_0_, bf16[4,256,768]{2,1,0:T(8,128)(2,1)S(1)} %get-tuple-element.155.refs_1_, bf16[4,128,768]{2,1,0:T(8,128)(2,1)S(1)} %get-tuple-element.190.refs_2_.refs_4_, ...), custom_call_target="tpu_custom_call" | custom-call | flops 27000000512 | bytes 90000000 | tf_op jit(solution)/shard_map/gqkv/pallas_call | solution.py:579
  144.8 2.5 %subtract_convert_fusion.1 = (bf16[96,768]{1,0:T(8,128)(2,1)S(1)}, f32[96,768]{1,0:T(8,128)}, f32[96,768]{1,0:T(8,128)}) fusion(f32[768,768]{1,0:T(8,128)S(1)} %copy-done.1, s32[]{:T(128)S(6)} %select_n.143, bf16[1,96,768]{2,1,0:T(8,128)(2,1)S(1)} %collective-permute-done.26, bf16[2,96,768]{2,1,0:T(8,128)(2,1)} %copy-done.66, ...), kind=kLoop, calls=%fused_computation.21 | loop fusion | flops 1916928 | bytes 2506756 | tf_op jit(solution)/shard_map/convert_element_type | solution.py:996
  151.9 12.1 %grad_in.1 = (f32[4,256,768]{2,1,0:T(8,128)}, f32[16,768]{1,0:T(8,128)S(1)}) custom-call(s32[52]{0:T(128)S(1)} %get-tuple-element.296.refs_0_, bf16[4,256,768]{2,1,0:T(8,128)(2,1)S(1)} %copy-done.10, bf16[4,256,128]{2,1,0:T(8,128)(2,1)S(1)} %copy-done.20, f32[16,768]{1,0:T(8,128)S(1)} %copy-done.22, bf16[4,128,768]{2,1,0:T(8,128)(2,1)S(1)} %copy-done.55, ...), custom_call_target="tpu_custom_call" | custom-call | flops 44999999488 | bytes 150000000 | tf_op jit(solution)/shard_map/grad_in/pallas_call | solution.py:579
  170.0 2.8 %copy-done.44 = bf16[4,256,3072]{2,1,0:T(8,128)(2,1)S(1)} copy-done((bf16[4,256,3072]{2,1,0:T(8,128)(2,1)S(1)}, bf16[4,256,3072]{2,1,0:T(8,128)(2,1)}, u32[]{:S(2)}) %copy-start.44) | copy-done | bytes 6291480
  172.8 9.3 %out.1 = bf16[4,256,768]{2,1,0:T(8,128)(2,1)} custom-call(s32[52]{0:T(128)S(1)} %get-tuple-element.296.refs_0_, bf16[4,256,3072]{2,1,0:T(8,128)(2,1)S(1)} %copy-done.44, f32[4,256,768]{2,1,0:T(8,128)S(1)} %copy-done.49, f32[16,768]{1,0:T(8,128)S(1)} %copy-done.22, bf16[4,256,256]{2,1,0:T(8,128)(2,1)S(1)} %copy-done.53, bf16[768,768]{1,0:T(8,128)(2,1)S(1)} %copy-done.30, ...), custom_call_target="tpu_custom_call" | custom-call | flops 38999998464 | bytes 130000000 | tf_op jit(solution)/shard_map/out/pallas_call | solution.py:579
  193.4 2.0 subtract_convert_fusion
  195.5 2.2 collective-permute-start.37
  202.0 2.8 %collective-permute-done.37 = bf16[1,24,3840]{2,1,0:T(8,128)(2,1)S(1)} collective-permute-done((bf16[1,24,3840]{2,1,0:T(8,128)(2,1)S(1)}, bf16[1,24,3840]{2,1,0:T(8,128)(2,1)S(1)}, u32[]{:S(2)}, u32[]{:S(2)}) %collective-permute-start.37) | collective-permute-done | bytes 184352 | tf_op jit(solution)/shard_map/ppermute | solution.py:112
  207.0 2.0 fusion.3
  209.0 2.7 %collective-permute-start.32 = (bf16[1,24,2304]{2,1,0:T(8,128)(2,1)S(1)}, bf16[1,24,2304]{2,1,0:T(8,128)(2,1)S(1)}, u32[]{:S(2)}, u32[]{:S(2)}) collective-permute-start(bf16[1,24,2304]{2,1,0:T(8,128)(2,1)S(1)} %get-tuple-element.238), channel_id=1, source_target_pairs={{0,24},{1,25},{2,26},{3,27},{4,28},{5,29},{6,30},{7,31},{8,16},{9,... | collective-permute-start | bytes 331784 | tf_op jit(solution)/shard_map/ppermute | solution.py:112
  211.7 2.8 %collective-permute-start.38 = (bf16[2,24,3840]{2,1,0:T(8,128)(2,1)S(1)}, bf16[2,24,3840]{2,1,0:T(8,128)(2,1)S(1)}, u32[]{:S(2)}, u32[]{:S(2)}) collective-permute-start(bf16[2,24,3840]{2,1,0:T(8,128)(2,1)S(1)} %constant_dynamic-update-slice_fusion.6), channel_id=1, source_target_pairs={{0,8},{1,5},{2,10},{3,7},{4,12},{5,1},{6,14},{7,3},{8,0},{9,13},{1... | collective-permute-start | bytes 1105928 | tf_op jit(solution)/shard_map/ppermute | solution.py:112
  216.3 3.4 %collective-permute-start.33 = (bf16[2,24,2304]{2,1,0:T(8,128)(2,1)S(1)}, bf16[2,24,2304]{2,1,0:T(8,128)(2,1)S(1)}, u32[]{:S(2)}, u32[]{:S(2)}) collective-permute-start(bf16[2,24,2304]{2,1,0:T(8,128)(2,1)S(1)} %constant_dynamic-update-slice_fusion.2), channel_id=1, source_target_pairs={{0,8},{1,5},{2,10},{3,7},{4,12},{5,1},{6,14},{7,3},{8,0},{9,13},{1... | collective-permute-start | bytes 663560 | tf_op jit(solution)/shard_map/ppermute | solution.py:112
  226.6 2.5 %place.5 = f32[768,768]{1,0:T(8,128)} custom-call(s32[52]{0:T(128)S(1)} %get-tuple-element.296.refs_0_, bf16[4,104,768]{2,1,0:T(8,128)(2,1)S(1)} %constant_dynamic-update-slice_fusion.10.refs_1_, bf16[4,104,768]{2,1,0:T(8,128)(2,1)S(1)} %collective-permute-done.41.refs_2_, bf16[4,24,2304]{2,1,0:T(8,128)(2,1)S(1)} %constant_dynamic-update-slice_fusion.4.refs_1_.refs_3_), custom_call_target="tpu_custom_call" | custom-call | flops 3000000000 | bytes 10000000 | tf_op jit(solution)/shard_map/place/pallas_call | solution.py:579
  229.1 9.6 %collective-permute-done.34.refs_2_ = bf16[4,24,2304]{2,1,0:T(8,128)(2,1)S(1)} collective-permute-done((bf16[4,24,2304]{2,1,0:T(8,128)(2,1)S(1)}, bf16[4,24,2304]{2,1,0:T(8,128)(2,1)S(1)}, u32[]{:S(2)}, u32[]{:S(2)}) %collective-permute-start.34) | collective-permute-done | bytes 442400 | tf_op jit(solution)/shard_map/ppermute | solution.py:112
  238.7 2.4 place.3
  241.1 4.9 %place.4 = (f32[192,3072]{1,0:T(8,128)}, f32[192,768]{1,0:T(8,128)}) custom-call(s32[52]{0:T(128)S(1)} %get-tuple-element.296.refs_0_, bf16[4,24,3840]{2,1,0:T(8,128)(2,1)} %constant_dynamic-update-slice_fusion.8.refs_1_, bf16[4,24,3840]{2,1,0:T(8,128)(2,1)S(1)} %collective-permute-done.39.refs_2_), custom_call_target="tpu_custom_call" | custom-call | flops 3000000000 | bytes 10000000 | tf_op jit(solution)/shard_map/place/pallas_call | solution.py:579
  (306 shorter events, 78.8 us)
Async XLA Ops:
  1.4 13.2 %collective-permute-start = (bf16[14,192]{1,0:T(8,128)(2,1)S(1)}, bf16[14,192]{1,0:T(8,128)(2,1)S(1)}, u32[]{:S(2)}, u32[]{:S(2)}) collective-permute-start(bf16[14,192]{1,0:T(8,128)(2,1)S(1)} %convert_element_type.251), channel_id=1, source_target_pairs={{0,2},{1,3},{2,0},{3,1},{4,6},{5,7},{6,4},{7,5},{8,10},{9,11},{10,... | collective-permute-start | bytes 16136 | tf_op jit(solution)/shard_map/ppermute | solution.py:112
  4.4 13.6 %collective-permute-start.2 = (bf16[14,192]{1,0:T(8,128)(2,1)S(1)}, bf16[14,192]{1,0:T(8,128)(2,1)S(1)}, u32[]{:S(2)}, u32[]{:S(2)}) collective-permute-start(bf16[14,192]{1,0:T(8,128)(2,1)S(1)} %convert_element_type.251), channel_id=1, source_target_pairs={{0,1},{1,0},{2,3},{3,2},{4,5},{5,4},{6,7},{7,6},{8,9},{9,8},{10,11... | collective-permute-start | bytes 16136 | tf_op jit(solution)/shard_map/ppermute | solution.py:112
  8.7 12.6 %collective-permute-start.4 = (bf16[96,2304]{1,0:T(8,128)(2,1)S(1)}, bf16[96,2304]{1,0:T(8,128)(2,1)S(1)}, u32[]{:S(2)}, u32[]{:S(2)}) collective-permute-start(bf16[96,2304]{1,0:T(8,128)(2,1)S(1)} %get-tuple-element.145.refs_4_), channel_id=1, source_target_pairs={{0,2},{1,3},{2,0},{3,1},{4,6},{5,7},{6,4},{7,5},{8,10},{9,11},{10,... | collective-permute-start | bytes 1327112 | tf_op jit(solution)/shard_map/ppermute | solution.py:112
  22.8 8.7 %collective-permute-start.3 = (bf16[192,2304]{1,0:T(8,128)(2,1)}, bf16[192,2304]{1,0:T(8,128)(2,1)}, u32[]{:S(2)}, u32[]{:S(2)}) collective-permute-start(bf16[192,2304]{1,0:T(8,128)(2,1)} %get-tuple-element.148.refs_4_.refs_12_), channel_id=1, source_target_pairs={{0,1},{1,0},{2,3},{3,2},{4,5},{5,4},{6,7},{7,6},{8,9},{9,8},{10,11... | collective-permute-start | bytes 2654216 | tf_op jit(solution)/shard_map/ppermute | solution.py:112
  22.8 19.1 %collective-permute-start.8 = (bf16[96,3840]{1,0:T(8,128)(2,1)}, bf16[96,3840]{1,0:T(8,128)(2,1)S(1)}, u32[]{:S(2)}, u32[]{:S(2)}) collective-permute-start(bf16[96,3840]{1,0:T(8,128)(2,1)} %get-tuple-element.152.refs_4_), channel_id=1, source_target_pairs={{0,2},{1,3},{2,0},{3,1},{4,6},{5,7},{6,4},{7,5},{8,10},{9,11},{10,... | collective-permute-start | bytes 2211848 | tf_op jit(solution)/shard_map/ppermute | solution.py:112
  41.9 11.5 %collective-permute-start.10 = (bf16[96,3840]{1,0:T(8,128)(2,1)S(1)}, bf16[96,3840]{1,0:T(8,128)(2,1)S(1)}, u32[]{:S(2)}, u32[]{:S(2)}) collective-permute-start(bf16[96,3840]{1,0:T(8,128)(2,1)S(1)} %collective-permute-done.8.refs_1_.refs_7_), channel_id=1, source_target_pairs={{0,4},{1,9},{2,6},{3,11},{4,0},{5,13},{6,2},{7,15},{8,12},{9,1},{1... | collective-permute-start | bytes 2211848 | tf_op jit(solution)/shard_map/ppermute | solution.py:112
  42.4 11.7 %collective-permute-start.9 = (bf16[192,3840]{1,0:T(8,128)(2,1)S(1)}, bf16[192,3840]{1,0:T(8,128)(2,1)S(1)}, u32[]{:S(2)}, u32[]{:S(2)}) collective-permute-start(bf16[192,3840]{1,0:T(8,128)(2,1)S(1)} %copy-done.28), channel_id=1, source_target_pairs={{0,1},{1,0},{2,3},{3,2},{4,5},{5,4},{6,7},{7,6},{8,9},{9,8},{10,11... | collective-permute-start | bytes 4423688 | tf_op jit(solution)/shard_map/ppermute | solution.py:112
  42.8 11.4 %collective-permute-start.11 = (bf16[96,3840]{1,0:T(8,128)(2,1)S(1)}, bf16[96,3840]{1,0:T(8,128)(2,1)S(1)}, u32[]{:S(2)}, u32[]{:S(2)}) collective-permute-start(bf16[96,3840]{1,0:T(8,128)(2,1)S(1)} %collective-permute-done.8.refs_1_.refs_7_), channel_id=1, source_target_pairs={{0,1},{1,0},{2,3},{3,2},{4,5},{5,4},{6,7},{7,6},{8,9},{9,8},{10,11... | collective-permute-start | bytes 2211848 | tf_op jit(solution)/shard_map/ppermute | solution.py:112
  53.4 15.7 %collective-permute-start.14 = (bf16[384,768]{1,0:T(8,128)(2,1)S(1)}, bf16[384,768]{1,0:T(8,128)(2,1)S(1)}, u32[]{:S(2)}, u32[]{:S(2)}) collective-permute-start(bf16[384,768]{1,0:T(8,128)(2,1)S(1)} %get-tuple-element.153.refs_10_), channel_id=1, source_target_pairs={{0,2},{1,3},{2,0},{3,1},{4,6},{5,7},{6,4},{7,5},{8,10},{9,11},{10,... | collective-permute-start | bytes 1769480 | tf_op jit(solution)/shard_map/ppermute | solution.py:112
  53.9 25.6 %collective-permute-start.13 = (bf16[768,768]{1,0:T(8,128)(2,1)S(1)}, bf16[768,768]{1,0:T(8,128)(2,1)S(1)}, u32[]{:S(2)}, u32[]{:S(2)}) collective-permute-start(bf16[768,768]{1,0:T(8,128)(2,1)S(1)} %get-tuple-element.161.refs_3_.refs_5_), channel_id=1, source_target_pairs={{0,1},{1,0},{2,3},{3,2},{4,5},{5,4},{6,7},{7,6},{8,9},{9,8},{10,11... | collective-permute-start | bytes 3538952 | tf_op jit(solution)/shard_map/ppermute | solution.py:112
  69.1 9.9 %collective-permute-start.15 = (bf16[384,768]{1,0:T(8,128)(2,1)S(1)}, bf16[384,768]{1,0:T(8,128)(2,1)S(1)}, u32[]{:S(2)}, u32[]{:S(2)}) collective-permute-start(bf16[384,768]{1,0:T(8,128)(2,1)S(1)} %collective-permute-done.14.refs_5_.refs_7_), channel_id=1, source_target_pairs={{0,4},{1,9},{2,6},{3,11},{4,0},{5,13},{6,2},{7,15},{8,12},{9,1},{1... | collective-permute-start | bytes 1769480 | tf_op jit(solution)/shard_map/ppermute | solution.py:112
  69.6 9.9 %collective-permute-start.16 = (bf16[384,768]{1,0:T(8,128)(2,1)S(1)}, bf16[384,768]{1,0:T(8,128)(2,1)S(1)}, u32[]{:S(2)}, u32[]{:S(2)}) collective-permute-start(bf16[384,768]{1,0:T(8,128)(2,1)S(1)} %collective-permute-done.14.refs_5_.refs_7_), channel_id=1, source_target_pairs={{0,1},{1,0},{2,3},{3,2},{4,5},{5,4},{6,7},{7,6},{8,9},{9,8},{10,11... | collective-permute-start | bytes 1769480 | tf_op jit(solution)/shard_map/ppermute | solution.py:112
  86.9 16.3 %collective-permute-start.19 = (bf16[8,96,768]{2,1,0:T(8,128)(2,1)S(1)}, bf16[8,96,768]{2,1,0:T(8,128)(2,1)S(1)}, u32[]{:S(2)}, u32[]{:S(2)}) collective-permute-start(bf16[8,96,768]{2,1,0:T(8,128)(2,1)S(1)} %add_convert_fusion.1.refs_11_), channel_id=1, source_target_pairs={{0,4},{1,9},{2,6},{3,11},{4,0},{5,13},{6,2},{7,15},{8,12},{9,1},{1... | collective-permute-start | bytes 3538952 | tf_op jit(solution)/shard_map/ppermute | solution.py:112
  103.0 14.2 %collective-permute-start.20 = (bf16[16,24,3840]{2,1,0:T(8,128)(2,1)S(1)}, bf16[16,24,3840]{2,1,0:T(8,128)(2,1)S(1)}, u32[]{:S(2)}, u32[]{:S(2)}) collective-permute-start(bf16[16,24,3840]{2,1,0:T(8,128)(2,1)S(1)} %get-tuple-element.176.refs_3_), channel_id=1, source_target_pairs={{0,1},{1,0},{2,3},{3,2},{4,5},{5,4},{6,7},{7,6},{8,9},{9,8},{10,11... | collective-permute-start | bytes 8847368 | tf_op jit(solution)/shard_map/ppermute | solution.py:112
  103.4 10.8 %collective-permute-start.21 = (bf16[4,96,768]{2,1,0:T(8,128)(2,1)S(1)}, bf16[4,96,768]{2,1,0:T(8,128)(2,1)S(1)}, u32[]{:S(2)}, u32[]{:S(2)}) collective-permute-start(bf16[4,96,768]{2,1,0:T(8,128)(2,1)S(1)} %add_convert_fusion.4.refs_2_), channel_id=1, source_target_pairs={{0,8},{1,5},{2,10},{3,7},{4,12},{5,1},{6,14},{7,3},{8,0},{9,13},{1... | collective-permute-start | bytes 1769480 | tf_op jit(solution)/shard_map/ppermute | solution.py:112
  114.4 14.6 %collective-permute-start.22 = (bf16[2,96,768]{2,1,0:T(8,128)(2,1)S(1)}, bf16[2,96,768]{2,1,0:T(8,128)(2,1)S(1)}, u32[]{:S(2)}, u32[]{:S(2)}) collective-permute-start(bf16[2,96,768]{2,1,0:T(8,128)(2,1)S(1)} %add_convert_fusion.7.refs_6_), channel_id=1, source_target_pairs={{0,24},{1,3},{2,26},{3,1},{4,28},{5,7},{6,30},{7,5},{8,16},{9,11},... | collective-permute-start | bytes 884744 | tf_op jit(solution)/shard_map/ppermute | solution.py:112
  119.3 19.8 %collective-permute-start.25 = (bf16[8,24,3840]{2,1,0:T(8,128)(2,1)}, bf16[8,24,3840]{2,1,0:T(8,128)(2,1)}, u32[]{:S(2)}, u32[]{:S(2)}) collective-permute-start(bf16[8,24,3840]{2,1,0:T(8,128)(2,1)} %add_convert_fusion.refs_5_), channel_id=1, source_target_pairs={{0,4},{1,9},{2,6},{3,11},{4,0},{5,13},{6,2},{7,15},{8,12},{9,1},{1... | collective-permute-start | bytes 4423688 | tf_op jit(solution)/shard_map/ppermute | solution.py:112
  141.1 24.5 %collective-permute-start.27 = (bf16[4,24,3840]{2,1,0:T(8,128)(2,1)S(1)}, bf16[4,24,3840]{2,1,0:T(8,128)(2,1)S(1)}, u32[]{:S(2)}, u32[]{:S(2)}) collective-permute-start(bf16[4,24,3840]{2,1,0:T(8,128)(2,1)S(1)} %add_convert_fusion.3.refs_18_), channel_id=1, source_target_pairs={{0,8},{1,5},{2,10},{3,7},{4,12},{5,1},{6,14},{7,3},{8,0},{9,13},{1... | collective-permute-start | bytes 2211848 | tf_op jit(solution)/shard_map/ppermute | solution.py:112
  143.2 25.5 %collective-permute-start.24 = (bf16[8,24,2304]{2,1,0:T(8,128)(2,1)S(1)}, bf16[8,24,2304]{2,1,0:T(8,128)(2,1)S(1)}, u32[]{:S(2)}, u32[]{:S(2)}) collective-permute-start(bf16[8,24,2304]{2,1,0:T(8,128)(2,1)S(1)} %add_convert_fusion.2.refs_19_), channel_id=1, source_target_pairs={{0,4},{1,9},{2,6},{3,11},{4,0},{5,13},{6,2},{7,15},{8,12},{9,1},{1... | collective-permute-start | bytes 2654216 | tf_op jit(solution)/shard_map/ppermute | solution.py:112
  147.3 17.6 %collective-permute-start.28 = (bf16[1,104,768]{2,1,0:T(8,128)(2,1)S(1)}, bf16[1,104,768]{2,1,0:T(8,128)(2,1)S(1)}, u32[]{:S(2)}, u32[]{:S(2)}) collective-permute-start(bf16[1,104,768]{2,1,0:T(8,128)(2,1)S(1)} %maximum_bitcast_fusion.1.refs_20_), channel_id=1, source_target_pairs={{0,24},{1,25},{2,26},{3,27},{4,28},{5,29},{6,30},{7,31},{8,16},{9,... | collective-permute-start | bytes 479240 | tf_op jit(solution)/shard_map/ppermute | solution.py:112
  163.9 22.3 %collective-permute-start.42 = (f32[16,768]{1,0:T(8,128)S(1)}, f32[16,768]{1,0:T(8,128)S(1)}, u32[]{:S(2)}, u32[]{:S(2)}) collective-permute-start(f32[16,768]{1,0:T(8,128)S(1)} %get-tuple-element.263.refs_14_), channel_id=1, source_target_pairs={{0,1},{1,0},{2,3},{3,2},{4,5},{5,4},{6,7},{7,6},{8,9},{9,8},{10,11... | collective-permute-start | bytes 147464 | tf_op jit(solution)/shard_map/ppermute | solution.py:112
  164.9 20.0 %collective-permute-start.40 = (bf16[2,104,768]{2,1,0:T(8,128)(2,1)S(1)}, bf16[2,104,768]{2,1,0:T(8,128)(2,1)S(1)}, u32[]{:S(2)}, u32[]{:S(2)}) collective-permute-start(bf16[2,104,768]{2,1,0:T(8,128)(2,1)S(1)} %constant_dynamic-update-slice_fusion.refs_13_), channel_id=1, source_target_pairs={{0,8},{1,5},{2,10},{3,7},{4,12},{5,1},{6,14},{7,3},{8,0},{9,13},{1... | collective-permute-start | bytes 958472 | tf_op jit(solution)/shard_map/ppermute | solution.py:112
  167.5 14.7 %collective-permute-start.35 = (bf16[2,24,3840]{2,1,0:T(8,128)(2,1)S(1)}, bf16[2,24,3840]{2,1,0:T(8,128)(2,1)S(1)}, u32[]{:S(2)}, u32[]{:S(2)}) collective-permute-start(bf16[2,24,3840]{2,1,0:T(8,128)(2,1)S(1)} %add_convert_fusion.6.refs_12_), channel_id=1, source_target_pairs={{0,24},{1,3},{2,26},{3,1},{4,28},{5,7},{6,30},{7,5},{8,16},{9,11},... | collective-permute-start | bytes 1105928 | tf_op jit(solution)/shard_map/ppermute | solution.py:112
  169.9 17.8 %collective-permute-start.29 = (bf16[4,24,2304]{2,1,0:T(8,128)(2,1)S(1)}, bf16[4,24,2304]{2,1,0:T(8,128)(2,1)S(1)}, u32[]{:S(2)}, u32[]{:S(2)}) collective-permute-start(bf16[4,24,2304]{2,1,0:T(8,128)(2,1)S(1)} %add_convert_fusion.5.refs_11_), channel_id=1, source_target_pairs={{0,8},{1,5},{2,10},{3,7},{4,12},{5,1},{6,14},{7,3},{8,0},{9,13},{1... | collective-permute-start | bytes 1327112 | tf_op jit(solution)/shard_map/ppermute | solution.py:112
  185.0 39.4 %collective-permute-start.41 = (bf16[4,104,768]{2,1,0:T(8,128)(2,1)S(1)}, bf16[4,104,768]{2,1,0:T(8,128)(2,1)S(1)}, u32[]{:S(2)}, u32[]{:S(2)}) collective-permute-start(bf16[4,104,768]{2,1,0:T(8,128)(2,1)S(1)} %constant_dynamic-update-slice_fusion.10.refs_1_), channel_id=1, source_target_pairs={{0,4},{1,9},{2,6},{3,11},{4,0},{5,13},{6,2},{7,15},{8,12},{9,1},{1... | collective-permute-start | bytes 1916936 | tf_op jit(solution)/shard_map/ppermute | solution.py:112
  186.3 11.4 %collective-permute-start.43 = (f32[16,768]{1,0:T(8,128)S(1)}, f32[16,768]{1,0:T(8,128)S(1)}, u32[]{:S(2)}, u32[]{:S(2)}) collective-permute-start(f32[16,768]{1,0:T(8,128)S(1)} %add.346), channel_id=1, source_target_pairs={{0,8},{1,9},{2,10},{3,11},{4,12},{5,13},{6,14},{7,15},{8,0},{9,1},... | collective-permute-start | bytes 147464 | tf_op jit(solution)/shard_map/ppermute | solution.py:112
  188.8 10.7 %collective-permute-start.30 = (bf16[2,24,2304]{2,1,0:T(8,128)(2,1)S(1)}, bf16[2,24,2304]{2,1,0:T(8,128)(2,1)S(1)}, u32[]{:S(2)}, u32[]{:S(2)}) collective-permute-start(bf16[2,24,2304]{2,1,0:T(8,128)(2,1)S(1)} %add_convert_fusion.8), channel_id=1, source_target_pairs={{0,24},{1,3},{2,26},{3,1},{4,28},{5,7},{6,30},{7,5},{8,16},{9,11},... | collective-permute-start | bytes 663560 | tf_op jit(solution)/shard_map/ppermute | solution.py:112
  195.5 9.3 %collective-permute-start.37 = (bf16[1,24,3840]{2,1,0:T(8,128)(2,1)S(1)}, bf16[1,24,3840]{2,1,0:T(8,128)(2,1)S(1)}, u32[]{:S(2)}, u32[]{:S(2)}) collective-permute-start(bf16[1,24,3840]{2,1,0:T(8,128)(2,1)S(1)} %maximum_bitcast_fusion), channel_id=1, source_target_pairs={{0,24},{1,25},{2,26},{3,27},{4,28},{5,29},{6,30},{7,31},{8,16},{9,... | collective-permute-start | bytes 552968 | tf_op jit(solution)/shard_map/ppermute | solution.py:112
  205.6 9.0 %collective-permute-start.45 = (f32[16,768]{1,0:T(8,128)S(1)}, f32[16,768]{1,0:T(8,128)S(1)}, u32[]{:S(2)}, u32[]{:S(2)}) collective-permute-start(f32[16,768]{1,0:T(8,128)S(1)} %add.348), channel_id=1, source_target_pairs={{0,4},{1,5},{2,6},{3,7},{4,0},{5,1},{6,2},{7,3},{8,12},{9,13},{10,... | collective-permute-start | bytes 147464 | tf_op jit(solution)/shard_map/ppermute | solution.py:112
  211.7 9.1 %collective-permute-start.38 = (bf16[2,24,3840]{2,1,0:T(8,128)(2,1)S(1)}, bf16[2,24,3840]{2,1,0:T(8,128)(2,1)S(1)}, u32[]{:S(2)}, u32[]{:S(2)}) collective-permute-start(bf16[2,24,3840]{2,1,0:T(8,128)(2,1)S(1)} %constant_dynamic-update-slice_fusion.6), channel_id=1, source_target_pairs={{0,8},{1,5},{2,10},{3,7},{4,12},{5,1},{6,14},{7,3},{8,0},{9,13},{1... | collective-permute-start | bytes 1105928 | tf_op jit(solution)/shard_map/ppermute | solution.py:112
  222.3 18.8 %collective-permute-start.39 = (bf16[4,24,3840]{2,1,0:T(8,128)(2,1)}, bf16[4,24,3840]{2,1,0:T(8,128)(2,1)S(1)}, u32[]{:S(2)}, u32[]{:S(2)}) collective-permute-start(bf16[4,24,3840]{2,1,0:T(8,128)(2,1)} %constant_dynamic-update-slice_fusion.8.refs_1_), channel_id=1, source_target_pairs={{0,4},{1,9},{2,6},{3,11},{4,0},{5,13},{6,2},{7,15},{8,12},{9,1},{1... | collective-permute-start | bytes 2211848 | tf_op jit(solution)/shard_map/ppermute | solution.py:112
  224.1 14.7 %collective-permute-start.34 = (bf16[4,24,2304]{2,1,0:T(8,128)(2,1)S(1)}, bf16[4,24,2304]{2,1,0:T(8,128)(2,1)S(1)}, u32[]{:S(2)}, u32[]{:S(2)}) collective-permute-start(bf16[4,24,2304]{2,1,0:T(8,128)(2,1)S(1)} %constant_dynamic-update-slice_fusion.4.refs_1_.refs_3_), channel_id=1, source_target_pairs={{0,4},{1,9},{2,6},{3,11},{4,0},{5,13},{6,2},{7,15},{8,12},{9,1},{1... | collective-permute-start | bytes 1327112 | tf_op jit(solution)/shard_map/ppermute | solution.py:112
  (97 other events, 854.5 us)

commit v5 on v3

--- a/solution.py
+++ b/solution.py
@@ -767,9 +767,7 @@
     )
 
     set_b = cast([w_out, w_fc1])
-    near_a = set_a[2]
     set_a = last_piece(spread_pieces(set_a, [set_b[0]] + vec_parts))
-    set_c = cast([w_fc2], [near_a])
 
     n1, qkv = call(
         functools.partial(qkv_kernel, rows_d),
@@ -800,6 +798,7 @@
     )
 
     set_b = last_piece(set_b, mixed)
+    set_c = cast([w_fc2])
     h1, n2, z, slope = call(
         functools.partial(fc1_kernel, rows_d),
         (pairs,),

time: 244 us -> 242 us (level)
  local copies, waits for them, and re-layouts: 18.9 us -> 14.6 us
  waiting for transfers between devices: 39.5 us -> 42.7 us
    unnamed x146 -> x134, local copies, waits for them, and re-layouts: 15.2 us -> 11.6 us
    ppermute x47, waiting for transfers between devices: 39.5 us -> 42.7 us  [exchange(): return lax.ppermute(value, ('batch', 'fsdp'), pairs)]
  transfers between devices with their start and end apart: 47 -> 47, of which waited for: 19 -> 21; matrix products, arithmetic and copies ran while one was open for 9% -> 8% of each run, Pallas kernels for 48% -> 49%
where the time goes in v5:
time: 242 us; the launch traced here: 240 us
  Pallas kernels  120 us (50%)
  starting transfers between devices  43.2 us (18%)
  waiting for transfers between devices  42.7 us (18%)
  other arithmetic  18 us (7%)
  local copies, waits for them, and re-layouts  14.6 us (6%)
    pallas_call x19, Pallas kernels, __call__(): pl.pallas_call(body, grid_spec=pltpu.PrefetchScalarGridSpec(num_scalar_pr...  120 us
    ppermute x47, starting transfers between devices, exchange(): return lax.ppermute(value, ('batch', 'fsdp'), pairs)  43.2 us
    ppermute x47, waiting for transfers between devices, exchange(): return lax.ppermute(value, ('batch', 'fsdp'), pairs)  42.7 us
    unnamed x134, local copies, waits for them, and re-layouts  11.6 us
    convert_element_type x12, other arithmetic, add(): self.sent = self.call.hold(total.astype(BF16))  6.65 us
    convert_element_type x3, other arithmetic, finish(): news.append(new_w.astype(BF16))  5.77 us
  transfers between devices with their start and end apart: 47, of which 21 were waited for; matrix products, arithmetic and copies ran while one was open for 8% of the time, Pallas kernels for 49%

profile of v5, /device:TPU:0, one launch (start us, length us, event | category | flops | bytes accessed | tf_op | source)
XLA Modules:
  0.0 240.3 jit_solution(11644938253012506087)
XLA Ops:
  1.4 3.0 %collective-permute-start = (bf16[14,192]{1,0:T(8,128)(2,1)S(1)}, bf16[14,192]{1,0:T(8,128)(2,1)S(1)}, u32[]{:S(2)}, u32[]{:S(2)}) collective-permute-start(bf16[14,192]{1,0:T(8,128)(2,1)S(1)} %convert_element_type.251), channel_id=1, source_target_pairs={{0,2},{1,3},{2,0},{3,1},{4,6},{5,7},{6,4},{7,5},{8,10},{9,11},{10,... | collective-permute-start | bytes 16136 | tf_op jit(solution)/shard_map/ppermute | solution.py:112
  9.9 3.3 %order.1 = (bf16[4,256,256]{2,1,0:T(8,128)(2,1)S(1)}, bf16[4,256,768]{2,1,0:T(8,128)(2,1)S(1)}, bf16[4,256,128]{2,1,0:T(8,128)(2,1)S(1)}, bf16[4,128,768]{2,1,0:T(8,128)(2,1)S(1)}) custom-call(s32[4]{0:T(128)S(1)} %copy-done.30, s32[4,1,128]{2,1,0:T(1,128)S(1)} %bitcast.31, bf16[4,256,768]{2,1,0:T(8,128)(2,1)S(1)} %copy-done.14, ...), custom_call_target="tpu_custom_call" | custom-call | flops 17999998976 | bytes 60000000 | tf_op jit(solution)/shard_map/order/pallas_call | solution.py:579
  16.5 4.1 %collective-permute-done.4.refs_6_.refs_14_ = bf16[96,2304]{1,0:T(8,128)(2,1)} collective-permute-done((bf16[96,2304]{1,0:T(8,128)(2,1)S(1)}, bf16[96,2304]{1,0:T(8,128)(2,1)}, u32[]{:S(2)}, u32[]{:S(2)}) %collective-permute-start.4) | collective-permute-done | bytes 442400 | tf_op jit(solution)/shard_map/ppermute | solution.py:112
  22.7 6.5 %collective-permute-done.5.refs_7_.refs_15_ = bf16[96,2304]{1,0:T(8,128)(2,1)S(1)} collective-permute-done((bf16[96,2304]{1,0:T(8,128)(2,1)}, bf16[96,2304]{1,0:T(8,128)(2,1)S(1)}, u32[]{:S(2)}, u32[]{:S(2)}) %collective-permute-start.5) | collective-permute-done | bytes 442400 | tf_op jit(solution)/shard_map/ppermute | solution.py:112
  31.1 8.0 %qkv.1 = (bf16[4,256,768]{2,1,0:T(8,128)(2,1)S(1)}, bf16[4,256,2304]{2,1,0:T(8,128)(2,1)S(1)}) custom-call(s32[52]{0:T(128)S(1)} %get-tuple-element.296.refs_0_, bf16[4,256,768]{2,1,0:T(8,128)(2,1)S(1)} %get-tuple-element.146.refs_1_, bf16[4,256,128]{2,1,0:T(8,128)(2,1)S(1)} %get-tuple-element.147.refs_2_, f32[16,768]{1,0:T(8,128)S(1)} %fusion.12.refs_3_.refs_4_, ...), custom_call_target="tpu_custom_call" | custom-call | flops 300000000 | bytes 1000000 | tf_op jit(solution)/shard_map/qkv/pallas_call | solution.py:579
  41.9 6.0 %mix.1.refs_2_.refs_3_ = bf16[4,256,768]{2,1,0:T(8,128)(2,1)S(1)} custom-call(bf16[4,256,2304]{2,1,0:T(8,128)(2,1)S(1)} %get-tuple-element.153.refs_0_.refs_2_, bf16[96,3840]{1,0:T(8,128)(2,1)} %collective-permute-done.8.refs_1_.refs_7_, bf16[4,256,2304]{2,1,0:T(8,128)(2,1)S(1)} %get-tuple-element.153.refs_0_.refs_2_), custom_call_target="tpu_custom_call" | custom-call | flops 3000000000 | bytes 10000000 | tf_op jit(solution)/shard_map/mix/pallas_call | solution.py:579
  47.9 3.6 %collective-permute-done.10.refs_8_ = bf16[96,3840]{1,0:T(8,128)(2,1)S(1)} collective-permute-done((bf16[96,3840]{1,0:T(8,128)(2,1)}, bf16[96,3840]{1,0:T(8,128)(2,1)S(1)}, u32[]{:S(2)}, u32[]{:S(2)}) %collective-permute-start.10) | collective-permute-done | bytes 737312 | tf_op jit(solution)/shard_map/ppermute | solution.py:112
  54.4 13.8 %fc1.1 = (f32[4,256,768]{2,1,0:T(8,128)S(1)}, bf16[4,256,768]{2,1,0:T(8,128)(2,1)S(1)}, bf16[4,256,3072]{2,1,0:T(8,128)(2,1)S(1)}, bf16[4,128,3072]{2,1,0:T(8,128)(2,1)S(1)}) custom-call(s32[52]{0:T(128)S(1)} %get-tuple-element.296.refs_0_, bf16[4,256,768]{2,1,0:T(8,128)(2,1)S(1)} %get-tuple-element.146.refs_1_, ...), custom_call_target="tpu_custom_call" | custom-call | flops 54000001024 | bytes 180000000 | tf_op jit(solution)/shard_map/fc1/pallas_call | solution.py:579
  70.7 6.6 %gw2.1 = (bf16[16,96,768]{2,1,0:T(8,128)(2,1)S(1)}, bf16[16,96,768]{2,1,0:T(8,128)(2,1)}, f32[1,768]{1,0:T(1,128)S(1)}) custom-call(s32[52]{0:T(128)S(1)} %get-tuple-element.296.refs_0_, bf16[4,256,3072]{2,1,0:T(8,128)(2,1)S(1)} %get-tuple-element.158.refs_1_, bf16[4,128,768]{2,1,0:T(8,128)(2,1)S(1)} %copy-done.9, ...), custom_call_target="tpu_custom_call" | custom-call | flops 24000000000 | bytes 80000000 | tf_op jit(solution)/shard_map/gw2/pallas_call | solution.py:579
  84.7 7.1 %df.1 = (bf16[512,3072]{1,0:T(8,128)(2,1)S(1)}, f32[1,3072]{1,0:T(1,128)S(1)}) custom-call(s32[52]{0:T(128)S(1)} %get-tuple-element.296.refs_0_, bf16[4,128,768]{2,1,0:T(8,128)(2,1)S(1)} %copy-done.10, bf16[4,128,3072]{2,1,0:T(8,128)(2,1)S(1)} %copy-done.35, bf16[768,768]{1,0:T(8,128)(2,1)} %get-tuple-element.161.refs_3_.refs_5_, ...), custom_call_target="tpu_custom_call" | custom-call | flops 20999999488 | bytes 70000000 | tf_op jit(solution)/shard_map/df/pallas_call | solution.py:579
  95.3 7.5 %mlp_back.1 = (f32[4,128,768]{2,1,0:T(8,128)S(1)}, bf16[4,128,768]{2,1,0:T(8,128)(2,1)S(1)}, bf16[4,128,768]{2,1,0:T(8,128)(2,1)S(1)}, f32[8,768]{1,0:T(8,128)S(1)}) custom-call(s32[52]{0:T(128)S(1)} %get-tuple-element.296.refs_0_, bf16[512,3072]{1,0:T(8,128)(2,1)S(1)} %get-tuple-element.167.refs_1_.refs_2_, bf16[4,128,768]{2,1,0:T(8,128)(2,1)S(1)} %copy-done.10, ...), custom_call_target="tpu_custom_call" | custom-call | flops 30000001024 | bytes 100000000 | tf_op jit(solution)/shard_map/mlp_back/pallas_call | solution.py:579
  102.8 6.9 %gw1o.1 = (bf16[16,24,3840]{2,1,0:T(8,128)(2,1)S(1)}, bf16[16,24,3840]{2,1,0:T(8,128)(2,1)S(1)}) custom-call(s32[52]{0:T(128)S(1)} %get-tuple-element.296.refs_0_, bf16[4,256,768]{2,1,0:T(8,128)(2,1)S(1)} %copy-done.40, bf16[512,3072]{1,0:T(8,128)(2,1)S(1)} %get-tuple-element.167.refs_1_.refs_2_, bf16[4,256,768]{2,1,0:T(8,128)(2,1)S(1)} %mix.1.refs_2_.refs_3_, ...), custom_call_target="tpu_custom_call" | custom-call | flops 27000000512 | bytes 90000000 | tf_op jit(solution)/shard_map/gw1o/pallas_call | solution.py:579
  112.2 9.1 %attn_back.2 = (bf16[4,128,768]{2,1,0:T(8,128)(2,1)S(1)}, bf16[4,256,1536]{2,1,0:T(8,128)(2,1)S(1)}, f32[8,768]{1,0:T(8,128)S(1)}) custom-call(bf16[4,256,2304]{2,1,0:T(8,128)(2,1)S(1)} %bitcast.30, bf16[4,128,768]{2,1,0:T(8,128)(2,1)S(1)} %get-tuple-element.173.refs_1_, bf16[4,96,768]{2,1,0:T(8,128)(2,1)S(1)} %add_convert_fusion.4.refs_2_, ...), custom_call_target="tpu_custom_call" | custom-call | flops 35999997952 | bytes 120000000 | tf_op jit(solution)/shard_map/attn_back/pallas_call | solution.py:579
  122.5 3.2 %collective-permute-start.22 = (bf16[2,96,768]{2,1,0:T(8,128)(2,1)S(1)}, bf16[2,96,768]{2,1,0:T(8,128)(2,1)S(1)}, u32[]{:S(2)}, u32[]{:S(2)}) collective-permute-start(bf16[2,96,768]{2,1,0:T(8,128)(2,1)S(1)} %add_convert_fusion.7.refs_6_), channel_id=1, source_target_pairs={{0,24},{1,3},{2,26},{3,1},{4,28},{5,7},{6,30},{7,5},{8,16},{9,11},... | collective-permute-start | bytes 884744 | tf_op jit(solution)/shard_map/ppermute | solution.py:112
  127.5 9.1 %attn_back.3 = (bf16[4,128,768]{2,1,0:T(8,128)(2,1)S(1)}, bf16[4,256,1536]{2,1,0:T(8,128)(2,1)S(1)}, f32[8,768]{1,0:T(8,128)S(1)}) custom-call(bf16[4,256,2304]{2,1,0:T(8,128)(2,1)S(1)} %bitcast.30, bf16[4,128,768]{2,1,0:T(8,128)(2,1)S(1)} %get-tuple-element.173.refs_1_, ...), custom_call_target="tpu_custom_call", output_to_operand_aliasing={{0}: (2, {}), {1}: (3, {})} | custom-call | flops 35999997952 | bytes 120000000 | tf_op jit(solution)/shard_map/attn_back/pallas_call | solution.py:579
  137.7 6.3 %gqkv.1 = (bf16[16,24,2304]{2,1,0:T(8,128)(2,1)S(1)}, bf16[16,24,2304]{2,1,0:T(8,128)(2,1)S(1)}) custom-call(s32[52]{0:T(128)S(1)} %get-tuple-element.296.refs_0_, bf16[4,256,768]{2,1,0:T(8,128)(2,1)S(1)} %copy-done.17, bf16[4,128,768]{2,1,0:T(8,128)(2,1)S(1)} %get-tuple-element.190.refs_2_.refs_4_, ...), custom_call_target="tpu_custom_call" | custom-call | flops 27000000512 | bytes 90000000 | tf_op jit(solution)/shard_map/gqkv/pallas_call | solution.py:579
  145.8 1.9 collective-permute-done.23
  149.5 2.1 subtract_convert_fusion.1
  152.5 12.3 %grad_in.1 = (f32[4,256,768]{2,1,0:T(8,128)}, f32[16,768]{1,0:T(8,128)S(1)}) custom-call(s32[52]{0:T(128)S(1)} %get-tuple-element.296.refs_0_, bf16[4,256,768]{2,1,0:T(8,128)(2,1)S(1)} %get-tuple-element.146.refs_1_, bf16[4,256,128]{2,1,0:T(8,128)(2,1)S(1)} %get-tuple-element.147.refs_2_, f32[16,768]{1,0:T(8,128)S(1)} %fusion.12.refs_3_.refs_4_, ...), custom_call_target="tpu_custom_call" | custom-call | flops 44999999488 | bytes 150000000 | tf_op jit(solution)/shard_map/grad_in/pallas_call | solution.py:579
  164.7 2.1 collective-permute-start.42
  167.8 2.9 %collective-permute-start.35 = (bf16[2,24,3840]{2,1,0:T(8,128)(2,1)S(1)}, bf16[2,24,3840]{2,1,0:T(8,128)(2,1)S(1)}, u32[]{:S(2)}, u32[]{:S(2)}) collective-permute-start(bf16[2,24,3840]{2,1,0:T(8,128)(2,1)S(1)} %add_convert_fusion.6.refs_12_), channel_id=1, source_target_pairs={{0,24},{1,3},{2,26},{3,1},{4,28},{5,7},{6,30},{7,5},{8,16},{9,11},... | collective-permute-start | bytes 1105928 | tf_op jit(solution)/shard_map/ppermute | solution.py:112
  172.1 10.6 %out.1 = bf16[4,256,768]{2,1,0:T(8,128)(2,1)} custom-call(s32[52]{0:T(128)S(1)} %get-tuple-element.296.refs_0_, bf16[4,256,3072]{2,1,0:T(8,128)(2,1)S(1)} %bitcast.33, f32[4,256,768]{2,1,0:T(8,128)S(1)} %copy-done.38, f32[16,768]{1,0:T(8,128)S(1)} %fusion.12.refs_3_.refs_4_, bf16[4,256,256]{2,1,0:T(8,128)(2,1)S(1)} %copy-done.42, ...), custom_call_target="tpu_custom_call" | custom-call | flops 38999998464 | bytes 130000000 | tf_op jit(solution)/shard_map/out/pallas_call | solution.py:579
  190.2 2.0 subtract_convert_fusion
  194.1 2.2 collective-permute-start.44
  198.0 3.7 %collective-permute-done.37 = bf16[1,24,3840]{2,1,0:T(8,128)(2,1)S(1)} collective-permute-done((bf16[1,24,3840]{2,1,0:T(8,128)(2,1)S(1)}, bf16[1,24,3840]{2,1,0:T(8,128)(2,1)S(1)}, u32[]{:S(2)}, u32[]{:S(2)}) %collective-permute-start.37) | collective-permute-done | bytes 184352 | tf_op jit(solution)/shard_map/ppermute | solution.py:112
  208.6 4.2 %collective-permute-done.32 = bf16[1,24,2304]{2,1,0:T(8,128)(2,1)S(1)} collective-permute-done((bf16[1,24,2304]{2,1,0:T(8,128)(2,1)S(1)}, bf16[1,24,2304]{2,1,0:T(8,128)(2,1)S(1)}, u32[]{:S(2)}, u32[]{:S(2)}) %collective-permute-start.32) | collective-permute-done | bytes 110624 | tf_op jit(solution)/shard_map/ppermute | solution.py:112
  213.7 2.4 collective-permute-done.38
  217.6 2.4 collective-permute-done.33
  222.2 2.6 %place.3.refs_3_ = f32[768,768]{1,0:T(8,128)} custom-call(s32[52]{0:T(128)S(1)} %get-tuple-element.296.refs_0_, bf16[4,104,768]{2,1,0:T(8,128)(2,1)S(1)} %constant_dynamic-update-slice_fusion.10.refs_1_, bf16[4,104,768]{2,1,0:T(8,128)(2,1)S(1)} %collective-permute-done.41.refs_2_, bf16[4,24,2304]{2,1,0:T(8,128)(2,1)S(1)} %constant_dynamic-update-slice_fusion.4.refs_3_.refs_1_), custom_call_target="tpu_custom_call" | custom-call | flops 3000000000 | bytes 10000000 | tf_op jit(solution)/shard_map/place/pallas_call | solution.py:579
  226.2 4.4 %collective-permute-done.39.refs_2_ = bf16[4,24,3840]{2,1,0:T(8,128)(2,1)S(1)} collective-permute-done((bf16[4,24,3840]{2,1,0:T(8,128)(2,1)S(1)}, bf16[4,24,3840]{2,1,0:T(8,128)(2,1)S(1)}, u32[]{:S(2)}, u32[]{:S(2)}) %collective-permute-start.39) | collective-permute-done | bytes 737312 | tf_op jit(solution)/shard_map/ppermute | solution.py:112
  232.2 3.5 %place.4 = (f32[192,3072]{1,0:T(8,128)}, f32[192,768]{1,0:T(8,128)}) custom-call(s32[52]{0:T(128)S(1)} %get-tuple-element.296.refs_0_, bf16[4,24,3840]{2,1,0:T(8,128)(2,1)S(1)} %constant_dynamic-update-slice_fusion.8.refs_1_, bf16[4,24,3840]{2,1,0:T(8,128)(2,1)S(1)} %collective-permute-done.39.refs_2_, f32[768,768]{1,0:T(8,128)S(1)} %copy-done.31), custom_call_target="tpu_custom_call" | custom-call | flops 3000000000 | bytes 10000000 | tf_op jit(solution)/shard_map/place/pallas_call | solution.py:579
  236.8 3.5 %place.5 = f32[192,2304]{1,0:T(8,128)} custom-call(s32[52]{0:T(128)S(1)} %get-tuple-element.296.refs_0_, bf16[4,24,2304]{2,1,0:T(8,128)(2,1)S(1)} %constant_dynamic-update-slice_fusion.4.refs_3_.refs_1_, bf16[4,24,2304]{2,1,0:T(8,128)(2,1)} %collective-permute-done.34.refs_2_, f32[192,768]{1,0:T(8,128)S(1)} %copy-done.32), custom_call_target="tpu_custom_call" | custom-call | flops 3000000000 | bytes 10000000 | tf_op jit(solution)/shard_map/place/pallas_call | solution.py:579
  (271 shorter events, 72.0 us)
Async XLA Ops:
  1.4 11.8 %collective-permute-start = (bf16[14,192]{1,0:T(8,128)(2,1)S(1)}, bf16[14,192]{1,0:T(8,128)(2,1)S(1)}, u32[]{:S(2)}, u32[]{:S(2)}) collective-permute-start(bf16[14,192]{1,0:T(8,128)(2,1)S(1)} %convert_element_type.251), channel_id=1, source_target_pairs={{0,2},{1,3},{2,0},{3,1},{4,6},{5,7},{6,4},{7,5},{8,10},{9,11},{10,... | collective-permute-start | bytes 16136 | tf_op jit(solution)/shard_map/ppermute | solution.py:112
  4.4 12.2 %collective-permute-start.2 = (bf16[14,192]{1,0:T(8,128)(2,1)S(1)}, bf16[14,192]{1,0:T(8,128)(2,1)S(1)}, u32[]{:S(2)}, u32[]{:S(2)}) collective-permute-start(bf16[14,192]{1,0:T(8,128)(2,1)S(1)} %convert_element_type.251), channel_id=1, source_target_pairs={{0,1},{1,0},{2,3},{3,2},{4,5},{5,4},{6,7},{7,6},{8,9},{9,8},{10,11... | collective-permute-start | bytes 16136 | tf_op jit(solution)/shard_map/ppermute | solution.py:112
  7.8 21.5 %collective-permute-start.3 = (bf16[192,2304]{1,0:T(8,128)(2,1)S(1)}, bf16[192,2304]{1,0:T(8,128)(2,1)}, u32[]{:S(2)}, u32[]{:S(2)}) collective-permute-start(bf16[192,2304]{1,0:T(8,128)(2,1)S(1)} %get-tuple-element.148.refs_4_.refs_12_), channel_id=1, source_target_pairs={{0,1},{1,0},{2,3},{3,2},{4,5},{5,4},{6,7},{7,6},{8,9},{9,8},{10,11... | collective-permute-start | bytes 2654216 | tf_op jit(solution)/shard_map/ppermute | solution.py:112
  8.4 12.3 %collective-permute-start.4 = (bf16[96,2304]{1,0:T(8,128)(2,1)S(1)}, bf16[96,2304]{1,0:T(8,128)(2,1)}, u32[]{:S(2)}, u32[]{:S(2)}) collective-permute-start(bf16[96,2304]{1,0:T(8,128)(2,1)S(1)} %get-tuple-element.145.refs_4_), channel_id=1, source_target_pairs={{0,2},{1,3},{2,0},{3,1},{4,6},{5,7},{6,4},{7,5},{8,10},{9,11},{10,... | collective-permute-start | bytes 1327112 | tf_op jit(solution)/shard_map/ppermute | solution.py:112
  22.2 17.7 %collective-permute-start.8 = (bf16[96,3840]{1,0:T(8,128)(2,1)}, bf16[96,3840]{1,0:T(8,128)(2,1)}, u32[]{:S(2)}, u32[]{:S(2)}) collective-permute-start(bf16[96,3840]{1,0:T(8,128)(2,1)} %get-tuple-element.152.refs_10_), channel_id=1, source_target_pairs={{0,2},{1,3},{2,0},{3,1},{4,6},{5,7},{6,4},{7,5},{8,10},{9,11},{10,... | collective-permute-start | bytes 2211848 | tf_op jit(solution)/shard_map/ppermute | solution.py:112
  39.9 11.7 %collective-permute-start.10 = (bf16[96,3840]{1,0:T(8,128)(2,1)}, bf16[96,3840]{1,0:T(8,128)(2,1)S(1)}, u32[]{:S(2)}, u32[]{:S(2)}) collective-permute-start(bf16[96,3840]{1,0:T(8,128)(2,1)} %collective-permute-done.8.refs_1_.refs_7_), channel_id=1, source_target_pairs={{0,4},{1,9},{2,6},{3,11},{4,0},{5,13},{6,2},{7,15},{8,12},{9,1},{1... | collective-permute-start | bytes 2211848 | tf_op jit(solution)/shard_map/ppermute | solution.py:112
  41.4 13.0 %collective-permute-start.9 = (bf16[192,3840]{1,0:T(8,128)(2,1)S(1)}, bf16[192,3840]{1,0:T(8,128)(2,1)S(1)}, u32[]{:S(2)}, u32[]{:S(2)}) collective-permute-start(bf16[192,3840]{1,0:T(8,128)(2,1)S(1)} %copy-done.19), channel_id=1, source_target_pairs={{0,1},{1,0},{2,3},{3,2},{4,5},{5,4},{6,7},{7,6},{8,9},{9,8},{10,11... | collective-permute-start | bytes 4423688 | tf_op jit(solution)/shard_map/ppermute | solution.py:112
  41.4 13.0 %collective-permute-start.11 = (bf16[96,3840]{1,0:T(8,128)(2,1)}, bf16[96,3840]{1,0:T(8,128)(2,1)S(1)}, u32[]{:S(2)}, u32[]{:S(2)}) collective-permute-start(bf16[96,3840]{1,0:T(8,128)(2,1)} %collective-permute-done.8.refs_1_.refs_7_), channel_id=1, source_target_pairs={{0,1},{1,0},{2,3},{3,2},{4,5},{5,4},{6,7},{7,6},{8,9},{9,8},{10,11... | collective-permute-start | bytes 2211848 | tf_op jit(solution)/shard_map/ppermute | solution.py:112
  53.3 27.3 %collective-permute-start.13 = (bf16[768,768]{1,0:T(8,128)(2,1)}, bf16[768,768]{1,0:T(8,128)(2,1)}, u32[]{:S(2)}, u32[]{:S(2)}) collective-permute-start(bf16[768,768]{1,0:T(8,128)(2,1)} %get-tuple-element.161.refs_3_.refs_5_), channel_id=1, source_target_pairs={{0,1},{1,0},{2,3},{3,2},{4,5},{5,4},{6,7},{7,6},{8,9},{9,8},{10,11... | collective-permute-start | bytes 3538952 | tf_op jit(solution)/shard_map/ppermute | solution.py:112
  53.8 15.3 %collective-permute-start.14 = (bf16[384,768]{1,0:T(8,128)(2,1)S(1)}, bf16[384,768]{1,0:T(8,128)(2,1)}, u32[]{:S(2)}, u32[]{:S(2)}) collective-permute-start(bf16[384,768]{1,0:T(8,128)(2,1)S(1)} %get-tuple-element.157.refs_11_), channel_id=1, source_target_pairs={{0,2},{1,3},{2,0},{3,1},{4,6},{5,7},{6,4},{7,5},{8,10},{9,11},{10,... | collective-permute-start | bytes 1769480 | tf_op jit(solution)/shard_map/ppermute | solution.py:112
  69.1 10.2 %collective-permute-start.15 = (bf16[384,768]{1,0:T(8,128)(2,1)}, bf16[384,768]{1,0:T(8,128)(2,1)}, u32[]{:S(2)}, u32[]{:S(2)}) collective-permute-start(bf16[384,768]{1,0:T(8,128)(2,1)} %collective-permute-done.14.refs_5_.refs_7_), channel_id=1, source_target_pairs={{0,4},{1,9},{2,6},{3,11},{4,0},{5,13},{6,2},{7,15},{8,12},{9,1},{1... | collective-permute-start | bytes 1769480 | tf_op jit(solution)/shard_map/ppermute | solution.py:112
  70.7 9.9 %collective-permute-start.16 = (bf16[384,768]{1,0:T(8,128)(2,1)}, bf16[384,768]{1,0:T(8,128)(2,1)}, u32[]{:S(2)}, u32[]{:S(2)}) collective-permute-start(bf16[384,768]{1,0:T(8,128)(2,1)} %collective-permute-done.14.refs_5_.refs_7_), channel_id=1, source_target_pairs={{0,1},{1,0},{2,3},{3,2},{4,5},{5,4},{6,7},{7,6},{8,9},{9,8},{10,11... | collective-permute-start | bytes 1769480 | tf_op jit(solution)/shard_map/ppermute | solution.py:112
  79.3 12.5 %collective-permute-start.18 = (bf16[16,96,768]{2,1,0:T(8,128)(2,1)}, bf16[16,96,768]{2,1,0:T(8,128)(2,1)}, u32[]{:S(2)}, u32[]{:S(2)}) collective-permute-start(bf16[16,96,768]{2,1,0:T(8,128)(2,1)} %get-tuple-element.169), channel_id=1, source_target_pairs={{0,1},{1,0},{2,3},{3,2},{4,5},{5,4},{6,7},{7,6},{8,9},{9,8},{10,11... | collective-permute-start | bytes 7077896 | tf_op jit(solution)/shard_map/ppermute | solution.py:112
  93.6 16.3 %collective-permute-start.19 = (bf16[8,96,768]{2,1,0:T(8,128)(2,1)S(1)}, bf16[8,96,768]{2,1,0:T(8,128)(2,1)S(1)}, u32[]{:S(2)}, u32[]{:S(2)}) collective-permute-start(bf16[8,96,768]{2,1,0:T(8,128)(2,1)S(1)} %add_convert_fusion.1.refs_11_), channel_id=1, source_target_pairs={{0,4},{1,9},{2,6},{3,11},{4,0},{5,13},{6,2},{7,15},{8,12},{9,1},{1... | collective-permute-start | bytes 3538952 | tf_op jit(solution)/shard_map/ppermute | solution.py:112
  109.7 15.9 %collective-permute-start.20 = (bf16[16,24,3840]{2,1,0:T(8,128)(2,1)S(1)}, bf16[16,24,3840]{2,1,0:T(8,128)(2,1)S(1)}, u32[]{:S(2)}, u32[]{:S(2)}) collective-permute-start(bf16[16,24,3840]{2,1,0:T(8,128)(2,1)S(1)} %get-tuple-element.176.refs_3_), channel_id=1, source_target_pairs={{0,1},{1,0},{2,3},{3,2},{4,5},{5,4},{6,7},{7,6},{8,9},{9,8},{10,11... | collective-permute-start | bytes 8847368 | tf_op jit(solution)/shard_map/ppermute | solution.py:112
  111.2 10.1 %collective-permute-start.21 = (bf16[4,96,768]{2,1,0:T(8,128)(2,1)S(1)}, bf16[4,96,768]{2,1,0:T(8,128)(2,1)S(1)}, u32[]{:S(2)}, u32[]{:S(2)}) collective-permute-start(bf16[4,96,768]{2,1,0:T(8,128)(2,1)S(1)} %add_convert_fusion.4.refs_2_), channel_id=1, source_target_pairs={{0,8},{1,5},{2,10},{3,7},{4,12},{5,1},{6,14},{7,3},{8,0},{9,13},{1... | collective-permute-start | bytes 1769480 | tf_op jit(solution)/shard_map/ppermute | solution.py:112
  122.5 14.2 %collective-permute-start.22 = (bf16[2,96,768]{2,1,0:T(8,128)(2,1)S(1)}, bf16[2,96,768]{2,1,0:T(8,128)(2,1)S(1)}, u32[]{:S(2)}, u32[]{:S(2)}) collective-permute-start(bf16[2,96,768]{2,1,0:T(8,128)(2,1)S(1)} %add_convert_fusion.7.refs_6_), channel_id=1, source_target_pairs={{0,24},{1,3},{2,26},{3,1},{4,28},{5,7},{6,30},{7,5},{8,16},{9,11},... | collective-permute-start | bytes 884744 | tf_op jit(solution)/shard_map/ppermute | solution.py:112
  126.0 19.4 %collective-permute-start.25 = (bf16[8,24,3840]{2,1,0:T(8,128)(2,1)S(1)}, bf16[8,24,3840]{2,1,0:T(8,128)(2,1)S(1)}, u32[]{:S(2)}, u32[]{:S(2)}) collective-permute-start(bf16[8,24,3840]{2,1,0:T(8,128)(2,1)S(1)} %add_convert_fusion.refs_5_), channel_id=1, source_target_pairs={{0,4},{1,9},{2,6},{3,11},{4,0},{5,13},{6,2},{7,15},{8,12},{9,1},{1... | collective-permute-start | bytes 4423688 | tf_op jit(solution)/shard_map/ppermute | solution.py:112
  145.7 21.9 %collective-permute-start.27 = (bf16[4,24,3840]{2,1,0:T(8,128)(2,1)S(1)}, bf16[4,24,3840]{2,1,0:T(8,128)(2,1)S(1)}, u32[]{:S(2)}, u32[]{:S(2)}) collective-permute-start(bf16[4,24,3840]{2,1,0:T(8,128)(2,1)S(1)} %add_convert_fusion.3.refs_18_), channel_id=1, source_target_pairs={{0,8},{1,5},{2,10},{3,7},{4,12},{5,1},{6,14},{7,3},{8,0},{9,13},{1... | collective-permute-start | bytes 2211848 | tf_op jit(solution)/shard_map/ppermute | solution.py:112
  148.0 22.7 %collective-permute-start.24 = (bf16[8,24,2304]{2,1,0:T(8,128)(2,1)S(1)}, bf16[8,24,2304]{2,1,0:T(8,128)(2,1)S(1)}, u32[]{:S(2)}, u32[]{:S(2)}) collective-permute-start(bf16[8,24,2304]{2,1,0:T(8,128)(2,1)S(1)} %add_convert_fusion.2.refs_19_), channel_id=1, source_target_pairs={{0,4},{1,9},{2,6},{3,11},{4,0},{5,13},{6,2},{7,15},{8,12},{9,1},{1... | collective-permute-start | bytes 2654216 | tf_op jit(solution)/shard_map/ppermute | solution.py:112
  151.6 15.2 %collective-permute-start.28 = (bf16[1,104,768]{2,1,0:T(8,128)(2,1)S(1)}, bf16[1,104,768]{2,1,0:T(8,128)(2,1)S(1)}, u32[]{:S(2)}, u32[]{:S(2)}) collective-permute-start(bf16[1,104,768]{2,1,0:T(8,128)(2,1)S(1)} %maximum_bitcast_fusion.1.refs_20_), channel_id=1, source_target_pairs={{0,24},{1,25},{2,26},{3,27},{4,28},{5,29},{6,30},{7,31},{8,16},{9,... | collective-permute-start | bytes 479240 | tf_op jit(solution)/shard_map/ppermute | solution.py:112
  164.7 20.4 %collective-permute-start.42 = (f32[16,768]{1,0:T(8,128)S(1)}, f32[16,768]{1,0:T(8,128)S(1)}, u32[]{:S(2)}, u32[]{:S(2)}) collective-permute-start(f32[16,768]{1,0:T(8,128)S(1)} %get-tuple-element.263.refs_14_), channel_id=1, source_target_pairs={{0,1},{1,0},{2,3},{3,2},{4,5},{5,4},{6,7},{7,6},{8,9},{9,8},{10,11... | collective-permute-start | bytes 147464 | tf_op jit(solution)/shard_map/ppermute | solution.py:112
  166.9 16.7 %collective-permute-start.40 = (bf16[2,104,768]{2,1,0:T(8,128)(2,1)S(1)}, bf16[2,104,768]{2,1,0:T(8,128)(2,1)S(1)}, u32[]{:S(2)}, u32[]{:S(2)}) collective-permute-start(bf16[2,104,768]{2,1,0:T(8,128)(2,1)S(1)} %constant_dynamic-update-slice_fusion.refs_13_), channel_id=1, source_target_pairs={{0,8},{1,5},{2,10},{3,7},{4,12},{5,1},{6,14},{7,3},{8,0},{9,13},{1... | collective-permute-start | bytes 958472 | tf_op jit(solution)/shard_map/ppermute | solution.py:112
  167.8 14.9 %collective-permute-start.35 = (bf16[2,24,3840]{2,1,0:T(8,128)(2,1)S(1)}, bf16[2,24,3840]{2,1,0:T(8,128)(2,1)S(1)}, u32[]{:S(2)}, u32[]{:S(2)}) collective-permute-start(bf16[2,24,3840]{2,1,0:T(8,128)(2,1)S(1)} %add_convert_fusion.6.refs_12_), channel_id=1, source_target_pairs={{0,24},{1,3},{2,26},{3,1},{4,28},{5,7},{6,30},{7,5},{8,16},{9,11},... | collective-permute-start | bytes 1105928 | tf_op jit(solution)/shard_map/ppermute | solution.py:112
  170.9 15.2 %collective-permute-start.29 = (bf16[4,24,2304]{2,1,0:T(8,128)(2,1)S(1)}, bf16[4,24,2304]{2,1,0:T(8,128)(2,1)S(1)}, u32[]{:S(2)}, u32[]{:S(2)}) collective-permute-start(bf16[4,24,2304]{2,1,0:T(8,128)(2,1)S(1)} %add_convert_fusion.5.refs_11_), channel_id=1, source_target_pairs={{0,8},{1,5},{2,10},{3,7},{4,12},{5,1},{6,14},{7,3},{8,0},{9,13},{1... | collective-permute-start | bytes 1327112 | tf_op jit(solution)/shard_map/ppermute | solution.py:112
  183.7 37.3 %collective-permute-start.41 = (bf16[4,104,768]{2,1,0:T(8,128)(2,1)S(1)}, bf16[4,104,768]{2,1,0:T(8,128)(2,1)S(1)}, u32[]{:S(2)}, u32[]{:S(2)}) collective-permute-start(bf16[4,104,768]{2,1,0:T(8,128)(2,1)S(1)} %constant_dynamic-update-slice_fusion.10.refs_1_), channel_id=1, source_target_pairs={{0,4},{1,9},{2,6},{3,11},{4,0},{5,13},{6,2},{7,15},{8,12},{9,1},{1... | collective-permute-start | bytes 1916936 | tf_op jit(solution)/shard_map/ppermute | solution.py:112
  185.2 8.9 %collective-permute-start.43 = (f32[16,768]{1,0:T(8,128)S(1)}, f32[16,768]{1,0:T(8,128)S(1)}, u32[]{:S(2)}, u32[]{:S(2)}) collective-permute-start(f32[16,768]{1,0:T(8,128)S(1)} %add.346), channel_id=1, source_target_pairs={{0,8},{1,9},{2,10},{3,11},{4,12},{5,13},{6,14},{7,15},{8,0},{9,1},... | collective-permute-start | bytes 147464 | tf_op jit(solution)/shard_map/ppermute | solution.py:112
  186.3 10.2 %collective-permute-start.30 = (bf16[2,24,2304]{2,1,0:T(8,128)(2,1)S(1)}, bf16[2,24,2304]{2,1,0:T(8,128)(2,1)S(1)}, u32[]{:S(2)}, u32[]{:S(2)}) collective-permute-start(bf16[2,24,2304]{2,1,0:T(8,128)(2,1)S(1)} %add_convert_fusion.8), channel_id=1, source_target_pairs={{0,24},{1,3},{2,26},{3,1},{4,28},{5,7},{6,30},{7,5},{8,16},{9,11},... | collective-permute-start | bytes 663560 | tf_op jit(solution)/shard_map/ppermute | solution.py:112
  192.3 9.4 %collective-permute-start.37 = (bf16[1,24,3840]{2,1,0:T(8,128)(2,1)S(1)}, bf16[1,24,3840]{2,1,0:T(8,128)(2,1)S(1)}, u32[]{:S(2)}, u32[]{:S(2)}) collective-permute-start(bf16[1,24,3840]{2,1,0:T(8,128)(2,1)S(1)} %maximum_bitcast_fusion), channel_id=1, source_target_pairs={{0,24},{1,25},{2,26},{3,27},{4,28},{5,29},{6,30},{7,31},{8,16},{9,... | collective-permute-start | bytes 552968 | tf_op jit(solution)/shard_map/ppermute | solution.py:112
  207.3 8.8 %collective-permute-start.38 = (bf16[2,24,3840]{2,1,0:T(8,128)(2,1)S(1)}, bf16[2,24,3840]{2,1,0:T(8,128)(2,1)S(1)}, u32[]{:S(2)}, u32[]{:S(2)}) collective-permute-start(bf16[2,24,3840]{2,1,0:T(8,128)(2,1)S(1)} %constant_dynamic-update-slice_fusion.6), channel_id=1, source_target_pairs={{0,8},{1,5},{2,10},{3,7},{4,12},{5,1},{6,14},{7,3},{8,0},{9,13},{1... | collective-permute-start | bytes 1105928 | tf_op jit(solution)/shard_map/ppermute | solution.py:112
  216.1 14.5 %collective-permute-start.39 = (bf16[4,24,3840]{2,1,0:T(8,128)(2,1)S(1)}, bf16[4,24,3840]{2,1,0:T(8,128)(2,1)S(1)}, u32[]{:S(2)}, u32[]{:S(2)}) collective-permute-start(bf16[4,24,3840]{2,1,0:T(8,128)(2,1)S(1)} %constant_dynamic-update-slice_fusion.8.refs_1_), channel_id=1, source_target_pairs={{0,4},{1,9},{2,6},{3,11},{4,0},{5,13},{6,2},{7,15},{8,12},{9,1},{1... | collective-permute-start | bytes 2211848 | tf_op jit(solution)/shard_map/ppermute | solution.py:112
  220.0 15.7 %collective-permute-start.34 = (bf16[4,24,2304]{2,1,0:T(8,128)(2,1)S(1)}, bf16[4,24,2304]{2,1,0:T(8,128)(2,1)}, u32[]{:S(2)}, u32[]{:S(2)}) collective-permute-start(bf16[4,24,2304]{2,1,0:T(8,128)(2,1)S(1)} %constant_dynamic-update-slice_fusion.4.refs_3_.refs_1_), channel_id=1, source_target_pairs={{0,4},{1,9},{2,6},{3,11},{4,0},{5,13},{6,2},{7,15},{8,12},{9,1},{1... | collective-permute-start | bytes 1327112 | tf_op jit(solution)/shard_map/ppermute | solution.py:112
  (79 other events, 593.4 us)
